TPU v7x, 32 devices: a whole 2x2x4 slice. The times are simulated.
32 devices in a mesh: groups: 2 (over x), tm: 8 (over z, y), space: 2 (over core).
Axes of the slice: x: 2, y: 2, z: 4, core: 2. Of those that a mesh axis runs over, the one named last changes fastest.
Arguments:
- frames_in: bfloat16 [16, 32, 80, 2240], P(('groups', 'tm'), 'space'), parts along dimension 0, may hold values from -6 to 6
- queries: bfloat16 [16, 32, 80, 1120], P(('groups', 'tm'), 'space'), parts along dimension 0, may hold values from -6 to 6
- key_weight: bfloat16 [2240, 1120], replicated, may hold values from -0.125 to 0.125
- value_weight: bfloat16 [2240, 1120], replicated, may hold values from -0.125 to 0.125
- conv_weight: float32 [9, 1120], replicated, may hold values from -2 to 2
- norm_gain: float32 [1120], replicated, may hold values from 0.1 to 1.9
Outputs:
- mixed: bfloat16 [16, 32, 80, 1120], P(('groups', 'tm'), 'space'), parts along dimension 0
There are 2 independent parts, one for each index of `groups`. A program takes and returns all parts, laid end to end along the dimension named above; an argument that names none is the same for every part. Nothing has to cross between parts.
All inputs are finite; a program needn't handle non-finite values.
Results may differ from a plain program's by a relative error of at most 0.005.
Values may be sent and summed in bfloat16 or wider, within the bound.
No kernel may reach another device: no remote copies, remote signals or barrier semaphores. Data moves between devices by JAX's collectives and lax.ppermute only.
A program may use at most 192 MiB of HBM per device.

v0:
```python
import jax
import jax.numpy as jnp
from jax import lax
from jax.sharding import PartitionSpec as P

HEADS = 10
HEAD = 112


def carried_in(part, axis, combine, identity):
    place = lax.axis_index(axis)
    gathered = lax.all_gather(part, axis)
    state = jnp.zeros_like(part) + jnp.asarray(identity, part.dtype)

    def one(turn, state):
        return combine(state, lax.dynamic_index_in_dim(gathered, turn, 0, False))

    return lax.fori_loop(0, place, one, state)


def from_behind(block, axis, distance):
    devices = range(lax.axis_size(axis))
    route = [(i - distance, i) for i in devices if i - distance in devices]
    return lax.ppermute(block, axis, route)


def padded_2(block, sides, width):
    for axis, dim in sides:
        count = lax.axis_size(axis)
        forward = [(i, i + 1) for i in range(count - 1)]
        backward = [(target, source) for source, target in forward]
        low = lax.ppermute(
            lax.slice_in_dim(block, block.shape[dim] - width, None, axis=dim), axis, forward
        )
        high = lax.ppermute(lax.slice_in_dim(block, 0, width, axis=dim), axis, backward)
        block = jnp.concatenate([low, block, high], axis=dim)
    return block


def feature_map(a):
    return jnp.where(a > 0, a + 1.0, jnp.exp(jnp.minimum(a, 0.0)))


def add_states(earlier, later):
    return earlier + later


def shards(frames_in, queries, key_weight, value_weight, conv_weight, norm_gain):
    _, rows, width, model = frames_in.shape
    inner = key_weight.shape[1]
    count = rows * width
    flat = frames_in.reshape(count, model)
    keys = feature_map(jnp.dot(flat, key_weight, preferred_element_type=jnp.float32)).astype(
        jnp.bfloat16
    )
    values = jnp.dot(flat, value_weight, preferred_element_type=jnp.float32).astype(jnp.bfloat16)
    key_heads = keys.reshape(count, HEADS, HEAD)
    value_heads = values.reshape(count, HEADS, HEAD)
    partial_state = jnp.einsum(
        "tha,thb->hab", key_heads, value_heads, preferred_element_type=jnp.float32
    )
    zeros_state = jnp.zeros_like(partial_state)
    earlier = carried_in(partial_state, ("tm", "space"), add_states, zeros_state)
    later_half = from_behind(partial_state, "space", -1)
    prefix = earlier + partial_state + later_half
    qfeat = feature_map(queries.reshape(count, HEADS, HEAD).astype(jnp.float32))
    attn = jnp.einsum("tha,hab->thb", qfeat, prefix, precision=lax.Precision.HIGHEST)
    scale = lax.rsqrt(jnp.mean(attn * attn, axis=-1, keepdims=True) + 1e-06)
    normed = (attn * scale).reshape(rows, width, inner) * norm_gain
    image = values.reshape(rows, width, inner)
    extended = padded_2(image, (("space", 0),), 1)
    padded = jnp.pad(extended, ((0, 0), (1, 1), (0, 0))).astype(jnp.float32)
    local = jnp.zeros((rows, width, inner), jnp.float32)
    for row_off in range(3):
        for col_off in range(3):
            local = (
                local
                + conv_weight[row_off * 3 + col_off]
                * padded[row_off : row_off + rows, col_off : col_off + width, :]
            )
    mixed = (normed + local).astype(jnp.bfloat16)
    return mixed.reshape(1, rows, width, inner)


def solution(mesh):
    in_specs = (
        P(("groups", "tm"), "space", None, None),
        P(("groups", "tm"), "space", None, None),
        P(),
        P(),
        P(),
        P(),
    )
    out_specs = P(("groups", "tm"), "space", None, None)
    return jax.shard_map(shards, mesh=mesh, in_specs=in_specs, out_specs=out_specs, check_vma=False)
```

profile of v0, /device:TPU:29, one launch (start us, length us, event | category | flops | bytes accessed | tf_op | source)
XLA Modules:
  0.0 213.0 jit_solution(6245308538739894845)
XLA Ops:
  6.5 0.0 all-gather.3.cloned.1.call-start
  6.5 0.0 copy-start.3
  6.5 0.0 copy-start.4
  6.5 11.3 %convolution_convert_fusion = bf16[1280,1120]{0,1:T(8,128)(2,1)S(1)} fusion(bf16[1280,2240]{1,0:T(8,128)(2,1)} %bitcast.34, bf16[2240,1120]{1,0:T(8,128)(2,1)} %param.11), kind=kOutput, calls=%fused_computation.29 | convolution fusion | flops 6423961600 | bytes 13619200 | tf_op jit(solution)/shard_map/dot_general | solution.py:56
  17.8 0.0 copy-done.3
  17.8 0.0 copy-done.4
  17.8 8.1 %select_convert_fusion = bf16[1280,1120]{0,1:T(8,128)(2,1)S(1)} fusion(bf16[1280,2240]{1,0:T(8,128)(2,1)S(1)} %bitcast.35, bf16[2240,1120]{1,0:T(8,128)(2,1)S(1)} %copy-done.4), kind=kOutput, calls=%fused_computation.40 | convolution fusion | flops 6429696000 | bytes 13619200 | tf_op jit(solution)/shard_map/dot_general | solution.py:53
  25.9 1.7 fusion.25
  27.6 0.0 all-gather.3.cloned.1.call-update
  27.6 2.6 %collective-permute-start = (f32[10,112,112]{2,1,0:T(8,128)}, f32[10,112,112]{2,1,0:T(8,128)S(1)}, u32[]{:S(2)}, u32[]{:S(2)}) collective-permute-start(f32[10,112,112]{2,1,0:T(8,128)} %fusion.25), channel_id=1, source_target_pairs={{1,0},{3,2},{5,4},{7,6},{9,8},{11,10},{13,12},{15,14},{17,16},{19,... | collective-permute-start | bytes 1505288 | tf_op jit(solution)/shard_map/ppermute | solution.py:24
  30.3 0.9 slice_bitcast_fusion.1
  31.2 1.3 collective-permute-start.1
  32.5 4.5 %collective-permute-start.2 = (bf16[1,80,1120]{1,2,0:T(8,128)(2,1)}, bf16[1,80,1120]{1,2,0:T(8,128)(2,1)}, u32[]{:S(2)}, u32[]{:S(2)}) collective-permute-start(bf16[1,80,1120]{1,2,0:T(8,128)(2,1)} %get-tuple-element.47), channel_id=1, source_target_pairs={{1,0},{3,2},{5,4},{7,6},{9,8},{11,10},{13,12},{15,14},{17,16},{19,... | collective-permute-start | bytes 537608 | tf_op jit(solution)/shard_map/ppermute | solution.py:35
  36.9 5.8 %fusion.19 = f32[1,16,80,1120]{3,2,1,0:T(8,128)} fusion(bf16[1,16,80,1120]{3,2,1,0:T(8,128)(2,1)} %param.9), kind=kLoop, calls=%fused_computation.35 | loop fusion | flops 7168000 | bytes 8601600 | tf_op jit(solution)/shard_map/jit(_where)/select_n | solution.py:41
  42.8 3.3 %copy.29 = bf16[1280,1120]{1,0:T(8,128)(2,1)} copy(bf16[1280,1120]{0,1:T(8,128)(2,1)S(1)} %convolution_convert_fusion) | data formatting | bytes 5734400 | tf_op jit(solution)/shard_map/convert_element_type | solution.py:56
  46.1 0.0 copy-start
  46.1 10.7 %reshape.55 = f32[1280,10,112]{2,1,0:T(8,128)} reshape(f32[1,16,80,1120]{3,2,1,0:T(8,128)} %fusion.19) | data formatting | bytes 11468800 | tf_op jit(solution)/shard_map/jit(_where)/select_n | solution.py:41
  56.8 0.0 copy-done
  56.8 4.8 %copy.31 = bf16[16,80,1120]{1,0,2:T(8,128)(2,1)} copy(bf16[16,80,1120]{2,1,0:T(8,128)(2,1)S(1)} %bitcast.31) | data formatting | bytes 5734400 | tf_op jit(solution)/shard_map/reshape | solution.py:70
  61.6 1.4 slice_reduce_fusion.8
  63.0 0.0 collective-permute-done.1
  63.0 3.3 %copy.30 = bf16[1,80,1120]{1,0,2:T(2,128)(2,1)S(1)} copy(bf16[1,80,1120]{1,2,0:T(8,128)(2,1)} %collective-permute-done.1) | data formatting | bytes 358400 | tf_op jit(solution)/shard_map/ppermute | solution.py:32
  66.3 0.0 collective-permute-done.2
  66.3 3.3 %copy.32 = bf16[1,80,1120]{1,0,2:T(2,128)(2,1)S(1)} copy(bf16[1,80,1120]{1,2,0:T(8,128)(2,1)} %collective-permute-done.2) | data formatting | bytes 358400 | tf_op jit(solution)/shard_map/ppermute | solution.py:35
  69.6 10.5 %fusion.16 = f32[18,82,1120]{1,0,2:T(8,128)} fusion(bf16[1,80,1120]{1,0,2:T(2,128)(2,1)S(1)} %copy.32, bf16[16,80,1120]{1,0,2:T(8,128)(2,1)} %copy.31, bf16[1,80,1120]{1,0,2:T(2,128)(2,1)S(1)} %copy.30), kind=kLoop, calls=%fused_computation.32 | loop fusion | flops 19837440 | bytes 9838080 | tf_op jit(solution)/shard_map/convert_element_type | solution.py:72
  80.1 0.0 copy-start.1
  80.1 26.2 %all-gather.3.cloned.1.call-done = f32[160,112,112]{2,1,0:T(8,128)} async-done(((f32[10,112,112]{2,1,0:T(8,128)}), f32[160,112,112]{2,1,0:T(8,128)}) %all-gather.3.cloned.1.call-update) | async-done | bytes 8028176 | tf_op jit(solution)/shard_map/all_gather | solution.py:12
  106.3 18.3 %while.10 = (s32[]{:T(128)}, f32[10,112,112]{2,1,0:T(8,128)S(1)}, s32[]{:T(128)}, f32[16,10,112,112]{3,2,1,0:T(8,128)}, s32[]{:T(128)}, /*index=5*/s32[]{:T(128)}, s32[]{:T(128)}) while((s32[]{:T(128)}, f32[10,112,112]{2,1,0:T(8,128)S(1)}, s32[]{:T(128)}, f32[16,10,112,112]{3,2,1,0:T(8,128)}, s32[]{:T(128)}, /*index=5*/s32[]{:T(128)}, ...), condition=%wide.region_1.2_spmd, body=%wide.region_0.1_spmd.sunk | while | flops 125445 | bytes 1505395 | solution.py:18
  106.3 1.2 bitcast_add_fusion.2
  107.5 1.2 bitcast_add_fusion.2
  108.8 1.2 bitcast_add_fusion.2
  110.0 1.2 bitcast_add_fusion.2
  111.2 1.2 bitcast_add_fusion.2
  112.4 1.2 bitcast_add_fusion.2
  113.6 1.2 bitcast_add_fusion.2
  114.8 1.2 bitcast_add_fusion.2
  116.0 1.2 bitcast_add_fusion.2
  117.2 1.2 bitcast_add_fusion.2
  118.4 1.2 bitcast_add_fusion.2
  119.6 1.2 bitcast_add_fusion.2
  120.8 1.2 bitcast_add_fusion.2
  122.0 1.2 bitcast_add_fusion.2
  123.2 1.2 bitcast_add_fusion.2
  124.6 0.0 collective-permute-done
  124.6 0.0 copy-done.1
  124.6 13.0 %fusion.21 = (f32[1280,10]{0,1:T(8,128)S(1)}, f32[10,112,1280]{2,1,0:T(8,128)S(1)}) fusion(f32[1280,10,112]{2,1,0:T(8,128)} %reshape.55, f32[10,112,112]{2,1,0:T(8,128)S(1)} %collective-permute-done, f32[10,112,112]{2,1,0:T(8,128)S(1)} %get-tuple-element.28, f32[10,112,112]{2,1,0:T(8,128)S(1)} %copy-done.1), kind=kOutput, calls=%fused_computation.39 | convolution fusion | flops 1929863680 | bytes 13025280 | tf_op jit(solution)/shard_map/tha,hab->thb/dot_general | solution.py:67
  137.7 2.9 %bitcast_multiply_fusion = f32[1280,10,112]{0,2,1:T(8,128)} fusion(f32[10,112,1280]{2,1,0:T(8,128)S(1)} %get-tuple-element.49, f32[1280,10]{0,1:T(8,128)S(1)} %add_rsqrt_fusion), kind=kLoop, calls=%fused_computation.37 | loop fusion | flops 1433600 | bytes 11520000 | tf_op jit(solution)/shard_map/mul | solution.py:69
  140.6 0.0 copy-start.2
  140.6 10.3 %reshape.51 = f32[16,80,1120]{1,0,2:T(8,128)} reshape(f32[1280,10,112]{0,2,1:T(8,128)} %bitcast_multiply_fusion) | data formatting | bytes 11468800 | tf_op jit(solution)/shard_map/reshape | solution.py:69
  150.9 0.0 copy-done.2
  150.9 48.7 %fusion.22 = bf16[1,16,80,1120]{2,1,3,0:T(8,128)(2,1)} fusion(f32[18,82,1120]{1,0,2:T(8,128)} %fusion.16, f32[1120]{0:T(1024)S(1)} %get-tuple-element.36, f32[1120]{0:T(1024)S(1)} %get-tuple-element.37, f32[1120]{0:T(1024)S(1)} %get-tuple-element.30, f32[1120]{0:T(1024)S(1)} %get-tuple-element.31, f32[1120]{0:T(1024)S(1)} %get-tuple-element.32, ...), kind=kLoop, calls=%fused_computation.41 | loop fusion | flops 28672000 | bytes 60256000 | tf_op jit(solution)/shard_map/reshape | solution.py:82
  199.7 6.5 %copy.33 = bf16[1,16,80,1120]{3,2,1,0:T(8,128)(2,1)} copy(bf16[1,16,80,1120]{2,1,3,0:T(8,128)(2,1)} %fusion.22) | data formatting | bytes 5734400 | tf_op jit(solution)/shard_map/reshape | solution.py:82
  (2 shorter events, 0.1 us)
Async XLA Ops:
  6.5 99.7 %all-gather.3.cloned.1.call-start = ((), (), s32[]{:S(2)}) async-start(), calls=%async_computation | async-start | bytes 9748480 | tf_op jit(solution)/shard_map/all_gather | solution.py:12
  6.5 11.3 %copy-start.3 = (bf16[1,16,80,2240]{3,2,1,0:T(8,128)(2,1)S(1)}, bf16[1,16,80,2240]{3,2,1,0:T(8,128)(2,1)}, u32[]{:S(2)}) copy-start(bf16[1,16,80,2240]{3,2,1,0:T(8,128)(2,1)} %param.8) | copy-start | bytes 17203204
  6.5 11.3 %copy-start.4 = (bf16[2240,1120]{1,0:T(8,128)(2,1)S(1)}, bf16[2240,1120]{1,0:T(8,128)(2,1)}, u32[]{:S(2)}) copy-start(bf16[2240,1120]{1,0:T(8,128)(2,1)} %param.10) | copy-start | bytes 15052804
  27.6 97.0 %collective-permute-start = (f32[10,112,112]{2,1,0:T(8,128)}, f32[10,112,112]{2,1,0:T(8,128)S(1)}, u32[]{:S(2)}, u32[]{:S(2)}) collective-permute-start(f32[10,112,112]{2,1,0:T(8,128)} %fusion.25), channel_id=1, source_target_pairs={{1,0},{3,2},{5,4},{7,6},{9,8},{11,10},{13,12},{15,14},{17,16},{19,... | collective-permute-start | bytes 1505288 | tf_op jit(solution)/shard_map/ppermute | solution.py:24
  31.2 31.8 %collective-permute-start.1 = (bf16[1,80,1120]{1,2,0:T(8,128)(2,1)}, bf16[1,80,1120]{1,2,0:T(8,128)(2,1)}, u32[]{:S(2)}, u32[]{:S(2)}) collective-permute-start(bf16[1,80,1120]{1,2,0:T(8,128)(2,1)} %get-tuple-element.46), channel_id=1, source_target_pairs={{0,1},{2,3},{4,5},{6,7},{8,9},{10,11},{12,13},{14,15},{16,17},{18,... | collective-permute-start | bytes 537608 | tf_op jit(solution)/shard_map/ppermute | solution.py:32
  32.5 33.8 %collective-permute-start.2 = (bf16[1,80,1120]{1,2,0:T(8,128)(2,1)}, bf16[1,80,1120]{1,2,0:T(8,128)(2,1)}, u32[]{:S(2)}, u32[]{:S(2)}) collective-permute-start(bf16[1,80,1120]{1,2,0:T(8,128)(2,1)} %get-tuple-element.47), channel_id=1, source_target_pairs={{1,0},{3,2},{5,4},{7,6},{9,8},{11,10},{13,12},{15,14},{17,16},{19,... | collective-permute-start | bytes 537608 | tf_op jit(solution)/shard_map/ppermute | solution.py:35
  46.1 10.7 %copy-start = (bf16[1280,1120]{1,0:T(8,128)(2,1)S(1)}, bf16[1280,1120]{1,0:T(8,128)(2,1)}, u32[]{:S(2)}) copy-start(bf16[1280,1120]{1,0:T(8,128)(2,1)} %copy.29) | copy-start | bytes 8601604
  80.1 44.5 %copy-start.1 = (f32[10,112,112]{2,1,0:T(8,128)S(1)}, f32[10,112,112]{2,1,0:T(8,128)}, u32[]{:S(2)}) copy-start(f32[10,112,112]{2,1,0:T(8,128)} %fusion.25) | copy-start | bytes 1505284
  140.6 10.3 %copy-start.2 = (f32[1120]{0:T(1024)S(1)}, f32[1120]{0:T(1024)}, u32[]{:S(2)}) copy-start(f32[1120]{0:T(1024)} %param.13) | copy-start | bytes 13444
Sparse Core Ops, SparseCore 0:
  27.8 78.4 all-gather.2
where the time goes:
time: 215 us; the launch traced here: 213 us
  other arithmetic  85.6 us (40%)
  local copies, waits for them, and re-layouts  44.6 us (21%)
  matrix products  34.1 us (16%)
  waiting for transfers between devices  26.2 us (12%)
  between operations  13.5 us (6%)
  starting transfers between devices  8.35 us (4%)
    reshape x1, other arithmetic, shards(): return mixed.reshape(1, rows, width, inner)  48.7 us
    all_gather x1, waiting for transfers between devices, carried_in(): gathered = lax.all_gather(part, axis)  26.2 us
    add x15, other arithmetic, add_states(): return earlier + later  17.7 us
    dot_general x1, matrix products, shards(): jnp.einsum('tha,hab->thb', qfeat, prefix, precision=lax.Precision.HIGHEST)  13 us
    dot_general x1, matrix products, shards(): jnp.dot(flat, value_weight, preferred_element_type=jnp.float32)  11.3 us
    select_n x1, local copies, waits for them, and re-layouts, feature_map(): return jnp.where(a > 0, a + 1.0, jnp.exp(jnp.minimum(a, 0.0)))  10.7 us
    convert_element_type x1, other arithmetic, shards(): padded = jnp.pad(extended, ((0, 0), (1, 1), (0, 0))).astype(jnp.float32)  10.5 us
    reshape x1, local copies, waits for them, and re-layouts, shards(): normed = (attn * scale).reshape(rows, width, inner) * norm_gain  10.3 us
  transfers between devices with their start and end apart: 4, of which 1 were waited for; matrix products, arithmetic and copies ran while one was open for 29% of the time, Pallas kernels for 0%

commit v1 on v0

v1 whole, which is shorter than its diff:
```python
import functools

import jax
import jax.numpy as jnp
from jax import lax
from jax.experimental import pallas as pl
from jax.experimental.pallas import tpu as pltpu
from jax.sharding import PartitionSpec as P

HEADS = 10
HEAD = 112
TILE = 256
F32 = jnp.float32
BF16 = jnp.bfloat16
MIB = 1 << 20


def feature_map(a):
    return jnp.where(a > 0, a + 1.0, jnp.exp(jnp.minimum(a, 0.0)))


def first_head(tile, inner):
    return min(tile * TILE // HEAD, inner // HEAD - 4)


def project_kernel(
    core_ref, x_ref, wk_ref, wv_ref, v_ref, mine_ref, send_ref, edge_ref, kt, vs, state, *, chunk, width
):
    j = pl.program_id(0)
    steps = pl.num_programs(0)
    count = x_ref.shape[0]
    inner = state.shape[1]
    last_head = inner // HEAD - 4

    def one(m, carry):
        at = pl.multiple_of(m * chunk, chunk)
        rows = pl.ds(at, chunk)
        x = x_ref[rows, :]
        k = feature_map(jnp.dot(x, wk_ref[...], preferred_element_type=F32)).astype(BF16)
        kt[pl.ds(pl.multiple_of(j * TILE, TILE), TILE), rows] = k.T
        v = jnp.dot(x, wv_ref[...], preferred_element_type=F32).astype(BF16)
        v_ref[rows, :] = v
        vs[j, rows, :] = v
        return carry

    lax.fori_loop(0, count // chunk, one, 0)

    def state_tile(i):
        head = jnp.minimum(2 * i, last_head)
        keys = kt[pl.ds(pl.multiple_of(head * HEAD, 16), 4 * HEAD), :]
        full = jnp.dot(keys, vs[i], preferred_element_type=F32)
        column = lax.broadcasted_iota(jnp.int32, (HEAD, TILE), 1) + i * TILE
        total = jnp.zeros((HEAD, TILE), F32)
        for m in range(4):
            low = (head + m) * HEAD
            inside = (column >= low) & (column < low + HEAD)
            total = total + jnp.where(inside, full[m * HEAD : (m + 1) * HEAD, :], 0.0)
        return total

    def keep(i, total):
        for t in range(inner // TILE):

            @pl.when(i == t)
            def _():
                state[:, t * TILE : (t + 1) * TILE] = total

    @pl.when(j > 0)
    def _():
        keep(j - 1, state_tile(j - 1))

    @pl.when(j == steps - 1)
    def _():
        rest = inner - inner // TILE * TILE
        state[:, inner - rest :] = state_tile(j)[:, :rest]
        core = core_ref[0]
        half = HEAD // 2
        mine_ref[...] = state[pl.ds(pl.multiple_of(core * half, 8), half), :]
        send_ref[...] = state[pl.ds(pl.multiple_of((1 - core) * half, 8), half), :].astype(BF16)
        start = pl.multiple_of((1 - core) * (count - width), 16)
        for t in range(inner // TILE):
            edge_ref[:, t * TILE : (t + 1) * TILE] = vs[t, pl.ds(start, width), :]
        edge_ref[:, inner - rest :] = vs[inner // TILE, pl.ds(start, width), :rest]


def project(core, flat, key_weight, value_weight, width):
    count, model = flat.shape
    inner = key_weight.shape[1]
    steps = pl.cdiv(inner, TILE)
    half = HEAD // 2
    return pl.pallas_call(
        functools.partial(project_kernel, chunk=256, width=width),
        grid_spec=pltpu.PrefetchScalarGridSpec(
            num_scalar_prefetch=1,
            grid=(steps,),
            in_specs=[
                pl.BlockSpec((count, model), lambda j, c: (0, 0)),
                pl.BlockSpec((model, TILE), lambda j, c: (0, j)),
                pl.BlockSpec((model, TILE), lambda j, c: (0, j)),
            ],
            out_specs=[
                pl.BlockSpec((count, TILE), lambda j, c: (0, j)),
                pl.BlockSpec((half, inner), lambda j, c: (0, 0)),
                pl.BlockSpec((half, inner), lambda j, c: (0, 0)),
                pl.BlockSpec((width, inner), lambda j, c: (0, 0)),
            ],
            scratch_shapes=[
                pltpu.VMEM((steps * TILE, count), BF16),
                pltpu.VMEM((steps, count, TILE), BF16),
                pltpu.VMEM((HEAD, inner), F32),
            ],
        ),
        out_shape=[
            jax.ShapeDtypeStruct((count, inner), BF16),
            jax.ShapeDtypeStruct((half, inner), F32),
            jax.ShapeDtypeStruct((half, inner), BF16),
            jax.ShapeDtypeStruct((width, inner), BF16),
        ],
        compiler_params=pltpu.CompilerParams(vmem_limit_bytes=50 * MIB),
        cost_estimate=pl.CostEstimate(
            flops=4 * count * model * inner, bytes_accessed=2 * (count * model + 2 * model * inner), transcendentals=0
        ),
        name="project",
    )(core, flat, key_weight, value_weight)


def local_kernel(core_ref, v_ref, halo_ref, q_ref, w_ref, local_ref, qf_ref, ext, *, width, rows):
    i = pl.program_id(0)
    count, inner = v_ref.shape

    @pl.when(i == 0)
    def _():
        core = core_ref[0]
        halo = halo_ref[...]
        nothing = jnp.zeros_like(halo)
        ext[0:width, :] = jnp.where(core == 1, halo, nothing)
        ext[width : width + count, :] = v_ref[...]
        ext[width + count :, :] = jnp.where(core == 0, halo, nothing)

    lanes = [(a, min(a + 128, inner)) for a in range(0, inner, 128)]

    def row(r, carry):
        at = pl.multiple_of((i * rows + r) * width, 16)
        here = pl.ds(pl.multiple_of(r * width, 16), width)
        for low, high in lanes:
            taps = [ext[pl.ds(at + d * width, width), low:high].astype(F32) for d in range(3)]
            side = []
            for c in range(3):
                acc = taps[0] * w_ref[c : c + 1, low:high]
                acc = acc + taps[1] * w_ref[3 + c : 4 + c, low:high]
                side.append(acc + taps[2] * w_ref[6 + c : 7 + c, low:high])
            place = lax.broadcasted_iota(jnp.int32, side[0].shape, 0)
            left = jnp.where(place > 0, pltpu.roll(side[0], 1, 0), 0.0)
            right = jnp.where(place < width - 1, pltpu.roll(side[2], width - 1, 0), 0.0)
            local_ref[here, low:high] = side[1] + left + right
            qf_ref[here, low:high] = feature_map(q_ref[here, low:high].astype(F32)).astype(BF16)
        return carry

    lax.fori_loop(0, rows, row, 0)


def local_branch(core, values, halo, queries, conv_weight, width):
    count, inner = values.shape
    rows = 4
    block = rows * width
    return pl.pallas_call(
        functools.partial(local_kernel, width=width, rows=rows),
        grid_spec=pltpu.PrefetchScalarGridSpec(
            num_scalar_prefetch=1,
            grid=(count // block,),
            in_specs=[
                pl.BlockSpec((count, inner), lambda i, c: (0, 0)),
                pl.BlockSpec((width, inner), lambda i, c: (0, 0)),
                pl.BlockSpec((block, inner), lambda i, c: (i, 0)),
                pl.BlockSpec(conv_weight.shape, lambda i, c: (0, 0)),
            ],
            out_specs=[
                pl.BlockSpec((block, inner), lambda i, c: (i, 0)),
                pl.BlockSpec((block, inner), lambda i, c: (i, 0)),
            ],
            scratch_shapes=[pltpu.VMEM((count + 2 * width, inner), BF16)],
        ),
        out_shape=[
            jax.ShapeDtypeStruct((count, inner), F32),
            jax.ShapeDtypeStruct((count, inner), BF16),
        ],
        compiler_params=pltpu.CompilerParams(vmem_limit_bytes=32 * MIB),
        cost_estimate=pl.CostEstimate(
            flops=20 * count * inner, bytes_accessed=12 * count * inner, transcendentals=count * inner
        ),
        name="local_branch",
    )(core, values, halo, queries, conv_weight)


def attend_kernel(p_ref, qf_ref, local_ref, gain_ref, out_ref, band, ones):
    inner = p_ref.shape[1]
    heads = inner // HEAD

    @pl.when(pl.program_id(0) == 0)
    def _():
        p = p_ref[...]
        column = lax.broadcasted_iota(jnp.int32, p.shape, 1)
        for h in range(heads):
            inside = (column >= h * HEAD) & (column < (h + 1) * HEAD)
            band[h * HEAD : (h + 1) * HEAD, :] = jnp.where(inside, p, jnp.zeros_like(p))
            ones[h * HEAD : (h + 1) * HEAD, :] = inside.astype(F32).astype(BF16)

    tiles = [(a, min(a + TILE, inner)) for a in range(0, inner, TILE)]
    spans = []
    for low, high in tiles:
        start = low // HEAD * HEAD // 128 * 128
        stop = min(-(-(-(-high // HEAD) * HEAD) // 128) * 128, inner)
        spans.append((start, stop))
    attn = []
    for (low, high), (start, stop) in zip(tiles, spans):
        attn.append(jnp.dot(qf_ref[:, start:stop], band[start:stop, low:high], preferred_element_type=F32))
    attn = jnp.concatenate(attn, axis=1)
    square = (attn * attn).astype(BF16)
    for (low, high), (start, stop) in zip(tiles, spans):
        total = jnp.dot(square[:, start:stop], ones[start:stop, low:high], preferred_element_type=F32)
        scale = lax.rsqrt(total * (1.0 / HEAD) + 1e-06)
        normed = attn[:, low:high] * scale * gain_ref[:, low:high]
        out_ref[:, low:high] = (normed + local_ref[:, low:high]).astype(BF16)


def attend(prefix, qfeat, local, gain):
    count, inner = qfeat.shape
    block = 256
    return pl.pallas_call(
        attend_kernel,
        grid=(count // block,),
        in_specs=[
            pl.BlockSpec((HEAD, inner), lambda i: (0, 0)),
            pl.BlockSpec((block, inner), lambda i: (i, 0)),
            pl.BlockSpec((block, inner), lambda i: (i, 0)),
            pl.BlockSpec((1, inner), lambda i: (0, 0)),
        ],
        out_specs=pl.BlockSpec((block, inner), lambda i: (i, 0)),
        scratch_shapes=[pltpu.VMEM((inner, inner), BF16), pltpu.VMEM((inner, inner), BF16)],
        out_shape=jax.ShapeDtypeStruct((count, inner), BF16),
        compiler_params=pltpu.CompilerParams(vmem_limit_bytes=32 * MIB),
        cost_estimate=pl.CostEstimate(
            flops=4 * count * inner * 512, bytes_accessed=8 * count * inner, transcendentals=count * inner
        ),
        name="attend",
    )(prefix, qfeat, local, gain)


def swapped(block, axis, bit):
    return lax.ppermute(block, axis, [(i, i ^ bit) for i in range(lax.axis_size(axis))])


def shards(frames_in, queries, key_weight, value_weight, conv_weight, norm_gain):
    _, rows, width, model = frames_in.shape
    inner = key_weight.shape[1]
    count = rows * width
    core_index = lax.axis_index("space")
    frame = lax.axis_index("tm")
    core = core_index.astype(jnp.int32).reshape(1)
    values, mine, send, edge = project(core, frames_in.reshape(count, model), key_weight, value_weight, width)
    total = mine + swapped(send, "space", 1).astype(F32)
    halo = swapped(edge, "space", 1)
    local, qfeat = local_branch(core, values, halo, queries.reshape(count, inner), conv_weight, width)
    prefix = total
    bit = 1
    while bit < lax.axis_size("tm"):
        other = swapped(total.astype(BF16), "tm", bit).astype(F32)
        prefix = prefix + jnp.where(frame & bit != 0, other, 0.0)
        total = total + other
        bit *= 2
    prefix = prefix.astype(BF16)
    pair = swapped(prefix, "space", 1)
    low = jnp.where(core_index == 0, prefix, pair)
    high = jnp.where(core_index == 0, pair, prefix)
    whole = jnp.concatenate([low, high], axis=0)
    mixed = attend(whole, qfeat, local, norm_gain.reshape(1, inner))
    return mixed.reshape(1, rows, width, inner)


def solution(mesh):
    in_specs = (
        P(("groups", "tm"), "space", None, None),
        P(("groups", "tm"), "space", None, None),
        P(),
        P(),
        P(),
        P(),
    )
    out_specs = P(("groups", "tm"), "space", None, None)
    return jax.shard_map(shards, mesh=mesh, in_specs=in_specs, out_specs=out_specs, check_vma=False)
```

time: 215 us -> 68.5 us (0.32)
  the two profiles are of different devices: /device:TPU:29 before, /device:TPU:0 now
where the time goes in v1:
time: 68.5 us; the launch traced here: 68.2 us
  Pallas kernels  39.8 us (58%)
  waiting for transfers between devices  13.2 us (19%)
  starting transfers between devices  8.09 us (12%)
  other arithmetic  3.59 us (5%)
  local copies, waits for them, and re-layouts  3.45 us (5%)
    pallas_call x1, Pallas kernels, project(): pl.pallas_call(functools.partial(project_kernel, chunk=256, width=width),...  28.1 us
    ppermute x6, waiting for transfers between devices, swapped(): lax.ppermute(block, axis, [(i, i ^ bit) for i in range(lax.axis_size(axis...  13.2 us
    ppermute x6, starting transfers between devices, swapped(): lax.ppermute(block, axis, [(i, i ^ bit) for i in range(lax.axis_size(axis...  8.09 us
    pallas_call x1, Pallas kernels, local_branch(): pl.pallas_call(functools.partial(local_kernel, width=width, rows=rows), g...  6.57 us
    pallas_call x1, Pallas kernels, attend(): pl.pallas_call(attend_kernel, grid=(count // block,), in_specs=[pl.BlockS...  5.11 us
    unnamed x16, local copies, waits for them, and re-layouts  3.45 us
    convert_element_type x1, other arithmetic, shards(): prefix = prefix.astype(BF16)  1.85 us
  transfers between devices with their start and end apart: 6, of which 4 were waited for; matrix products, arithmetic and copies ran while one was open for 3% of the time, Pallas kernels for 10%

profile of v1, /device:TPU:0, one launch (start us, length us, event | category | flops | bytes accessed | tf_op | source)
XLA Modules:
  0.0 68.2 jit_solution(294328759027875186)
XLA Ops:
  0.0 0.0 copy-start.7
  0.0 0.0 copy-start
  0.0 0.0 copy-start.3
  0.0 28.1 %project.1 = (bf16[1280,1120]{1,0:T(8,128)(2,1)S(1)}, f32[56,1120]{1,0:T(8,128)S(1)}, bf16[56,1120]{1,0:T(8,128)(2,1)S(1)}, bf16[80,1120]{1,0:T(8,128)(2,1)}) custom-call(s32[1]{0:T(128)} %bitcast.core_ref, bf16[1280,2240]{1,0:T(8,128)(2,1)} %bitcast.5, bf16[2240,1120]{1,0:T(8,128)(2,1)} %wk_ref.1, bf16[2240,1120]{1,0:T(8,128)(2,1)} %wv_ref.1), custom_call_target="tpu_custom_call" | custom-call | flops 12845056000 | bytes 15769600 | tf_op jit(solution)/shard_map/project/pallas_call | solution.py:90
  28.1 0.0 copy-start.1
  28.2 1.6 %copy-done.1 = bf16[1280,1120]{1,0:T(8,128)(2,1)} copy-done((bf16[1280,1120]{1,0:T(8,128)(2,1)}, bf16[1280,1120]{1,0:T(8,128)(2,1)S(1)}, u32[]{:S(2)}) %copy-start.1) | copy-done | bytes 2867224
  29.7 0.5 collective-permute-start
  30.2 1.0 %collective-permute-done = bf16[56,1120]{1,0:T(8,128)(2,1)S(1)} collective-permute-done((bf16[56,1120]{1,0:T(8,128)(2,1)S(1)}, bf16[56,1120]{1,0:T(8,128)(2,1)S(1)}, u32[]{:S(2)}, u32[]{:S(2)}) %collective-permute-start) | collective-permute-done | bytes 125472 | tf_op jit(solution)/shard_map/ppermute | solution.py:249
  31.2 0.0 copy-start.4
  31.2 2.9 %collective-permute-start.1 = (bf16[56,1120]{1,0:T(8,128)(2,1)S(1)}, bf16[56,1120]{1,0:T(8,128)(2,1)S(1)}, u32[]{:S(2)}, u32[]{:S(2)}) collective-permute-start(bf16[56,1120]{1,0:T(8,128)(2,1)S(1)} %fusion.6), channel_id=1, source_target_pairs={{0,2},{2,0},{4,6},{6,4},{8,10},{10,8},{12,14},{14,12},{1,3},{3,1},... | collective-permute-start | bytes 376328 | tf_op jit(solution)/shard_map/ppermute | solution.py:249
  34.2 3.8 %collective-permute-done.1 = bf16[56,1120]{1,0:T(8,128)(2,1)S(1)} collective-permute-done((bf16[56,1120]{1,0:T(8,128)(2,1)S(1)}, bf16[56,1120]{1,0:T(8,128)(2,1)S(1)}, u32[]{:S(2)}, u32[]{:S(2)}) %collective-permute-start.1) | collective-permute-done | bytes 125472 | tf_op jit(solution)/shard_map/ppermute | solution.py:249
  37.9 0.0 copy-start.5
  38.0 1.9 %collective-permute-start.2 = (bf16[56,1120]{1,0:T(8,128)(2,1)S(1)}, bf16[56,1120]{1,0:T(8,128)(2,1)S(1)}, u32[]{:S(2)}, u32[]{:S(2)}) collective-permute-start(bf16[56,1120]{1,0:T(8,128)(2,1)S(1)} %fusion.5), channel_id=1, source_target_pairs={{0,4},{2,6},{4,0},{6,2},{8,12},{10,14},{12,8},{14,10},{1,5},{3,7},... | collective-permute-start | bytes 376328 | tf_op jit(solution)/shard_map/ppermute | solution.py:249
  39.9 3.2 %collective-permute-done.2 = bf16[56,1120]{1,0:T(8,128)(2,1)S(1)} collective-permute-done((bf16[56,1120]{1,0:T(8,128)(2,1)S(1)}, bf16[56,1120]{1,0:T(8,128)(2,1)S(1)}, u32[]{:S(2)}, u32[]{:S(2)}) %collective-permute-start.2) | collective-permute-done | bytes 125472 | tf_op jit(solution)/shard_map/ppermute | solution.py:249
  43.1 0.0 copy-start.6
  43.1 0.7 %fusion.4 = bf16[56,1120]{1,0:T(8,128)(2,1)} fusion(bf16[56,1120]{1,0:T(8,128)(2,1)S(1)} %collective-permute-done.2, bf16[56,1120]{1,0:T(8,128)(2,1)S(1)} %collective-permute-done.1, f32[56,1120]{1,0:T(8,128)S(1)} %get-tuple-element.11, bf16[56,1120]{1,0:T(8,128)(2,1)S(1)} %collective-permute-done), kind=kLoop, calls=%fused_computation.8 | loop fusion | flops 439040 | bytes 752640 | tf_op jit(solution)/shard_map/convert_element_type | solution.py:266
  43.8 2.8 %collective-permute-start.3 = (bf16[56,1120]{1,0:T(8,128)(2,1)}, bf16[56,1120]{1,0:T(8,128)(2,1)}, u32[]{:S(2)}, u32[]{:S(2)}) collective-permute-start(bf16[56,1120]{1,0:T(8,128)(2,1)} %fusion.4), channel_id=1, source_target_pairs={{0,8},{2,10},{4,12},{6,14},{8,0},{10,2},{12,4},{14,6},{1,9},{3,11}... | collective-permute-start | bytes 376328 | tf_op jit(solution)/shard_map/ppermute | solution.py:249
  46.5 0.0 copy-done.4
  46.5 0.0 copy-done.5
  46.5 0.0 copy-done.6
  46.5 0.1 collective-permute-start.5
  46.6 5.2 %collective-permute-done.3 = bf16[56,1120]{1,0:T(8,128)(2,1)} collective-permute-done((bf16[56,1120]{1,0:T(8,128)(2,1)}, bf16[56,1120]{1,0:T(8,128)(2,1)}, u32[]{:S(2)}, u32[]{:S(2)}) %collective-permute-start.3) | collective-permute-done | bytes 125472 | tf_op jit(solution)/shard_map/ppermute | solution.py:249
  51.8 1.8 %fusion.3 = bf16[56,1120]{1,0:T(8,128)(2,1)} fusion(bf16[56,1120]{1,0:T(8,128)(2,1)} %copy-done.5, bf16[56,1120]{1,0:T(8,128)(2,1)} %copy-done.6, bf16[56,1120]{1,0:T(8,128)(2,1)} %collective-permute-done.3, pred[]{:T(512)S(6)} %ne.11, pred[]{:T(512)S(6)} %ne.10, pred[]{:T(512)S(6)} %ne.9, f32[56,1120]{1,0:T(8,128)S(1)} %get-tuple-element.11, ...), kind=kLoop, calls=%fused_computation.7 | loop fusion | flops 752640 | bytes 878083 | tf_op jit(solution)/shard_map/convert_element_type | solution.py:270
  53.7 0.0 collective-permute-start.4
  53.7 0.0 copy-done.7
  53.7 0.0 collective-permute-done.5.halo_ref
  53.7 0.0 copy-done
  53.7 0.0 copy-done.3
  53.7 0.0 copy-start.2
  53.8 1.8 %copy-done.2 = bf16[1280,1120]{1,0:T(8,128)(2,1)S(1)} copy-done((bf16[1280,1120]{1,0:T(8,128)(2,1)S(1)}, bf16[1280,1120]{1,0:T(8,128)(2,1)}, u32[]{:S(2)}) %copy-start.2) | copy-done | bytes 2867224
  55.6 6.6 %local_branch.1 = (f32[1280,1120]{1,0:T(8,128)S(1)}, bf16[1280,1120]{1,0:T(8,128)(2,1)S(1)}) custom-call(s32[1]{0:T(128)} %bitcast.core_ref, bf16[1280,1120]{1,0:T(8,128)(2,1)S(1)} %copy-done.2, bf16[80,1120]{1,0:T(8,128)(2,1)S(1)} %collective-permute-done.5.halo_ref, bf16[1280,1120]{1,0:T(8,128)(2,1)S(1)} %bitcast.4, f32[9,1120]{1,0:T(8,128)S(1)} %copy-done.3), custom_call_target="tpu_custom_call" | custom-call | flops 28672000 | bytes 17203200 | tf_op jit(solution)/shard_map/local_branch/pallas_call | solution.py:165
  62.2 0.0 collective-permute-done.4
  62.2 0.9 %broadcast_select_fusion.1 = (bf16[56,1120]{1,0:T(8,128)(2,1)S(1)}, bf16[56,1120]{1,0:T(8,128)(2,1)S(1)}) fusion(bf16[56,1120]{1,0:T(8,128)(2,1)} %fusion.3, bf16[56,1120]{1,0:T(8,128)(2,1)S(1)} %collective-permute-done.4, pred[]{:T(512)S(6)} %eq.4), kind=kLoop, calls=%fused_computation.13 | loop fusion | flops 125440 | bytes 501761 | tf_op jit(solution)/shard_map/jit(_where)/select_n | solution.py:272
  63.1 5.1 %attend.1 = bf16[1280,1120]{1,0:T(8,128)(2,1)} custom-call(bf16[112,1120]{1,0:T(8,128)(2,1)S(1)} %pad_maximum_fusion.p_ref, bf16[1280,1120]{1,0:T(8,128)(2,1)S(1)} %get-tuple-element.15.qf_ref, f32[1280,1120]{1,0:T(8,128)S(1)} %get-tuple-element.16.local_ref, f32[1,1120]{1,0:T(1,128)S(1)} %reshape.18.gain_ref), custom_call_target="tpu_custom_call" | custom-call | flops 2936012800 | bytes 11468800 | tf_op jit(solution)/shard_map/attend/pallas_call | solution.py:228
  (4 shorter events, 0.1 us)
Async XLA Ops:
  0.0 53.7 %copy-start.7 = (f32[1120]{0:T(1024)S(1)}, f32[1120]{0:T(1024)}, u32[]{:S(2)}) copy-start(f32[1120]{0:T(1024)} %param.11) | copy-start | bytes 13444
  0.0 53.7 %copy-start = (bf16[1,16,80,1120]{3,2,1,0:T(8,128)(2,1)S(1)}, bf16[1,16,80,1120]{3,2,1,0:T(8,128)(2,1)}, u32[]{:S(2)}) copy-start(bf16[1,16,80,1120]{3,2,1,0:T(8,128)(2,1)} %param.7) | copy-start | bytes 8601604
  0.0 53.7 %copy-start.3 = (f32[9,1120]{1,0:T(8,128)S(1)}, f32[9,1120]{1,0:T(8,128)}, u32[]{:S(2)}) copy-start(f32[9,1120]{1,0:T(8,128)} %w_ref.1) | copy-start | bytes 120964
  28.1 1.6 %copy-start.1 = (bf16[1280,1120]{1,0:T(8,128)(2,1)}, bf16[1280,1120]{1,0:T(8,128)(2,1)S(1)}, u32[]{:S(2)}) copy-start(bf16[1280,1120]{1,0:T(8,128)(2,1)S(1)} %get-tuple-element.13.v_ref) | copy-start | bytes 8601604
  29.7 1.4 %collective-permute-start = (bf16[56,1120]{1,0:T(8,128)(2,1)S(1)}, bf16[56,1120]{1,0:T(8,128)(2,1)S(1)}, u32[]{:S(2)}, u32[]{:S(2)}) collective-permute-start(bf16[56,1120]{1,0:T(8,128)(2,1)S(1)} %get-tuple-element.12), channel_id=1, source_target_pairs={{0,1},{1,0},{2,3},{3,2},{4,5},{5,4},{6,7},{7,6},{8,9},{9,8},{10,11... | collective-permute-start | bytes 376328 | tf_op jit(solution)/shard_map/ppermute | solution.py:249
  31.2 15.3 %copy-start.4 = (bf16[56,1120]{1,0:T(8,128)(2,1)}, bf16[56,1120]{1,0:T(8,128)(2,1)S(1)}, u32[]{:S(2)}) copy-start(bf16[56,1120]{1,0:T(8,128)(2,1)S(1)} %collective-permute-done) | copy-start | bytes 376324
  31.2 6.7 %collective-permute-start.1 = (bf16[56,1120]{1,0:T(8,128)(2,1)S(1)}, bf16[56,1120]{1,0:T(8,128)(2,1)S(1)}, u32[]{:S(2)}, u32[]{:S(2)}) collective-permute-start(bf16[56,1120]{1,0:T(8,128)(2,1)S(1)} %fusion.6), channel_id=1, source_target_pairs={{0,2},{2,0},{4,6},{6,4},{8,10},{10,8},{12,14},{14,12},{1,3},{3,1},... | collective-permute-start | bytes 376328 | tf_op jit(solution)/shard_map/ppermute | solution.py:249
  37.9 8.6 %copy-start.5 = (bf16[56,1120]{1,0:T(8,128)(2,1)}, bf16[56,1120]{1,0:T(8,128)(2,1)S(1)}, u32[]{:S(2)}) copy-start(bf16[56,1120]{1,0:T(8,128)(2,1)S(1)} %collective-permute-done.1) | copy-start | bytes 376324
  38.0 5.1 %collective-permute-start.2 = (bf16[56,1120]{1,0:T(8,128)(2,1)S(1)}, bf16[56,1120]{1,0:T(8,128)(2,1)S(1)}, u32[]{:S(2)}, u32[]{:S(2)}) collective-permute-start(bf16[56,1120]{1,0:T(8,128)(2,1)S(1)} %fusion.5), channel_id=1, source_target_pairs={{0,4},{2,6},{4,0},{6,2},{8,12},{10,14},{12,8},{14,10},{1,5},{3,7},... | collective-permute-start | bytes 376328 | tf_op jit(solution)/shard_map/ppermute | solution.py:249
  43.1 3.5 %copy-start.6 = (bf16[56,1120]{1,0:T(8,128)(2,1)}, bf16[56,1120]{1,0:T(8,128)(2,1)S(1)}, u32[]{:S(2)}) copy-start(bf16[56,1120]{1,0:T(8,128)(2,1)S(1)} %collective-permute-done.2) | copy-start | bytes 376324
  43.8 8.1 %collective-permute-start.3 = (bf16[56,1120]{1,0:T(8,128)(2,1)}, bf16[56,1120]{1,0:T(8,128)(2,1)}, u32[]{:S(2)}, u32[]{:S(2)}) collective-permute-start(bf16[56,1120]{1,0:T(8,128)(2,1)} %fusion.4), channel_id=1, source_target_pairs={{0,8},{2,10},{4,12},{6,14},{8,0},{10,2},{12,4},{14,6},{1,9},{3,11}... | collective-permute-start | bytes 376328 | tf_op jit(solution)/shard_map/ppermute | solution.py:249
  46.5 7.2 %collective-permute-start.5 = (bf16[80,1120]{1,0:T(8,128)(2,1)}, bf16[80,1120]{1,0:T(8,128)(2,1)S(1)}, u32[]{:S(2)}, u32[]{:S(2)}) collective-permute-start(bf16[80,1120]{1,0:T(8,128)(2,1)} %get-tuple-element.14), channel_id=1, source_target_pairs={{0,1},{1,0},{2,3},{3,2},{4,5},{5,4},{6,7},{7,6},{8,9},{9,8},{10,11... | collective-permute-start | bytes 537608 | tf_op jit(solution)/shard_map/ppermute | solution.py:249
  53.7 8.5 %collective-permute-start.4 = (bf16[56,1120]{1,0:T(8,128)(2,1)}, bf16[56,1120]{1,0:T(8,128)(2,1)S(1)}, u32[]{:S(2)}, u32[]{:S(2)}) collective-permute-start(bf16[56,1120]{1,0:T(8,128)(2,1)} %fusion.3), channel_id=1, source_target_pairs={{0,1},{1,0},{2,3},{3,2},{4,5},{5,4},{6,7},{7,6},{8,9},{9,8},{10,11... | collective-permute-start | bytes 376328 | tf_op jit(solution)/shard_map/ppermute | solution.py:249
  53.7 1.8 %copy-start.2 = (bf16[1280,1120]{1,0:T(8,128)(2,1)S(1)}, bf16[1280,1120]{1,0:T(8,128)(2,1)}, u32[]{:S(2)}) copy-start(bf16[1280,1120]{1,0:T(8,128)(2,1)} %copy-done.1) | copy-start | bytes 8601604

commit v2 on v0

v2 whole, which is shorter than its diff:
```python
import functools

import jax
import jax.numpy as jnp
from jax import lax
from jax.experimental import pallas as pl
from jax.experimental.pallas import tpu as pltpu
from jax.sharding import PartitionSpec as P

HEAD = 112
TILE = 256
FIRST = 2 * TILE
F32 = jnp.float32
BF16 = jnp.bfloat16
MIB = 1 << 20
VMEM = pl.BlockSpec(memory_space=pltpu.VMEM)
SMEM = pl.BlockSpec(memory_space=pltpu.SMEM)


def feature_map(a):
    return jnp.where(a > 0, a + 1.0, jnp.exp(jnp.minimum(a, 0.0)))


def matmul(a, b):
    return jnp.dot(a, b, preferred_element_type=F32)


def shape(dims, kind=BF16):
    return jax.ShapeDtypeStruct(dims, kind)


def cost(flops, moved, transcendentals=0):
    return pl.CostEstimate(flops=flops, bytes_accessed=moved, transcendentals=transcendentals)


def params(mib):
    return pltpu.CompilerParams(vmem_limit_bytes=mib * MIB)


def packed_state(keys, base, values, low):
    columns = values.shape[1]
    first, last = low // HEAD, (low + columns - 1) // HEAD
    full = matmul(keys[first * HEAD - base : (last + 1) * HEAD - base, :], values)
    column = lax.broadcasted_iota(jnp.int32, (HEAD, columns), 1) + low
    total = jnp.zeros((HEAD, columns), F32)
    for h in range(first, last + 1):
        inside = (column >= h * HEAD) & (column < (h + 1) * HEAD)
        total = total + jnp.where(inside, full[(h - first) * HEAD : (h - first + 1) * HEAD, :], 0.0)
    return total


def split_state(core, state, mine_ref, send_ref):
    half = HEAD // 2
    mine_ref[...] = state[pl.ds(pl.multiple_of(core * half, 8), half), :]
    send_ref[...] = state[pl.ds(pl.multiple_of((1 - core) * half, 8), half), :].astype(BF16)


def first_kernel(
    core_ref, x_hbm, wk_hbm, wv_hbm, q_hbm, va_ref, keep_ref, mine_ref, send_ref, x_ref, wk_ref, wv_ref, q_ref,
    kt, state, tiles, row_sems, tile_sems, rest_sems
):
    count = x_ref.shape[0]
    parts = row_sems.shape[0]
    step = count // parts
    row_copies = [
        pltpu.make_async_copy(x_hbm.at[pl.ds(i * step, step), :], x_ref.at[pl.ds(i * step, step), :], row_sems.at[i])
        for i in range(parts)
    ]
    sources = [(wk_hbm, t) for t in range(3)] + [(wv_hbm, t) for t in range(2)]
    tile_copies = [
        pltpu.make_async_copy(source.at[:, pl.ds(t * TILE, TILE)], tiles.at[i], tile_sems.at[i])
        for i, (source, t) in enumerate(sources)
    ]
    inner = wk_hbm.shape[1]
    rest_copies = [
        pltpu.make_async_copy(wk_hbm.at[:, pl.ds(3 * TILE, inner - 3 * TILE)], wk_ref, rest_sems.at[0]),
        pltpu.make_async_copy(wv_hbm.at[:, pl.ds(FIRST, inner - FIRST)], wv_ref, rest_sems.at[1]),
        pltpu.make_async_copy(q_hbm, q_ref, rest_sems.at[2]),
    ]

    def keys(t, rows):
        kt[t * TILE : (t + 1) * TILE, rows] = feature_map(matmul(x_ref[rows, :], tiles[t])).astype(BF16).T

    def go(*cs):
        for c in cs:
            c.start()

    def end(*cs):
        for c in cs:
            c.wait()

    whole = slice(0, count)
    low, high = slice(0, step), slice(step, count)
    r, t5, rest = row_copies, tile_copies, rest_copies

    go(t5[0], t5[1], r[0], r[1])
    end(t5[0], t5[1], r[0])
    go(*t5[2:])
    keys(0, low)
    keys(1, low)
    end(r[1])
    go(*rest)
    keys(0, high)
    keys(1, high)
    end(*t5[2:])
    keys(2, whole)
    for t in range(2):
        va_ref[:, t * TILE : (t + 1) * TILE] = matmul(x_ref[...], tiles[3 + t]).astype(BF16)
    for t in range(2):
        low = t * TILE
        state[:, low : low + TILE] = packed_state(kt, 0, va_ref[:, low : low + TILE], low)
    keep_ref[...] = kt[FIRST // HEAD * HEAD : 3 * TILE, :]
    split_state(core_ref[0], state, mine_ref, send_ref)
    for copy in rest_copies:
        copy.wait()


HBM = pl.BlockSpec(memory_space=pltpu.HBM)


def first_part(core, flat, key_weight, value_weight, queries):
    count, model = flat.shape
    inner = key_weight.shape[1]
    half = HEAD // 2
    kept = 3 * TILE - FIRST // HEAD * HEAD
    return pl.pallas_call(
        first_kernel,
        in_specs=[SMEM] + [HBM] * 4,
        out_specs=[VMEM] * 8,
        scratch_shapes=[
            pltpu.VMEM((3 * TILE, count), BF16),
            pltpu.VMEM((HEAD, FIRST), F32),
            pltpu.VMEM((5, model, TILE), BF16),
            pltpu.SemaphoreType.DMA((2,)),
            pltpu.SemaphoreType.DMA((5,)),
            pltpu.SemaphoreType.DMA((3,)),
        ],
        out_shape=[
            shape((count, FIRST)),
            shape((kept, count)),
            shape((half, FIRST), F32),
            shape((half, FIRST)),
            shape((count, model)),
            shape((model, inner - 3 * TILE)),
            shape((model, inner - FIRST)),
            shape((count, inner)),
        ],
        compiler_params=params(18),
        cost_estimate=cost(10 * count * model * TILE, 2 * model * (count + 5 * TILE)),
        name="first_part",
    )(core, *(pltpu.with_memory_space_constraint(a, pltpu.HBM) for a in (flat, key_weight, value_weight, queries)))


def keys_kernel(order_ref, x_ref, wk_ref, k_ref):
    k_ref[...] = feature_map(matmul(x_ref[...], wk_ref[:, :TILE])).astype(BF16).T


def keys_part(order, flat, key_weight):
    count, model = flat.shape
    return pl.pallas_call(
        keys_kernel,
        in_specs=[SMEM, VMEM, VMEM],
        out_specs=VMEM,
        out_shape=shape((TILE, count)),
        compiler_params=params(6),
        cost_estimate=cost(2 * count * model * TILE, 2 * model * count),
        name="keys_part",
    )(order, flat, key_weight)


def pair_span(pair):
    start = 2 * HEAD * pair
    base = start // 128 * 128
    return base, start - base, 256 if start - base + 2 * HEAD <= 256 else 384


def paired(block, base, pair, limit):
    low, offset, wide = pair_span(pair)
    piece = block[:, low - base : min(low + wide, limit) - base]
    if piece.shape[1] < wide:
        piece = jnp.concatenate([piece, jnp.zeros((piece.shape[0], wide - piece.shape[1]), piece.dtype)], axis=1)
    if offset:
        piece = pltpu.roll(piece, wide - offset, 1)
    return piece[:, :256]


def mixed_kernel(order_ref, x_ref, wk_ref, wv_ref, k_ref, v_ref, both):
    rest = k_ref.shape[0]
    both[...] = jnp.zeros_like(both)
    both[:, :rest] = wk_ref[:, TILE:]
    both[:, 128 : 128 + rest] = wv_ref[:, 2 * TILE :]
    v_ref[:, :TILE] = matmul(x_ref[...], wv_ref[:, :TILE]).astype(BF16)
    out = matmul(x_ref[...], both[...])
    k_ref[...] = feature_map(out[:, :128]).astype(BF16).T[:rest, :]
    v_ref[:, TILE:] = out[:, 128 : 128 + rest].astype(BF16)


def mixed_part(order, flat, wk, wv):
    count, model = flat.shape
    rest = wk.shape[1] - TILE
    return pl.pallas_call(
        mixed_kernel,
        in_specs=[SMEM] + [VMEM] * 3,
        out_specs=[VMEM] * 2,
        out_shape=[shape((rest, count)), shape((count, TILE + rest))],
        scratch_shapes=[pltpu.VMEM((model, TILE), BF16)],
        compiler_params=params(10),
        cost_estimate=cost(4 * count * model * TILE, 2 * model * count),
        name="mixed_part",
    )(order, flat, wk, wv)


def last_kernel(core_ref, x_ref, wv_ref, ka_ref, kb_ref, kc_ref, va_ref, vb_ref, v_ref, mine_ref, send_ref, edge_ref, kt, state):
    width = edge_ref.shape[0]
    count = x_ref.shape[0]
    base = FIRST // HEAD * HEAD
    at = 0
    for part in (ka_ref, kb_ref, kc_ref):
        kt[at : at + part.shape[0], :] = part[...]
        at += part.shape[0]
    state[:, :TILE] = packed_state(kt, base, vb_ref[:, :TILE], FIRST)
    state[:, 2 * TILE :] = packed_state(kt, base, vb_ref[:, TILE:], 4 * TILE)
    v_ref[...] = matmul(x_ref[...], wv_ref[:, TILE : 2 * TILE]).astype(BF16)
    state[:, TILE : 2 * TILE] = packed_state(kt, base, v_ref[...], 3 * TILE)
    core = core_ref[0]
    split_state(core, state, mine_ref, send_ref)
    rows = pl.ds(pl.multiple_of((1 - core) * (count - width), 16), width)
    edge_ref[:, :FIRST] = va_ref[rows, :]
    edge_ref[:, FIRST : 3 * TILE] = vb_ref[rows, :TILE]
    edge_ref[:, 3 * TILE : 4 * TILE] = v_ref[rows, :]
    edge_ref[:, 4 * TILE :] = vb_ref[rows, TILE:]


def last_part(core, flat, value_weight, ka, kb, kc, va, vb, width):
    count, model = flat.shape
    inner = value_weight.shape[1] + FIRST
    half = HEAD // 2
    return pl.pallas_call(
        last_kernel,
        in_specs=[SMEM] + [VMEM] * 7,
        out_specs=[VMEM] * 4,
        out_shape=[
            shape((count, TILE)),
            shape((half, inner - FIRST), F32),
            shape((half, inner - FIRST)),
            shape((width, inner)),
        ],
        scratch_shapes=[
            pltpu.VMEM((inner - FIRST // HEAD * HEAD, count), BF16),
            pltpu.VMEM((HEAD, inner - FIRST), F32),
        ],
        compiler_params=params(10),
        cost_estimate=cost(3 * count * model * TILE, 2 * model * count),
        name="last_part",
    )(core, flat, value_weight, ka, kb, kc, va, vb)


def phi_kernel(order_ref, q_ref, qf_ref):
    inner = q_ref.shape[1]
    step = 160

    def rows(i, carry):
        here = pl.ds(pl.multiple_of(i * step, 16), step)
        for pair in range(inner // (2 * HEAD)):
            low, _, wide = pair_span(pair)
            q = q_ref[here, low : min(low + wide, inner)].astype(F32)
            q = feature_map(paired(q, low, pair, inner))
            qf_ref[here, pair * 256 : (pair + 1) * 256] = q.astype(BF16)
        return carry

    lax.fori_loop(0, q_ref.shape[0] // step, rows, 0)


def phi_queries(order, queries):
    count, inner = queries.shape
    pairs = inner // (2 * HEAD)
    return pl.pallas_call(
        phi_kernel,
        in_specs=[SMEM, VMEM],
        out_specs=VMEM,
        out_shape=shape((count, pairs * 256)),
        compiler_params=params(4),
        cost_estimate=cost(8 * count * inner, 4 * count * inner, count * inner),
        name="phi_queries",
    )(order, queries)


def row_branch(taps, w_ref, low, high):
    side = []
    for c in range(3):
        acc = taps[0] * w_ref[c : c + 1, low:high]
        acc = acc + taps[1] * w_ref[3 + c : 4 + c, low:high]
        side.append(acc + taps[2] * w_ref[6 + c : 7 + c, low:high])
    width = side[0].shape[0]
    place = lax.broadcasted_iota(jnp.int32, side[0].shape, 0)
    left = jnp.where(place > 0, pltpu.roll(side[0], 1, 0), 0.0)
    right = jnp.where(place < width - 1, pltpu.roll(side[2], width - 1, 0), 0.0)
    return side[1] + left + right


def lane_parts(va_ref, vb_ref, vc_ref, inner):
    for low in range(0, inner, 128):
        high = min(low + 128, inner)
        if low < FIRST:
            yield va_ref, low, low, high
        elif low < 3 * TILE:
            yield vb_ref, low - FIRST, low, high
        elif low < 4 * TILE:
            yield vc_ref, low - 3 * TILE, low, high
        else:
            yield vb_ref, low - 4 * TILE + TILE, low, high


def inner_rows(refs, w_ref, out_ref, width, first, number, at):
    va_ref, vb_ref, vc_ref = refs
    inner = out_ref.shape[1]

    def row(r, carry):
        here = pl.ds(pl.multiple_of((at + r) * width, 16), width)
        for ref, lane, low, high in lane_parts(va_ref, vb_ref, vc_ref, inner):
            taps = [
                ref[pl.ds(pl.multiple_of((first + r + d - 1) * width, 16), width), lane : lane + high - low].astype(F32)
                for d in range(3)
            ]
            out_ref[here, low:high] = row_branch(taps, w_ref, low, high)
        return carry

    lax.fori_loop(0, number, row, 0)


def middle_kernel(order_ref, va_ref, vb_ref, vc_ref, w_ref, out_ref, *, width):
    rows = va_ref.shape[0] // width
    inner_rows((va_ref, vb_ref, vc_ref), w_ref, out_ref, width, rows // 4, rows // 2, 0)


def border_kernel(core_ref, va_ref, vb_ref, vc_ref, halo_ref, w_ref, out_ref, *, width):
    rows = va_ref.shape[0] // width
    quarter = rows // 4
    refs = (va_ref, vb_ref, vc_ref)
    inner = out_ref.shape[1]
    inner_rows(refs, w_ref, out_ref, width, 1, quarter - 1, 1)
    inner_rows(refs, w_ref, out_ref, width, rows - quarter, quarter - 1, quarter)
    core = core_ref[0]
    top = (core == 1).astype(F32)
    bottom = (core == 0).astype(F32)
    last = (rows - 1) * width
    for ref, lane, low, high in lane_parts(*refs, inner):
        lanes = slice(lane, lane + high - low)
        halo = halo_ref[:, low:high].astype(F32)
        taps = [halo * top] + [ref[d * width : (d + 1) * width, lanes].astype(F32) for d in range(2)]
        out_ref[:width, low:high] = row_branch(taps, w_ref, low, high)
        taps = [ref[last + d * width : last + (d + 1) * width, lanes].astype(F32) for d in (-1, 0)] + [halo * bottom]
        end = (2 * quarter - 1) * width
        out_ref[end : end + width, low:high] = row_branch(taps, w_ref, low, high)


def local_rows(order, va, vb, vc, halo, conv_weight, width):
    count = va.shape[0]
    inner = conv_weight.shape[1]
    kernel = middle_kernel if halo is None else border_kernel
    operands = [va, vb, vc] + ([] if halo is None else [halo]) + [conv_weight]
    return pl.pallas_call(
        functools.partial(kernel, width=width),
        in_specs=[SMEM] + [VMEM] * len(operands),
        out_specs=VMEM,
        out_shape=shape((count // 2, inner), F32),
        compiler_params=params(4),
        cost_estimate=cost(10 * count * inner, 4 * count * inner),
        name="middle_rows" if halo is None else "border_rows",
    )(order, *operands)


def halves(core, own, other):
    own, other = own.astype(F32), other.astype(F32)
    return jnp.concatenate([jnp.where(core == 0, own, other), jnp.where(core == 0, other, own)], axis=0)


def pair_matrix(state, base, pair, limit):
    block = paired(state, base, pair, limit)
    column = lax.broadcasted_iota(jnp.int32, block.shape, 1)
    top = jnp.where(column < HEAD, block, 0.0)
    bottom = jnp.where((column >= HEAD) & (column < 2 * HEAD), block, 0.0)
    rest = jnp.zeros((256 - 2 * HEAD, 256), F32)
    return jnp.concatenate([top, bottom, rest], axis=0).astype(BF16)


def head_sums():
    row = lax.broadcasted_iota(jnp.int32, (256, 256), 0)
    column = lax.broadcasted_iota(jnp.int32, (256, 256), 1)
    first = (row < HEAD) & (column < HEAD)
    second = (row >= HEAD) & (row < 2 * HEAD) & (column >= HEAD) & (column < 2 * HEAD)
    return jnp.where(first | second, 1.0, 0.0).astype(BF16)


def normed_pair(qf, matrix, sums):
    attn = matmul(qf, matrix)
    total = matmul((attn * attn).astype(BF16), sums)
    return attn * lax.rsqrt(total * (1.0 / HEAD) + 1e-06)


def placed(normed, pairs, low, high):
    tiles = {}
    for pair, block in zip(pairs, normed):
        base, offset, wide = pair_span(pair)
        if wide > 256:
            block = jnp.concatenate([block, jnp.zeros((block.shape[0], wide - 256), F32)], axis=1)
        if offset:
            block = pltpu.roll(block, offset, 1)
        for t in range(wide // 128):
            at = base + t * 128
            piece = block[:, t * 128 : (t + 1) * 128]
            tiles[at] = tiles[at] + piece if at in tiles else piece
    for at in range(low, high, 128):
        yield at, min(at + 128, high), tiles[at][:, : min(128, high - at)]


CHUNK = 640


def early_kernel(core_ref, own_ref, other_ref, qf_ref, out_ref):
    state = halves(core_ref[0], own_ref[...], other_ref[...])
    sums = head_sums()
    pairs = range(FIRST // (2 * HEAD))
    matrices = [pair_matrix(state, 0, pair, FIRST) for pair in pairs]
    for at in range(0, qf_ref.shape[0], CHUNK):
        rows = slice(at, at + CHUNK)
        normed = [normed_pair(qf_ref[rows, pair * 256 : (pair + 1) * 256], matrices[pair], sums) for pair in pairs]
        for low, high, tile in placed(normed, pairs, 0, FIRST):
            out_ref[rows, low:high] = tile


def early_heads(core, own, other, qfeat):
    count = qfeat.shape[0]
    return pl.pallas_call(
        early_kernel,
        in_specs=[SMEM] + [VMEM] * 3,
        out_specs=VMEM,
        out_shape=shape((count, FIRST), F32),
        compiler_params=params(8),
        cost_estimate=cost(4 * count * FIRST * 512, 4 * count * FIRST),
        name="early_heads",
    )(core, own, other, qfeat)


def late_kernel(
    core_ref, owna_ref, othera_ref, ownb_ref, otherb_ref, qf_ref, mid_ref, edge_ref, early_ref, gain_ref, out_hbm,
    out, sems
):
    core = core_ref[0]
    count, inner = out_hbm.shape
    quarter = count // 4
    first = FIRST // (2 * HEAD)
    low = 2 * HEAD * first // 128 * 128
    state = jnp.concatenate(
        [halves(core, owna_ref[:, low:], othera_ref[:, low:]), halves(core, ownb_ref[...], otherb_ref[...])], axis=1
    )
    sums = head_sums()
    pairs = range(first, inner // (2 * HEAD))
    matrices = [pair_matrix(state, low, pair, inner) for pair in pairs]
    local = [edge_ref.at[:quarter], mid_ref.at[:quarter], mid_ref.at[quarter:], edge_ref.at[quarter:]]
    copies = []
    for at in range(0, count, CHUNK):
        rows = slice(at, at + CHUNK)
        normed = [
            normed_pair(qf_ref[rows, pair * 256 : (pair + 1) * 256], matrices[pair - first], sums) for pair in pairs
        ]
        later = {a: (b, tile) for a, b, tile in placed(normed, pairs, low, inner)}
        for part in range(at // quarter, (at + CHUNK) // quarter):
            here = slice(part * quarter, (part + 1) * quarter)
            inside = slice(part * quarter - at, (part + 1) * quarter - at)
            for a in range(0, inner, 128):
                b, tile = later.get(a, (a + 128, None))
                value = 0.0 if tile is None else tile[inside]
                if a < FIRST:
                    value = value + early_ref[here, a:b]
                out[here, a:b] = (value * gain_ref[:, a:b] + local[part][:, a:b]).astype(BF16)
            copies.append(pltpu.make_async_copy(out.at[here], out_hbm.at[here], sems.at[part]))
            copies[-1].start()
    for copy in copies:
        copy.wait()


def late_heads(core, first, second, qfeat, mid, edge, early, gain):
    count, inner = qfeat.shape[0], gain.shape[1]
    return pl.pallas_call(
        late_kernel,
        in_specs=[SMEM] + [VMEM] * 9,
        out_specs=HBM,
        scratch_shapes=[pltpu.VMEM((count, inner), BF16), pltpu.SemaphoreType.DMA((4,))],
        out_shape=shape((count, inner)),
        compiler_params=params(14),
        cost_estimate=cost(4 * count * inner * 512, 8 * count * inner),
        name="late_heads",
    )(core, *first, *second, qfeat, mid, edge, early, gain)


def swapped(block, axis, bit):
    return lax.ppermute(block, axis, [(i, i ^ bit) for i in range(lax.axis_size(axis))])


class Chain:
    def __init__(self, mine, send, masks):
        self.masks = list(masks)
        self.total = self.prefix = mine
        self.send = send
        self.received = None
        bits = [1 << b for b in range(len(self.masks))]
        self.rounds = [("space", 1)] + [("tm", bit) for bit in bits] + [("space", 0)]
        self.at = 0

    def done(self):
        return self.at == len(self.rounds)

    def left(self):
        return len(self.rounds) - self.at

    def start(self, send):
        axis, bit = self.rounds[self.at]
        self.send = send
        self.received = swapped(send, axis, bit or 1)

    def finish(self, received):
        axis, bit = self.rounds[self.at]
        self.at += 1
        self.received = None
        if bit == 0:
            self.result = (self.send, received)
            return
        received = received.astype(F32)
        if axis == "space":
            self.prefix = self.total + received
        else:
            self.prefix = self.prefix + self.masks.pop(0) * received
        self.total = self.total + received
        last = self.rounds[self.at][1] == 0
        self.send = (self.prefix if last else self.total).astype(BF16)


def shards(frames_in, queries, key_weight, value_weight, conv_weight, norm_gain):
    _, rows, width, model = frames_in.shape
    inner = key_weight.shape[1]
    count = rows * width
    core = lax.axis_index("space").astype(jnp.int32).reshape(1)
    flat = frames_in.reshape(count, model)
    gain = norm_gain.reshape(1, inner)
    frame = lax.axis_index("tm")
    masks = [(frame >> b & 1).astype(F32) for b in range((lax.axis_size("tm") - 1).bit_length())]
    core, masks = lax.optimization_barrier((core, masks))

    def slot(filler, starts=(), ends=(), extra=None):
        held, extra, order = lax.optimization_barrier((tuple(c.send for c in starts), extra, core))
        for c, send in zip(starts, held):
            c.start(send)
        moved = None if extra is None else swapped(extra, "space", 1)
        out = None if filler is None else filler(order)
        received, moved, out = lax.optimization_barrier((tuple(c.received for c in ends), moved, out))
        for c, r in zip(ends, received):
            c.finish(r)
        return out if extra is None else (out, moved)

    va, ka, mine, send, x, wk, wv, q = first_part(
        core, flat, key_weight, value_weight, queries.reshape(count, inner)
    )
    first = Chain(mine, send, masks)
    kb = slot(lambda order: keys_part(order, x, wk), [first], [first])
    kc, vb = slot(lambda order: mixed_part(order, x, wk, wv), [first], [first])
    vc, mine, send, edge = slot(
        lambda order: last_part(order, x, wv, ka, kb, kc, va, vb, width), [first], [first]
    )
    second = Chain(mine, send, masks)
    qfeat, halo = slot(lambda order: phi_queries(order, q), [second], [second], edge)
    fillers = [
        lambda order: local_rows(order, va, vb, vc, None, conv_weight, width),
        lambda order: local_rows(order, va, vb, vc, halo, conv_weight, width),
    ]
    local = []
    early = None
    while not second.done():
        filler = None
        if len(local) < 2:
            filler = fillers[len(local)]
        elif first.done() and early is None:
            filler = lambda order: early_heads(order, *first.result, qfeat)
        starts, ends = [second], [second]
        if not first.done():
            if first.received is None:
                starts = [second, first]
                if first.left() >= second.left() - 1:
                    ends = [second, first]
            else:
                ends = [second, first]
        out = slot(filler, starts, ends)
        if filler is not None and len(local) < 2:
            local.append(out)
        elif filler is not None:
            early = out
    mixed = late_heads(core, first.result, second.result, qfeat, *local, early, gain)
    return mixed.reshape(1, rows, width, inner)


def solution(mesh):
    in_specs = (
        P(("groups", "tm"), "space", None, None),
        P(("groups", "tm"), "space", None, None),
        P(),
        P(),
        P(),
        P(),
    )
    out_specs = P(("groups", "tm"), "space", None, None)
    return jax.shard_map(shards, mesh=mesh, in_specs=in_specs, out_specs=out_specs, check_vma=False)
```

time: 215 us -> 49.5 us (0.23)
  the two profiles are of different devices: /device:TPU:29 before, /device:TPU:0 now
where the time goes in v2:
time: 49.5 us; the launch traced here: 49.3 us
  Pallas kernels  31.9 us (64%)
  starting transfers between devices  12.8 us (26%)
  waiting for transfers between devices  4.02 us (8%)
    ppermute x11, starting transfers between devices, swapped(): lax.ppermute(block, axis, [(i, i ^ bit) for i in range(lax.axis_size(axis...  12.8 us
    pallas_call x1, Pallas kernels, first_part(): pl.pallas_call(first_kernel, in_specs=[SMEM] + [HBM] * 4, out_specs=[VMEM...  12.1 us
    pallas_call x2, Pallas kernels, local_rows(): pl.pallas_call(functools.partial(kernel, width=width), in_specs=[SMEM] +...  4.76 us
    ppermute x11, waiting for transfers between devices, swapped(): lax.ppermute(block, axis, [(i, i ^ bit) for i in range(lax.axis_size(axis...  4.02 us
    pallas_call x1, Pallas kernels, mixed_part(): pl.pallas_call(mixed_kernel, in_specs=[SMEM] + [VMEM] * 3, out_specs=[VME...  3.48 us
    pallas_call x1, Pallas kernels, late_heads(): pl.pallas_call(late_kernel, in_specs=[SMEM] + [VMEM] * 9, out_specs=HBM,...  3.27 us
    pallas_call x1, Pallas kernels, last_part(): pl.pallas_call(last_kernel, in_specs=[SMEM] + [VMEM] * 7, out_specs=[VMEM...  2.97 us
    pallas_call x1, Pallas kernels, phi_queries(): pl.pallas_call(phi_kernel, in_specs=[SMEM, VMEM], out_specs=VMEM, out_sha...  2.46 us
  transfers between devices with their start and end apart: 11, of which 5 were waited for; matrix products, arithmetic and copies ran while one was open for 0% of the time, Pallas kernels for 34%

profile of v2, /device:TPU:0, one launch (start us, length us, event | category | flops | bytes accessed | tf_op | source)
XLA Modules:
  0.0 49.3 jit_solution(6934873059358492157)
XLA Ops:
  0.0 12.1 %first_part.1 = (bf16[1280,512]{1,0:T(8,128)(2,1)S(1)}, bf16[320,1280]{1,0:T(8,128)(2,1)S(1)}, f32[56,512]{1,0:T(8,128)S(1)}, bf16[56,512]{1,0:T(8,128)(2,1)S(1)...) custom-call(s32[1]{0:T(128)} %bitcast.core_ref.order_ref, ...), custom_call_target="tpu_custom_call" | custom-call | flops 7340032000 | bytes 11468800 | tf_op jit(solution)/shard_map/first_part/pallas_call | solution.py:126
  12.1 0.5 %collective-permute-start = (bf16[56,512]{1,0:T(8,128)(2,1)S(1)}, bf16[56,512]{1,0:T(8,128)(2,1)S(1)}, u32[]{:S(2)}, u32[]{:S(2)}) collective-permute-start(bf16[56,512]{1,0:T(8,128)(2,1)S(1)} %get-tuple-element.66), channel_id=1, source_target_pairs={{0,1},{1,0},{2,3},{3,2},{4,5},{5,4},{6,7},{7,6},{8,9},{9,8},{10,11... | collective-permute-start | bytes 172040 | tf_op jit(solution)/shard_map/ppermute | solution.py:498
  12.6 1.8 %keys_part.1.kb_ref = bf16[256,1280]{1,0:T(8,128)(2,1)S(1)} custom-call(s32[1]{0:T(128)} %bitcast.core_ref.order_ref, bf16[1280,2240]{1,0:T(8,128)(2,1)S(1)} %get-tuple-element.68.x_ref, bf16[2240,352]{1,0:T(8,128)(2,1)S(1)} %get-tuple-element.69.wk_ref), custom_call_target="tpu_custom_call" | custom-call | flops 1468006400 | bytes 5734400 | tf_op jit(solution)/shard_map/keys_part/pallas_call | solution.py:160
  14.4 0.0 collective-permute-done
  14.5 2.6 %collective-permute-start.1 = (bf16[56,512]{1,0:T(8,128)(2,1)S(1)}, bf16[56,512]{1,0:T(8,128)(2,1)S(1)}, u32[]{:S(2)}, u32[]{:S(2)}) collective-permute-start(bf16[56,512]{1,0:T(8,128)(2,1)S(1)} %fusion.13), channel_id=1, source_target_pairs={{0,2},{2,0},{4,6},{6,4},{8,10},{10,8},{12,14},{14,12},{1,3},{3,1},... | collective-permute-start | bytes 172040 | tf_op jit(solution)/shard_map/ppermute | solution.py:498
  17.1 3.5 %mixed_part.1 = (bf16[96,1280]{1,0:T(8,128)(2,1)S(1)}, bf16[1280,352]{1,0:T(8,128)(2,1)S(1)}) custom-call(s32[1]{0:T(128)} %bitcast.core_ref.order_ref, bf16[1280,2240]{1,0:T(8,128)(2,1)S(1)} %get-tuple-element.68.x_ref, bf16[2240,352]{1,0:T(8,128)(2,1)S(1)} %get-tuple-element.69.wk_ref, bf16[2240,608]{1,0:T(8,128)(2,1)S(1)} %get-tuple-element.73.wv_ref), custom_call_target="tpu_custom_call" | custom-call | flops 2936012800 | bytes 5734400 | tf_op jit(solution)/shard_map/mixed_part/pallas_call | solution.py:201
  20.6 0.0 collective-permute-done.1
  20.6 1.6 %collective-permute-start.2 = (bf16[56,512]{1,0:T(8,128)(2,1)S(1)}, bf16[56,512]{1,0:T(8,128)(2,1)S(1)}, u32[]{:S(2)}, u32[]{:S(2)}) collective-permute-start(bf16[56,512]{1,0:T(8,128)(2,1)S(1)} %fusion.11), channel_id=1, source_target_pairs={{0,4},{2,6},{4,0},{6,2},{8,12},{10,14},{12,8},{14,10},{1,5},{3,7},... | collective-permute-start | bytes 172040 | tf_op jit(solution)/shard_map/ppermute | solution.py:498
  22.2 3.0 %last_part.1 = (bf16[1280,256]{1,0:T(8,128)(2,1)S(1)}, f32[56,608]{1,0:T(8,128)S(1)}, bf16[56,608]{1,0:T(8,128)(2,1)S(1)}, bf16[80,1120]{1,0:T(8,128)(2,1)S(1)}) custom-call(s32[1]{0:T(128)} %bitcast.core_ref.order_ref, bf16[1280,2240]{1,0:T(8,128)(2,1)S(1)} %get-tuple-element.68.x_ref, bf16[2240,608]{1,0:T(8,128)(2,1)S(1)} %get-tuple-element.73.wv_ref, ...), custom_call_target="tpu_custom_call" | custom-call | flops 2202009600 | bytes 5734400 | tf_op jit(solution)/shard_map/last_part/pallas_call | solution.py:238
  25.2 0.0 collective-permute-done.2
  25.2 0.1 collective-permute-start.3
  25.3 0.5 %collective-permute-start.4 = (bf16[80,1120]{1,0:T(8,128)(2,1)S(1)}, bf16[80,1120]{1,0:T(8,128)(2,1)S(1)}, u32[]{:S(2)}, u32[]{:S(2)}) collective-permute-start(bf16[80,1120]{1,0:T(8,128)(2,1)S(1)} %get-tuple-element.92), channel_id=1, source_target_pairs={{0,1},{1,0},{2,3},{3,2},{4,5},{5,4},{6,7},{7,6},{8,9},{9,8},{10,11... | collective-permute-start | bytes 537608 | tf_op jit(solution)/shard_map/ppermute | solution.py:498
  25.8 0.0 copy-start
  25.9 2.5 %phi_queries.1.qf_ref = bf16[1280,1280]{1,0:T(8,128)(2,1)S(1)} custom-call(s32[1]{0:T(128)} %bitcast.core_ref.order_ref, bf16[1280,1120]{1,0:T(8,128)(2,1)S(1)} %get-tuple-element.94.q_ref), custom_call_target="tpu_custom_call" | custom-call | flops 11468800 | bytes 5734400 | tf_op jit(solution)/shard_map/phi_queries/pallas_call | solution.py:277
  28.3 0.0 collective-permute-done.3
  28.3 0.0 collective-permute-done.4.halo_ref
  28.4 0.9 %collective-permute-start.5 = (bf16[56,608]{1,0:T(8,128)(2,1)S(1)}, bf16[56,608]{1,0:T(8,128)(2,1)S(1)}, u32[]{:S(2)}, u32[]{:S(2)}) collective-permute-start(bf16[56,608]{1,0:T(8,128)(2,1)S(1)} %fusion.12), channel_id=1, source_target_pairs={{0,2},{2,0},{4,6},{6,4},{8,10},{10,8},{12,14},{14,12},{1,3},{3,1},... | collective-permute-start | bytes 204296 | tf_op jit(solution)/shard_map/ppermute | solution.py:498
  29.3 0.0 copy-done
  29.3 2.4 %middle_rows.1.mid_ref = f32[640,1120]{1,0:T(8,128)S(1)} custom-call(s32[1]{0:T(128)} %bitcast.core_ref.order_ref, bf16[1280,512]{1,0:T(8,128)(2,1)S(1)} %get-tuple-element.82.va_ref, bf16[1280,352]{1,0:T(8,128)(2,1)S(1)} %get-tuple-element.83.vb_ref, bf16[1280,256]{1,0:T(8,128)(2,1)S(1)} %get-tuple-element.99.vc_ref, f32[9,1120]{1,0:T(8,128)S(1)} %copy-done), custom_call_target="tpu_custom_call" | custom-call | flops 14336000 | bytes 5734400 | tf_op jit(solution)/shard_map/middle_rows/pallas_call | solution.py:362
  31.6 1.1 %collective-permute-done.5 = bf16[56,608]{1,0:T(8,128)(2,1)S(1)} collective-permute-done((bf16[56,608]{1,0:T(8,128)(2,1)S(1)}, bf16[56,608]{1,0:T(8,128)(2,1)S(1)}, u32[]{:S(2)}, u32[]{:S(2)}) %collective-permute-start.5) | collective-permute-done | bytes 68128 | tf_op jit(solution)/shard_map/ppermute | solution.py:498
  32.8 0.0 copy-start.1
  32.8 1.2 %collective-permute-start.6 = (bf16[56,608]{1,0:T(8,128)(2,1)S(1)}, bf16[56,608]{1,0:T(8,128)(2,1)S(1)}, u32[]{:S(2)}, u32[]{:S(2)}) collective-permute-start(bf16[56,608]{1,0:T(8,128)(2,1)S(1)} %fusion.10), channel_id=1, source_target_pairs={{0,4},{2,6},{4,0},{6,2},{8,12},{10,14},{12,8},{14,10},{1,5},{3,7},... | collective-permute-start | bytes 204296 | tf_op jit(solution)/shard_map/ppermute | solution.py:498
  34.0 2.6 %collective-permute-start.7 = (bf16[56,512]{1,0:T(8,128)(2,1)S(1)}, bf16[56,512]{1,0:T(8,128)(2,1)S(1)}, u32[]{:S(2)}, u32[]{:S(2)}) collective-permute-start(bf16[56,512]{1,0:T(8,128)(2,1)S(1)} %fusion.9), channel_id=1, source_target_pairs={{0,8},{2,10},{4,12},{6,14},{8,0},{10,2},{12,4},{14,6},{1,9},{3,11}... | collective-permute-start | bytes 172040 | tf_op jit(solution)/shard_map/ppermute | solution.py:498
  36.6 2.4 %border_rows.1.edge_ref = f32[640,1120]{1,0:T(8,128)S(1)} custom-call(s32[1]{0:T(128)} %bitcast.core_ref.order_ref, bf16[1280,512]{1,0:T(8,128)(2,1)S(1)} %get-tuple-element.82.va_ref, bf16[1280,352]{1,0:T(8,128)(2,1)S(1)} %get-tuple-element.83.vb_ref, bf16[1280,256]{1,0:T(8,128)(2,1)S(1)} %get-tuple-element.99.vc_ref, ...), custom_call_target="tpu_custom_call" | custom-call | flops 14336000 | bytes 5734400 | tf_op jit(solution)/shard_map/border_rows/pallas_call | solution.py:362
  39.0 0.1 collective-permute-done.7
  39.1 0.0 collective-permute-done.6
  39.1 0.1 fusion.8.own_ref.owna_ref
  39.2 2.7 %collective-permute-start.8 = (bf16[56,608]{1,0:T(8,128)(2,1)S(1)}, bf16[56,608]{1,0:T(8,128)(2,1)S(1)}, u32[]{:S(2)}, u32[]{:S(2)}) collective-permute-start(bf16[56,608]{1,0:T(8,128)(2,1)S(1)} %fusion.4), channel_id=1, source_target_pairs={{0,8},{2,10},{4,12},{6,14},{8,0},{10,2},{12,4},{14,6},{1,9},{3,11}... | collective-permute-start | bytes 204296 | tf_op jit(solution)/shard_map/ppermute | solution.py:498
  41.9 0.0 collective-permute-start.9
  41.9 0.0 copy-done.1
  41.9 1.2 %collective-permute-done.9.other_ref.othera_ref = bf16[56,512]{1,0:T(8,128)(2,1)S(1)} collective-permute-done((bf16[56,512]{1,0:T(8,128)(2,1)S(1)}, bf16[56,512]{1,0:T(8,128)(2,1)S(1)}, u32[]{:S(2)}, u32[]{:S(2)}) %collective-permute-start.9) | collective-permute-done | bytes 57376 | tf_op jit(solution)/shard_map/ppermute | solution.py:498
  43.1 1.3 %collective-permute-done.8 = bf16[56,608]{1,0:T(8,128)(2,1)S(1)} collective-permute-done((bf16[56,608]{1,0:T(8,128)(2,1)S(1)}, bf16[56,608]{1,0:T(8,128)(2,1)S(1)}, u32[]{:S(2)}, u32[]{:S(2)}) %collective-permute-start.8) | collective-permute-done | bytes 68128 | tf_op jit(solution)/shard_map/ppermute | solution.py:498
  44.5 0.1 fusion.3.ownb_ref
  44.5 0.1 collective-permute-start.10
  44.6 1.0 %early_heads.1.early_ref = f32[1280,512]{1,0:T(8,128)S(1)} custom-call(s32[1]{0:T(128)} %bitcast.core_ref.order_ref, bf16[56,512]{1,0:T(8,128)(2,1)S(1)} %fusion.8.own_ref.owna_ref, bf16[56,512]{1,0:T(8,128)(2,1)S(1)} %collective-permute-done.9.other_ref.othera_ref, bf16[1280,1280]{1,0:T(8,128)(2,1)S(1)} %phi_queries.1.qf_ref), custom_call_target="tpu_custom_call" | custom-call | flops 1342177280 | bytes 2621440 | tf_op jit(solution)/shard_map/early_heads/pallas_call | solution.py:434
  45.7 0.2 collective-permute-done.10.otherb_ref
  45.9 3.3 %late_heads.1 = bf16[1280,1120]{1,0:T(8,128)(2,1)} custom-call(s32[1]{0:T(128)} %bitcast.core_ref.order_ref, bf16[56,512]{1,0:T(8,128)(2,1)S(1)} %fusion.8.own_ref.owna_ref, bf16[56,512]{1,0:T(8,128)(2,1)S(1)} %collective-permute-done.9.other_ref.othera_ref, bf16[56,608]{1,0:T(8,128)(2,1)S(1)} %fusion.3.ownb_ref, ...), custom_call_target="tpu_custom_call" | custom-call | flops 2936012800 | bytes 11468800 | tf_op jit(solution)/shard_map/late_heads/pallas_call | solution.py:485
  (7 shorter events, 0.2 us)
Async XLA Ops:
  12.1 2.4 %collective-permute-start = (bf16[56,512]{1,0:T(8,128)(2,1)S(1)}, bf16[56,512]{1,0:T(8,128)(2,1)S(1)}, u32[]{:S(2)}, u32[]{:S(2)}) collective-permute-start(bf16[56,512]{1,0:T(8,128)(2,1)S(1)} %get-tuple-element.66), channel_id=1, source_target_pairs={{0,1},{1,0},{2,3},{3,2},{4,5},{5,4},{6,7},{7,6},{8,9},{9,8},{10,11... | collective-permute-start | bytes 172040 | tf_op jit(solution)/shard_map/ppermute | solution.py:498
  14.5 6.1 %collective-permute-start.1 = (bf16[56,512]{1,0:T(8,128)(2,1)S(1)}, bf16[56,512]{1,0:T(8,128)(2,1)S(1)}, u32[]{:S(2)}, u32[]{:S(2)}) collective-permute-start(bf16[56,512]{1,0:T(8,128)(2,1)S(1)} %fusion.13), channel_id=1, source_target_pairs={{0,2},{2,0},{4,6},{6,4},{8,10},{10,8},{12,14},{14,12},{1,3},{3,1},... | collective-permute-start | bytes 172040 | tf_op jit(solution)/shard_map/ppermute | solution.py:498
  20.6 4.6 %collective-permute-start.2 = (bf16[56,512]{1,0:T(8,128)(2,1)S(1)}, bf16[56,512]{1,0:T(8,128)(2,1)S(1)}, u32[]{:S(2)}, u32[]{:S(2)}) collective-permute-start(bf16[56,512]{1,0:T(8,128)(2,1)S(1)} %fusion.11), channel_id=1, source_target_pairs={{0,4},{2,6},{4,0},{6,2},{8,12},{10,14},{12,8},{14,10},{1,5},{3,7},... | collective-permute-start | bytes 172040 | tf_op jit(solution)/shard_map/ppermute | solution.py:498
  25.2 3.1 %collective-permute-start.3 = (bf16[56,608]{1,0:T(8,128)(2,1)S(1)}, bf16[56,608]{1,0:T(8,128)(2,1)S(1)}, u32[]{:S(2)}, u32[]{:S(2)}) collective-permute-start(bf16[56,608]{1,0:T(8,128)(2,1)S(1)} %get-tuple-element.91), channel_id=1, source_target_pairs={{0,1},{1,0},{2,3},{3,2},{4,5},{5,4},{6,7},{7,6},{8,9},{9,8},{10,11... | collective-permute-start | bytes 204296 | tf_op jit(solution)/shard_map/ppermute | solution.py:498
  25.3 3.0 %collective-permute-start.4 = (bf16[80,1120]{1,0:T(8,128)(2,1)S(1)}, bf16[80,1120]{1,0:T(8,128)(2,1)S(1)}, u32[]{:S(2)}, u32[]{:S(2)}) collective-permute-start(bf16[80,1120]{1,0:T(8,128)(2,1)S(1)} %get-tuple-element.92), channel_id=1, source_target_pairs={{0,1},{1,0},{2,3},{3,2},{4,5},{5,4},{6,7},{7,6},{8,9},{9,8},{10,11... | collective-permute-start | bytes 537608 | tf_op jit(solution)/shard_map/ppermute | solution.py:498
  25.8 3.4 %copy-start = (f32[9,1120]{1,0:T(8,128)S(1)}, f32[9,1120]{1,0:T(8,128)}, u32[]{:S(2)}) copy-start(f32[9,1120]{1,0:T(8,128)} %w_ref.3) | copy-start | bytes 120964
  28.4 4.4 %collective-permute-start.5 = (bf16[56,608]{1,0:T(8,128)(2,1)S(1)}, bf16[56,608]{1,0:T(8,128)(2,1)S(1)}, u32[]{:S(2)}, u32[]{:S(2)}) collective-permute-start(bf16[56,608]{1,0:T(8,128)(2,1)S(1)} %fusion.12), channel_id=1, source_target_pairs={{0,2},{2,0},{4,6},{6,4},{8,10},{10,8},{12,14},{14,12},{1,3},{3,1},... | collective-permute-start | bytes 204296 | tf_op jit(solution)/shard_map/ppermute | solution.py:498
  32.8 9.1 %copy-start.1 = (f32[1120]{0:T(1024)S(1)}, f32[1120]{0:T(1024)}, u32[]{:S(2)}) copy-start(f32[1120]{0:T(1024)} %param.11) | copy-start | bytes 13444
  32.8 6.3 %collective-permute-start.6 = (bf16[56,608]{1,0:T(8,128)(2,1)S(1)}, bf16[56,608]{1,0:T(8,128)(2,1)S(1)}, u32[]{:S(2)}, u32[]{:S(2)}) collective-permute-start(bf16[56,608]{1,0:T(8,128)(2,1)S(1)} %fusion.10), channel_id=1, source_target_pairs={{0,4},{2,6},{4,0},{6,2},{8,12},{10,14},{12,8},{14,10},{1,5},{3,7},... | collective-permute-start | bytes 204296 | tf_op jit(solution)/shard_map/ppermute | solution.py:498
  34.0 5.1 %collective-permute-start.7 = (bf16[56,512]{1,0:T(8,128)(2,1)S(1)}, bf16[56,512]{1,0:T(8,128)(2,1)S(1)}, u32[]{:S(2)}, u32[]{:S(2)}) collective-permute-start(bf16[56,512]{1,0:T(8,128)(2,1)S(1)} %fusion.9), channel_id=1, source_target_pairs={{0,8},{2,10},{4,12},{6,14},{8,0},{10,2},{12,4},{14,6},{1,9},{3,11}... | collective-permute-start | bytes 172040 | tf_op jit(solution)/shard_map/ppermute | solution.py:498
  39.2 5.3 %collective-permute-start.8 = (bf16[56,608]{1,0:T(8,128)(2,1)S(1)}, bf16[56,608]{1,0:T(8,128)(2,1)S(1)}, u32[]{:S(2)}, u32[]{:S(2)}) collective-permute-start(bf16[56,608]{1,0:T(8,128)(2,1)S(1)} %fusion.4), channel_id=1, source_target_pairs={{0,8},{2,10},{4,12},{6,14},{8,0},{10,2},{12,4},{14,6},{1,9},{3,11}... | collective-permute-start | bytes 204296 | tf_op jit(solution)/shard_map/ppermute | solution.py:498
  41.9 1.2 %collective-permute-start.9 = (bf16[56,512]{1,0:T(8,128)(2,1)S(1)}, bf16[56,512]{1,0:T(8,128)(2,1)S(1)}, u32[]{:S(2)}, u32[]{:S(2)}) collective-permute-start(bf16[56,512]{1,0:T(8,128)(2,1)S(1)} %fusion.8.own_ref.owna_ref), channel_id=1, source_target_pairs={{0,1},{1,0},{2,3},{3,2},{4,5},{5,4},{6,7},{7,6},{8,9},{9,8},{10,11... | collective-permute-start | bytes 172040 | tf_op jit(solution)/shard_map/ppermute | solution.py:498
  44.5 1.3 %collective-permute-start.10 = (bf16[56,608]{1,0:T(8,128)(2,1)S(1)}, bf16[56,608]{1,0:T(8,128)(2,1)S(1)}, u32[]{:S(2)}, u32[]{:S(2)}) collective-permute-start(bf16[56,608]{1,0:T(8,128)(2,1)S(1)} %fusion.3.ownb_ref), channel_id=1, source_target_pairs={{0,1},{1,0},{2,3},{3,2},{4,5},{5,4},{6,7},{7,6},{8,9},{9,8},{10,11... | collective-permute-start | bytes 204296 | tf_op jit(solution)/shard_map/ppermute | solution.py:498

commit v3 on v2

v3 whole, which is shorter than its diff:
```python
import functools

import jax
import jax.numpy as jnp
from jax import lax
from jax.experimental import pallas as pl
from jax.experimental.pallas import tpu as pltpu
from jax.sharding import PartitionSpec as P

HEAD = 112
TILE = 256
FIRST = 2 * TILE
F32 = jnp.float32
BF16 = jnp.bfloat16
MIB = 1 << 20
VMEM = pl.BlockSpec(memory_space=pltpu.VMEM)
SMEM = pl.BlockSpec(memory_space=pltpu.SMEM)


def feature_map(a):
    return jnp.maximum(a, 0.0) + jnp.exp(jnp.minimum(a, 0.0))


def matmul(a, b):
    return jnp.dot(a, b, preferred_element_type=F32)


def shape(dims, kind=BF16):
    return jax.ShapeDtypeStruct(dims, kind)


def cost(flops, moved, transcendentals=0):
    return pl.CostEstimate(flops=flops, bytes_accessed=moved, transcendentals=transcendentals)


def params(mib):
    return pltpu.CompilerParams(vmem_limit_bytes=mib * MIB)


def packed_state(keys, base, values, low):
    columns = values.shape[1]
    first, last = low // HEAD, (low + columns - 1) // HEAD
    full = matmul(keys[first * HEAD - base : (last + 1) * HEAD - base, :], values)
    column = lax.broadcasted_iota(jnp.int32, (HEAD, columns), 1) + low
    total = jnp.zeros((HEAD, columns), F32)
    for h in range(first, last + 1):
        inside = (column >= h * HEAD) & (column < (h + 1) * HEAD)
        total = total + jnp.where(inside, full[(h - first) * HEAD : (h - first + 1) * HEAD, :], 0.0)
    return total


def split_state(core, state, mine_ref, send_ref):
    half = HEAD // 2
    mine_ref[...] = state[pl.ds(pl.multiple_of(core * half, 8), half), :]
    send_ref[...] = state[pl.ds(pl.multiple_of((1 - core) * half, 8), half), :].astype(BF16)


def project_kernel(
    core_ref, x_hbm, wk_hbm, wv_hbm, q_hbm, v_ref, mine_ref, send_ref, edge_ref, q_ref,
    x_ref, tiles, ends, both, kt, state, row_sems, tile_sems, rest_sems
):
    count, inner = v_ref.shape
    width = edge_ref.shape[0]
    full = inner // TILE
    rest = inner - full * TILE
    step = count // 2
    low, high, whole = slice(0, step), slice(step, count), slice(0, count)
    rows = [
        pltpu.make_async_copy(x_hbm.at[pl.ds(i * step, step), :], x_ref.at[pl.ds(i * step, step), :], row_sems.at[i])
        for i in range(2)
    ]
    sources = [(wk_hbm, t) for t in range(full)] + [(wv_hbm, t) for t in range(full)]
    copies = [
        pltpu.make_async_copy(source.at[:, pl.ds(t * TILE, TILE)], tiles.at[i], tile_sems.at[i])
        for i, (source, t) in enumerate(sources)
    ]
    copies += [
        pltpu.make_async_copy(source.at[:, pl.ds(full * TILE, rest)], ends.at[i], rest_sems.at[i])
        for i, source in enumerate((wk_hbm, wv_hbm))
    ]
    query_copy = pltpu.make_async_copy(q_hbm, q_ref, rest_sems.at[2])

    def keys(t, here):
        kt[t * TILE : (t + 1) * TILE, here] = feature_map(matmul(x_ref[here, :], tiles[t])).astype(BF16).T

    def values(t):
        v_ref[:, t * TILE : (t + 1) * TILE] = matmul(x_ref[...], tiles[full + t]).astype(BF16)

    def states(t):
        at = slice(t * TILE, min((t + 1) * TILE, inner))
        state[:, at] = packed_state(kt, 0, v_ref[:, at], t * TILE)

    for copy in (copies[0], copies[1], *rows):
        copy.start()
    for copy in (copies[0], copies[1], rows[0]):
        copy.wait()
    for copy in copies[2:]:
        copy.start()
    keys(0, low)
    keys(1, low)
    rows[1].wait()
    query_copy.start()
    keys(0, high)
    keys(1, high)
    for copy in copies[2:]:
        copy.wait()
    both[...] = jnp.zeros_like(both)
    both[:, :rest] = ends[0]
    both[:, 128 : 128 + rest] = ends[1]
    for t in range(2, full):
        keys(t, whole)
    out = matmul(x_ref[...], both[...])
    kt[full * TILE :, :] = feature_map(out[:, :128]).astype(BF16).T[:rest, :]
    v_ref[:, full * TILE :] = out[:, 128 : 128 + rest].astype(BF16)
    for t in range(full):
        values(t)
    for t in range(full + 1):
        states(t)
    core = core_ref[0]
    split_state(core, state, mine_ref, send_ref)
    edge_ref[...] = v_ref[pl.ds(pl.multiple_of((1 - core) * (count - width), 16), width), :]
    query_copy.wait()


HBM = pl.BlockSpec(memory_space=pltpu.HBM)


def project(core, flat, key_weight, value_weight, queries, width):
    count, model = flat.shape
    inner = key_weight.shape[1]
    half = HEAD // 2
    full = inner // TILE
    return pl.pallas_call(
        project_kernel,
        in_specs=[SMEM] + [HBM] * 4,
        out_specs=[VMEM] * 5,
        scratch_shapes=[
            pltpu.VMEM((count, model), BF16),
            pltpu.VMEM((2 * full, model, TILE), BF16),
            pltpu.VMEM((2, model, inner - full * TILE), BF16),
            pltpu.VMEM((model, TILE), BF16),
            pltpu.VMEM((inner, count), BF16),
            pltpu.VMEM((HEAD, inner), F32),
            pltpu.SemaphoreType.DMA((2,)),
            pltpu.SemaphoreType.DMA((2 * full,)),
            pltpu.SemaphoreType.DMA((3,)),
        ],
        out_shape=[
            shape((count, inner)),
            shape((half, inner), F32),
            shape((half, inner)),
            shape((width, inner)),
            shape((count, inner)),
        ],
        compiler_params=params(30),
        cost_estimate=cost(4 * count * model * inner, 2 * model * (count + 2 * inner)),
        name="project",
    )(core, *(pltpu.with_memory_space_constraint(a, pltpu.HBM) for a in (flat, key_weight, value_weight, queries)))


def pair_span(pair):
    start = 2 * HEAD * pair
    base = start // 128 * 128
    return base, start - base, 256 if start - base + 2 * HEAD <= 256 else 384


def paired(block, base, pair, limit):
    low, offset, wide = pair_span(pair)
    piece = block[:, low - base : min(low + wide, limit) - base]
    if piece.shape[1] < wide:
        piece = jnp.concatenate([piece, jnp.zeros((piece.shape[0], wide - piece.shape[1]), piece.dtype)], axis=1)
    if offset:
        piece = pltpu.roll(piece, wide - offset, 1)
    return piece[:, :256]


def phi_kernel(order_ref, q_ref, qf_ref):
    inner = q_ref.shape[1]
    step = 160

    def rows(i, carry):
        here = pl.ds(pl.multiple_of(i * step, 16), step)
        for pair in range(inner // (2 * HEAD)):
            low, _, wide = pair_span(pair)
            q = q_ref[here, low : min(low + wide, inner)].astype(F32)
            q = feature_map(paired(q, low, pair, inner))
            qf_ref[here, pair * 256 : (pair + 1) * 256] = q.astype(BF16)
        return carry

    lax.fori_loop(0, q_ref.shape[0] // step, rows, 0)


def phi_queries(order, queries):
    count, inner = queries.shape
    pairs = inner // (2 * HEAD)
    return pl.pallas_call(
        phi_kernel,
        in_specs=[SMEM, VMEM],
        out_specs=VMEM,
        out_shape=shape((count, pairs * 256)),
        compiler_params=params(4),
        cost_estimate=cost(8 * count * inner, 4 * count * inner, count * inner),
        name="phi_queries",
    )(order, queries)


def row_branch(taps, w_ref, low, high):
    side = []
    for c in range(3):
        acc = taps[0] * w_ref[c : c + 1, low:high]
        acc = acc + taps[1] * w_ref[3 + c : 4 + c, low:high]
        side.append(acc + taps[2] * w_ref[6 + c : 7 + c, low:high])
    width = side[0].shape[0]
    place = lax.broadcasted_iota(jnp.int32, side[0].shape, 0)
    left = jnp.where(place > 0, pltpu.roll(side[0], 1, 0), 0.0)
    right = jnp.where(place < width - 1, pltpu.roll(side[2], width - 1, 0), 0.0)
    return side[1] + left + right


def lane_tiles(inner):
    return [(low, min(low + 128, inner)) for low in range(0, inner, 128)]


def inner_rows(v_ref, w_ref, out_ref, width, first, number, at):

    def row(r, carry):
        here = pl.ds(pl.multiple_of((at + r) * width, 16), width)
        for low, high in lane_tiles(out_ref.shape[1]):
            taps = [
                v_ref[pl.ds(pl.multiple_of((first + r + d - 1) * width, 16), width), low:high].astype(F32)
                for d in range(3)
            ]
            out_ref[here, low:high] = row_branch(taps, w_ref, low, high)
        return carry

    lax.fori_loop(0, number, row, 0)


def middle_kernel(order_ref, v_ref, w_ref, out_ref, *, width):
    rows = v_ref.shape[0] // width
    inner_rows(v_ref, w_ref, out_ref, width, rows // 4, rows // 2, 0)


def border_kernel(core_ref, v_ref, halo_ref, w_ref, out_ref, *, width):
    rows = v_ref.shape[0] // width
    quarter = rows // 4
    inner_rows(v_ref, w_ref, out_ref, width, 1, quarter - 1, 1)
    inner_rows(v_ref, w_ref, out_ref, width, rows - quarter, quarter - 1, quarter)
    core = core_ref[0]
    top = (core == 1).astype(F32)
    bottom = (core == 0).astype(F32)
    last = (rows - 1) * width
    for low, high in lane_tiles(out_ref.shape[1]):
        halo = halo_ref[:, low:high].astype(F32)
        taps = [halo * top] + [v_ref[d * width : (d + 1) * width, low:high].astype(F32) for d in range(2)]
        out_ref[:width, low:high] = row_branch(taps, w_ref, low, high)
        taps = [v_ref[last + d * width : last + (d + 1) * width, low:high].astype(F32) for d in (-1, 0)] + [halo * bottom]
        end = (2 * quarter - 1) * width
        out_ref[end : end + width, low:high] = row_branch(taps, w_ref, low, high)


def local_rows(order, values, halo, conv_weight, width):
    count, inner = values.shape
    kernel = middle_kernel if halo is None else border_kernel
    operands = [values] + ([] if halo is None else [halo]) + [conv_weight]
    return pl.pallas_call(
        functools.partial(kernel, width=width),
        in_specs=[SMEM] + [VMEM] * len(operands),
        out_specs=VMEM,
        out_shape=shape((count // 2, inner), F32),
        compiler_params=params(4),
        cost_estimate=cost(10 * count * inner, 4 * count * inner),
        name="middle_rows" if halo is None else "border_rows",
    )(order, *operands)


def halves(core, own, other):
    own, other = own.astype(F32), other.astype(F32)
    return jnp.concatenate([jnp.where(core == 0, own, other), jnp.where(core == 0, other, own)], axis=0)


def pair_matrix(state, base, pair, limit):
    block = paired(state, base, pair, limit)
    column = lax.broadcasted_iota(jnp.int32, block.shape, 1)
    top = jnp.where(column < HEAD, block, 0.0)
    bottom = jnp.where((column >= HEAD) & (column < 2 * HEAD), block, 0.0)
    rest = jnp.zeros((256 - 2 * HEAD, 256), F32)
    return jnp.concatenate([top, bottom, rest], axis=0).astype(BF16)


def head_sums():
    row = lax.broadcasted_iota(jnp.int32, (256, 256), 0)
    column = lax.broadcasted_iota(jnp.int32, (256, 256), 1)
    first = (row < HEAD) & (column < HEAD)
    second = (row >= HEAD) & (row < 2 * HEAD) & (column >= HEAD) & (column < 2 * HEAD)
    return jnp.where(first | second, 1.0, 0.0).astype(BF16)


def normed_pair(qf, matrix, sums):
    attn = matmul(qf, matrix)
    total = matmul((attn * attn).astype(BF16), sums)
    return attn * lax.rsqrt(total * (1.0 / HEAD) + 1e-06)


def placed(normed, pairs, low, high):
    tiles = {}
    for pair, block in zip(pairs, normed):
        base, offset, wide = pair_span(pair)
        if wide > 256:
            block = jnp.concatenate([block, jnp.zeros((block.shape[0], wide - 256), F32)], axis=1)
        if offset:
            block = pltpu.roll(block, offset, 1)
        for t in range(wide // 128):
            at = base + t * 128
            piece = block[:, t * 128 : (t + 1) * 128]
            tiles[at] = tiles[at] + piece if at in tiles else piece
    for at in range(low, high, 128):
        yield at, min(at + 128, high), tiles[at][:, : min(128, high - at)]


CHUNK = 640


def early_kernel(core_ref, own_ref, other_ref, qf_ref, out_ref):
    state = halves(core_ref[0], own_ref[...], other_ref[...])
    sums = head_sums()
    pairs = range(FIRST // (2 * HEAD))
    matrices = [pair_matrix(state, 0, pair, FIRST) for pair in pairs]
    for at in range(0, qf_ref.shape[0], CHUNK):
        rows = slice(at, at + CHUNK)
        normed = [normed_pair(qf_ref[rows, pair * 256 : (pair + 1) * 256], matrices[pair], sums) for pair in pairs]
        for low, high, tile in placed(normed, pairs, 0, FIRST):
            out_ref[rows, low:high] = tile


def early_heads(core, own, other, qfeat):
    count = qfeat.shape[0]
    return pl.pallas_call(
        early_kernel,
        in_specs=[SMEM] + [VMEM] * 3,
        out_specs=VMEM,
        out_shape=shape((count, FIRST), F32),
        compiler_params=params(8),
        cost_estimate=cost(4 * count * FIRST * 512, 4 * count * FIRST),
        name="early_heads",
    )(core, own, other, qfeat)


def late_kernel(
    core_ref, owna_ref, othera_ref, ownb_ref, otherb_ref, qf_ref, mid_ref, edge_ref, early_ref, gain_ref, out_hbm,
    out, sems
):
    core = core_ref[0]
    count, inner = out_hbm.shape
    quarter = count // 4
    first = FIRST // (2 * HEAD)
    low = 2 * HEAD * first // 128 * 128
    state = jnp.concatenate(
        [halves(core, owna_ref[:, low:], othera_ref[:, low:]), halves(core, ownb_ref[...], otherb_ref[...])], axis=1
    )
    sums = head_sums()
    pairs = range(first, inner // (2 * HEAD))
    matrices = [pair_matrix(state, low, pair, inner) for pair in pairs]
    local = [edge_ref.at[:quarter], mid_ref.at[:quarter], mid_ref.at[quarter:], edge_ref.at[quarter:]]
    copies = []
    for at in range(0, count, CHUNK):
        rows = slice(at, at + CHUNK)
        normed = [
            normed_pair(qf_ref[rows, pair * 256 : (pair + 1) * 256], matrices[pair - first], sums) for pair in pairs
        ]
        later = {a: (b, tile) for a, b, tile in placed(normed, pairs, low, inner)}
        for part in range(at // quarter, (at + CHUNK) // quarter):
            here = slice(part * quarter, (part + 1) * quarter)
            inside = slice(part * quarter - at, (part + 1) * quarter - at)
            for a in range(0, inner, 128):
                b, tile = later.get(a, (a + 128, None))
                value = 0.0 if tile is None else tile[inside]
                if a < FIRST:
                    value = value + early_ref[here, a:b]
                out[here, a:b] = (value * gain_ref[:, a:b] + local[part][:, a:b]).astype(BF16)
            copies.append(pltpu.make_async_copy(out.at[here], out_hbm.at[here], sems.at[part]))
            copies[-1].start()
    for copy in copies:
        copy.wait()


def late_heads(core, first, second, qfeat, mid, edge, early, gain):
    count, inner = qfeat.shape[0], gain.shape[1]
    return pl.pallas_call(
        late_kernel,
        in_specs=[SMEM] + [VMEM] * 9,
        out_specs=HBM,
        scratch_shapes=[pltpu.VMEM((count, inner), BF16), pltpu.SemaphoreType.DMA((4,))],
        out_shape=shape((count, inner)),
        compiler_params=params(14),
        cost_estimate=cost(4 * count * inner * 512, 8 * count * inner),
        name="late_heads",
    )(core, *first, *second, qfeat, mid, edge, early, gain)


def swapped(block, axis, bit):
    return lax.ppermute(block, axis, [(i, i ^ bit) for i in range(lax.axis_size(axis))])


def shards(frames_in, queries, key_weight, value_weight, conv_weight, norm_gain):
    _, rows, width, model = frames_in.shape
    inner = key_weight.shape[1]
    count = rows * width
    core = lax.axis_index("space").astype(jnp.int32).reshape(1)
    flat = frames_in.reshape(count, model)
    gain = norm_gain.reshape(1, inner)
    frame = lax.axis_index("tm")
    masks = [(frame >> b & 1).astype(F32) for b in range((lax.axis_size("tm") - 1).bit_length())]
    core, masks = lax.optimization_barrier((core, masks))

    def slot(filler, sends):
        arrays, order = lax.optimization_barrier((tuple(a for a, _, _ in sends), core))
        received = tuple(swapped(a, axis, bit) for a, (_, axis, bit) in zip(arrays, sends))
        out = None if filler is None else filler(order)
        return lax.optimization_barrier((received, out))

    values, mine, send, edge, q = project(
        core, flat, key_weight, value_weight, queries.reshape(count, inner), width
    )
    (other, halo), _ = slot(None, [(send, "space", 1), (edge, "space", 1)])
    total = prefix = mine + other.astype(F32)
    local, qfeat = [], None
    for b, mask in enumerate(masks):
        left = len(masks) - 1 - b
        filler = None
        if left == 0:
            filler = lambda order: phi_queries(order, q)
        elif left == 1:
            filler = lambda order: local_rows(order, values, halo, conv_weight, width)
        elif left == 2:
            filler = lambda order: local_rows(order, values, None, conv_weight, width)
        (other,), out = slot(filler, [(total.astype(BF16), "tm", 1 << b)])
        if left == 0:
            qfeat = out
        elif filler is not None:
            local.append(out)
        other = other.astype(F32)
        prefix = prefix + mask * other
        total = total + other
    prefix = prefix.astype(BF16)
    parts = prefix[:, :FIRST], prefix[:, FIRST:]
    parts = lax.optimization_barrier(parts)
    others = [swapped(part, "space", 1) for part in parts]
    early = early_heads(core, parts[0], others[0], qfeat)
    others[1], early = lax.optimization_barrier((others[1], early))
    mixed = late_heads(core, (parts[0], others[0]), (parts[1], others[1]), qfeat, *local, early, gain)
    return mixed.reshape(1, rows, width, inner)


def solution(mesh):
    in_specs = (
        P(("groups", "tm"), "space", None, None),
        P(("groups", "tm"), "space", None, None),
        P(),
        P(),
        P(),
        P(),
    )
    out_specs = P(("groups", "tm"), "space", None, None)
    return jax.shard_map(shards, mesh=mesh, in_specs=in_specs, out_specs=out_specs, check_vma=False)
```

time: 49.5 us -> 47.3 us (0.956)
  starting transfers between devices: 12.8 us -> 8.57 us
  waiting for transfers between devices: 4.02 us -> 7.33 us
  Pallas kernels: 31.9 us -> 30.7 us
    ppermute x11 -> x7, starting transfers between devices: 12.8 us -> 8.57 us  [swapped(): lax.ppermute(block, axis, [(i, i ^ bit) for i in range(lax.axis_size(axis...]
    ppermute x11 -> x7, waiting for transfers between devices: 4.02 us -> 7.33 us  [swapped(): lax.ppermute(block, axis, [(i, i ^ bit) for i in range(lax.axis_size(axis...]
    pallas_call x4 -> x1, Pallas kernels: 20.4 us -> 19.3 us  [project(): pl.pallas_call(project_kernel, in_specs=[SMEM] + [HBM] * 4, out_specs=[VM...]
  transfers between devices with their start and end apart: 11 -> 7, of which waited for: 5 -> 5; matrix products, arithmetic and copies ran while one was open for 0% -> 0% of each run, Pallas kernels for 34% -> 17%
where the time goes in v3:
time: 47.3 us; the launch traced here: 47.2 us
  Pallas kernels  30.7 us (65%)
  starting transfers between devices  8.57 us (18%)
  waiting for transfers between devices  7.33 us (15%)
    pallas_call x1, Pallas kernels, project(): pl.pallas_call(project_kernel, in_specs=[SMEM] + [HBM] * 4, out_specs=[VM...  19.3 us
    ppermute x7, starting transfers between devices, swapped(): lax.ppermute(block, axis, [(i, i ^ bit) for i in range(lax.axis_size(axis...  8.57 us
    ppermute x7, waiting for transfers between devices, swapped(): lax.ppermute(block, axis, [(i, i ^ bit) for i in range(lax.axis_size(axis...  7.33 us
    pallas_call x2, Pallas kernels, local_rows(): pl.pallas_call(functools.partial(kernel, width=width), in_specs=[SMEM] +...  4.77 us
    pallas_call x1, Pallas kernels, late_heads(): pl.pallas_call(late_kernel, in_specs=[SMEM] + [VMEM] * 9, out_specs=HBM,...  3.28 us
    pallas_call x1, Pallas kernels, phi_queries(): pl.pallas_call(phi_kernel, in_specs=[SMEM, VMEM], out_specs=VMEM, out_sha...  2.3 us
    pallas_call x1, Pallas kernels, early_heads(): pl.pallas_call(early_kernel, in_specs=[SMEM] + [VMEM] * 3, out_specs=VMEM...  1.04 us
  transfers between devices with their start and end apart: 7, of which 5 were waited for; matrix products, arithmetic and copies ran while one was open for 0% of the time, Pallas kernels for 17%

profile of v3, /device:TPU:0, one launch (start us, length us, event | category | flops | bytes accessed | tf_op | source)
XLA Modules:
  0.0 47.2 jit_solution(7003708311343090889)
XLA Ops:
  0.0 0.0 copy-start
  0.0 19.3 %project.1 = (bf16[1280,1120]{1,0:T(8,128)(2,1)S(1)}, f32[56,1120]{1,0:T(8,128)S(1)}, bf16[56,1120]{1,0:T(8,128)(2,1)S(1)}, bf16[80,1120]{1,0:T(8,128)(2,1)S(1)}, bf16[1280,1120]{1,0:T(8,128)(2,1)S(1)}) custom-call(s32[1]{0:T(128)} %bitcast.core_ref.order_ref, bf16[1280,2240]{1,0:T(8,128)(2,1)} %bitcast.4, bf16[2240,1120]{1,0:T(8,128)(2,1)} %wk_hbm.1, ...), custom_call_target="tpu_custom_call" | custom-call | flops 12845056000 | bytes 15769600 | tf_op jit(solution)/shard_map/project/pallas_call | solution.py:133
  19.4 0.5 %collective-permute-start.1 = (bf16[80,1120]{1,0:T(8,128)(2,1)S(1)}, bf16[80,1120]{1,0:T(8,128)(2,1)S(1)}, u32[]{:S(2)}, u32[]{:S(2)}) collective-permute-start(bf16[80,1120]{1,0:T(8,128)(2,1)S(1)} %get-tuple-element.39), channel_id=1, source_target_pairs={{0,1},{1,0},{2,3},{3,2},{4,5},{5,4},{6,7},{7,6},{8,9},{9,8},{10,11... | collective-permute-start | bytes 537608 | tf_op jit(solution)/shard_map/ppermute | solution.py:402
  19.9 0.1 collective-permute-start
  20.0 1.3 %collective-permute-done = bf16[56,1120]{1,0:T(8,128)(2,1)S(1)} collective-permute-done((bf16[56,1120]{1,0:T(8,128)(2,1)S(1)}, bf16[56,1120]{1,0:T(8,128)(2,1)S(1)}, u32[]{:S(2)}, u32[]{:S(2)}) %collective-permute-start) | collective-permute-done | bytes 125472 | tf_op jit(solution)/shard_map/ppermute | solution.py:402
  21.2 0.0 collective-permute-done.1.halo_ref
  21.3 2.8 %collective-permute-start.2 = (bf16[56,1120]{1,0:T(8,128)(2,1)S(1)}, bf16[56,1120]{1,0:T(8,128)(2,1)S(1)}, u32[]{:S(2)}, u32[]{:S(2)}) collective-permute-start(bf16[56,1120]{1,0:T(8,128)(2,1)S(1)} %fusion.6), channel_id=1, source_target_pairs={{0,2},{2,0},{4,6},{6,4},{8,10},{10,8},{12,14},{14,12},{1,3},{3,1},... | collective-permute-start | bytes 376328 | tf_op jit(solution)/shard_map/ppermute | solution.py:402
  24.1 0.0 copy-done
  24.1 2.4 %middle_rows.1.mid_ref = f32[640,1120]{1,0:T(8,128)S(1)} custom-call(s32[1]{0:T(128)} %bitcast.core_ref.order_ref, bf16[1280,1120]{1,0:T(8,128)(2,1)S(1)} %get-tuple-element.44.v_ref, f32[9,1120]{1,0:T(8,128)S(1)} %copy-done), custom_call_target="tpu_custom_call" | custom-call | flops 14336000 | bytes 5734400 | tf_op jit(solution)/shard_map/middle_rows/pallas_call | solution.py:266
  26.5 1.5 %collective-permute-done.2 = bf16[56,1120]{1,0:T(8,128)(2,1)S(1)} collective-permute-done((bf16[56,1120]{1,0:T(8,128)(2,1)S(1)}, bf16[56,1120]{1,0:T(8,128)(2,1)S(1)}, u32[]{:S(2)}, u32[]{:S(2)}) %collective-permute-start.2) | collective-permute-done | bytes 125472 | tf_op jit(solution)/shard_map/ppermute | solution.py:402
  28.0 1.9 %collective-permute-start.3 = (bf16[56,1120]{1,0:T(8,128)(2,1)S(1)}, bf16[56,1120]{1,0:T(8,128)(2,1)S(1)}, u32[]{:S(2)}, u32[]{:S(2)}) collective-permute-start(bf16[56,1120]{1,0:T(8,128)(2,1)S(1)} %fusion.5), channel_id=1, source_target_pairs={{0,4},{2,6},{4,0},{6,2},{8,12},{10,14},{12,8},{14,10},{1,5},{3,7},... | collective-permute-start | bytes 376328 | tf_op jit(solution)/shard_map/ppermute | solution.py:402
  29.9 2.4 %border_rows.1.edge_ref = f32[640,1120]{1,0:T(8,128)S(1)} custom-call(s32[1]{0:T(128)} %bitcast.core_ref.order_ref, bf16[1280,1120]{1,0:T(8,128)(2,1)S(1)} %get-tuple-element.44.v_ref, bf16[80,1120]{1,0:T(8,128)(2,1)S(1)} %collective-permute-done.1.halo_ref, f32[9,1120]{1,0:T(8,128)S(1)} %copy-done), custom_call_target="tpu_custom_call" | custom-call | flops 14336000 | bytes 5734400 | tf_op jit(solution)/shard_map/border_rows/pallas_call | solution.py:266
  32.3 0.9 %collective-permute-done.3 = bf16[56,1120]{1,0:T(8,128)(2,1)S(1)} collective-permute-done((bf16[56,1120]{1,0:T(8,128)(2,1)S(1)}, bf16[56,1120]{1,0:T(8,128)(2,1)S(1)}, u32[]{:S(2)}, u32[]{:S(2)}) %collective-permute-start.3) | collective-permute-done | bytes 125472 | tf_op jit(solution)/shard_map/ppermute | solution.py:402
  33.2 0.1 fusion.4
  33.3 2.7 %collective-permute-start.4 = (bf16[56,1120]{1,0:T(8,128)(2,1)S(1)}, bf16[56,1120]{1,0:T(8,128)(2,1)S(1)}, u32[]{:S(2)}, u32[]{:S(2)}) collective-permute-start(bf16[56,1120]{1,0:T(8,128)(2,1)S(1)} %fusion.4), channel_id=1, source_target_pairs={{0,8},{2,10},{4,12},{6,14},{8,0},{10,2},{12,4},{14,6},{1,9},{3,11}... | collective-permute-start | bytes 376328 | tf_op jit(solution)/shard_map/ppermute | solution.py:402
  36.0 0.0 copy-start.1
  36.0 2.3 %phi_queries.1.qf_ref = bf16[1280,1280]{1,0:T(8,128)(2,1)S(1)} custom-call(s32[1]{0:T(128)} %bitcast.core_ref.order_ref, bf16[1280,1120]{1,0:T(8,128)(2,1)S(1)} %get-tuple-element.54.q_ref), custom_call_target="tpu_custom_call" | custom-call | flops 11468800 | bytes 5734400 | tf_op jit(solution)/shard_map/phi_queries/pallas_call | solution.py:196
  38.3 2.9 %collective-permute-done.4 = bf16[56,1120]{1,0:T(8,128)(2,1)S(1)} collective-permute-done((bf16[56,1120]{1,0:T(8,128)(2,1)S(1)}, bf16[56,1120]{1,0:T(8,128)(2,1)S(1)}, u32[]{:S(2)}, u32[]{:S(2)}) %collective-permute-start.4) | collective-permute-done | bytes 125472 | tf_op jit(solution)/shard_map/ppermute | solution.py:402
  41.2 0.1 fusion.3
  41.4 0.1 collective-permute-start.5
  41.5 0.0 copy-done.1
  41.5 0.5 %collective-permute-start.6 = (bf16[56,608]{1,0:T(8,128)(2,1)S(1)}, bf16[56,608]{1,0:T(8,128)(2,1)S(1)}, u32[]{:S(2)}, u32[]{:S(2)}) collective-permute-start(bf16[56,608]{1,0:T(8,128)(2,1)S(1)} %slice.9.ownb_ref), channel_id=1, source_target_pairs={{0,1},{1,0},{2,3},{3,2},{4,5},{5,4},{6,7},{7,6},{8,9},{9,8},{10,11... | collective-permute-start | bytes 204296 | tf_op jit(solution)/shard_map/ppermute | solution.py:402
  42.0 0.7 %collective-permute-done.5.other_ref.othera_ref = bf16[56,512]{1,0:T(8,128)(2,1)S(1)} collective-permute-done((bf16[56,512]{1,0:T(8,128)(2,1)S(1)}, bf16[56,512]{1,0:T(8,128)(2,1)S(1)}, u32[]{:S(2)}, u32[]{:S(2)}) %collective-permute-start.5) | collective-permute-done | bytes 57376 | tf_op jit(solution)/shard_map/ppermute | solution.py:402
  42.7 1.0 %early_heads.1.early_ref = f32[1280,512]{1,0:T(8,128)S(1)} custom-call(s32[1]{0:T(128)} %bitcast.core_ref.order_ref, bf16[56,512]{1,0:T(8,128)(2,1)S(1)} %slice.8.own_ref.owna_ref, bf16[56,512]{1,0:T(8,128)(2,1)S(1)} %collective-permute-done.5.other_ref.othera_ref, bf16[1280,1280]{1,0:T(8,128)(2,1)S(1)} %phi_queries.1.qf_ref), custom_call_target="tpu_custom_call" | custom-call | flops 1342177280 | bytes 2621440 | tf_op jit(solution)/shard_map/early_heads/pallas_call | solution.py:338
  43.7 0.0 collective-permute-done.6.otherb_ref
  43.7 3.3 %late_heads.1 = bf16[1280,1120]{1,0:T(8,128)(2,1)} custom-call(s32[1]{0:T(128)} %bitcast.core_ref.order_ref, bf16[56,512]{1,0:T(8,128)(2,1)S(1)} %slice.8.own_ref.owna_ref, bf16[56,512]{1,0:T(8,128)(2,1)S(1)} %collective-permute-done.5.other_ref.othera_ref, bf16[56,608]{1,0:T(8,128)(2,1)S(1)} %slice.9.ownb_ref, ...), custom_call_target="tpu_custom_call" | custom-call | flops 2936012800 | bytes 11468800 | tf_op jit(solution)/shard_map/late_heads/pallas_call | solution.py:389
  (5 shorter events, 0.1 us)
Async XLA Ops:
  0.0 24.1 %copy-start = (f32[9,1120]{1,0:T(8,128)S(1)}, f32[9,1120]{1,0:T(8,128)}, u32[]{:S(2)}) copy-start(f32[9,1120]{1,0:T(8,128)} %w_ref.3) | copy-start | bytes 120964
  19.4 1.9 %collective-permute-start.1 = (bf16[80,1120]{1,0:T(8,128)(2,1)S(1)}, bf16[80,1120]{1,0:T(8,128)(2,1)S(1)}, u32[]{:S(2)}, u32[]{:S(2)}) collective-permute-start(bf16[80,1120]{1,0:T(8,128)(2,1)S(1)} %get-tuple-element.39), channel_id=1, source_target_pairs={{0,1},{1,0},{2,3},{3,2},{4,5},{5,4},{6,7},{7,6},{8,9},{9,8},{10,11... | collective-permute-start | bytes 537608 | tf_op jit(solution)/shard_map/ppermute | solution.py:402
  19.9 1.3 %collective-permute-start = (bf16[56,1120]{1,0:T(8,128)(2,1)S(1)}, bf16[56,1120]{1,0:T(8,128)(2,1)S(1)}, u32[]{:S(2)}, u32[]{:S(2)}) collective-permute-start(bf16[56,1120]{1,0:T(8,128)(2,1)S(1)} %get-tuple-element.38), channel_id=1, source_target_pairs={{0,1},{1,0},{2,3},{3,2},{4,5},{5,4},{6,7},{7,6},{8,9},{9,8},{10,11... | collective-permute-start | bytes 376328 | tf_op jit(solution)/shard_map/ppermute | solution.py:402
  21.3 6.7 %collective-permute-start.2 = (bf16[56,1120]{1,0:T(8,128)(2,1)S(1)}, bf16[56,1120]{1,0:T(8,128)(2,1)S(1)}, u32[]{:S(2)}, u32[]{:S(2)}) collective-permute-start(bf16[56,1120]{1,0:T(8,128)(2,1)S(1)} %fusion.6), channel_id=1, source_target_pairs={{0,2},{2,0},{4,6},{6,4},{8,10},{10,8},{12,14},{14,12},{1,3},{3,1},... | collective-permute-start | bytes 376328 | tf_op jit(solution)/shard_map/ppermute | solution.py:402
  28.0 5.2 %collective-permute-start.3 = (bf16[56,1120]{1,0:T(8,128)(2,1)S(1)}, bf16[56,1120]{1,0:T(8,128)(2,1)S(1)}, u32[]{:S(2)}, u32[]{:S(2)}) collective-permute-start(bf16[56,1120]{1,0:T(8,128)(2,1)S(1)} %fusion.5), channel_id=1, source_target_pairs={{0,4},{2,6},{4,0},{6,2},{8,12},{10,14},{12,8},{14,10},{1,5},{3,7},... | collective-permute-start | bytes 376328 | tf_op jit(solution)/shard_map/ppermute | solution.py:402
  33.3 8.0 %collective-permute-start.4 = (bf16[56,1120]{1,0:T(8,128)(2,1)S(1)}, bf16[56,1120]{1,0:T(8,128)(2,1)S(1)}, u32[]{:S(2)}, u32[]{:S(2)}) collective-permute-start(bf16[56,1120]{1,0:T(8,128)(2,1)S(1)} %fusion.4), channel_id=1, source_target_pairs={{0,8},{2,10},{4,12},{6,14},{8,0},{10,2},{12,4},{14,6},{1,9},{3,11}... | collective-permute-start | bytes 376328 | tf_op jit(solution)/shard_map/ppermute | solution.py:402
  36.0 5.5 %copy-start.1 = (f32[1120]{0:T(1024)S(1)}, f32[1120]{0:T(1024)}, u32[]{:S(2)}) copy-start(f32[1120]{0:T(1024)} %param.11) | copy-start | bytes 13444
  41.4 1.3 %collective-permute-start.5 = (bf16[56,512]{1,0:T(8,128)(2,1)S(1)}, bf16[56,512]{1,0:T(8,128)(2,1)S(1)}, u32[]{:S(2)}, u32[]{:S(2)}) collective-permute-start(bf16[56,512]{1,0:T(8,128)(2,1)S(1)} %slice.8.own_ref.owna_ref), channel_id=1, source_target_pairs={{0,1},{1,0},{2,3},{3,2},{4,5},{5,4},{6,7},{7,6},{8,9},{9,8},{10,11... | collective-permute-start | bytes 172040 | tf_op jit(solution)/shard_map/ppermute | solution.py:402
  41.5 2.3 %collective-permute-start.6 = (bf16[56,608]{1,0:T(8,128)(2,1)S(1)}, bf16[56,608]{1,0:T(8,128)(2,1)S(1)}, u32[]{:S(2)}, u32[]{:S(2)}) collective-permute-start(bf16[56,608]{1,0:T(8,128)(2,1)S(1)} %slice.9.ownb_ref), channel_id=1, source_target_pairs={{0,1},{1,0},{2,3},{3,2},{4,5},{5,4},{6,7},{7,6},{8,9},{9,8},{10,11... | collective-permute-start | bytes 204296 | tf_op jit(solution)/shard_map/ppermute | solution.py:402

commit v4 on v3

--- a/solution.py
+++ b/solution.py
@@ -413,17 +413,15 @@
     masks = [(frame >> b & 1).astype(F32) for b in range((lax.axis_size("tm") - 1).bit_length())]
     core, masks = lax.optimization_barrier((core, masks))
 
-    def slot(filler, sends):
-        arrays, order = lax.optimization_barrier((tuple(a for a, _, _ in sends), core))
-        received = tuple(swapped(a, axis, bit) for a, (_, axis, bit) in zip(arrays, sends))
-        out = None if filler is None else filler(order)
-        return lax.optimization_barrier((received, out))
-
     values, mine, send, edge, q = project(
         core, flat, key_weight, value_weight, queries.reshape(count, inner), width
     )
-    (other, halo), _ = slot(None, [(send, "space", 1), (edge, "space", 1)])
-    total = prefix = mine + other.astype(F32)
+    cuts = [slice(0, FIRST), slice(FIRST, inner)]
+    sends = [send[:, cut] for cut in cuts]
+    received = [swapped(part, "space", 1) for part in sends]
+    halo = swapped(edge, "space", 1)
+    totals = [mine[:, cut] + other.astype(F32) for cut, other in zip(cuts, received)]
+    prefixes = list(totals)
     local, qfeat = [], None
     for b, mask in enumerate(masks):
         left = len(masks) - 1 - b
@@ -434,17 +432,21 @@
             filler = lambda order: local_rows(order, values, halo, conv_weight, width)
         elif left == 2:
             filler = lambda order: local_rows(order, values, None, conv_weight, width)
-        (other,), out = slot(filler, [(total.astype(BF16), "tm", 1 << b)])
-        if left == 0:
-            qfeat = out
-        elif filler is not None:
-            local.append(out)
-        other = other.astype(F32)
-        prefix = prefix + mask * other
-        total = total + other
-    prefix = prefix.astype(BF16)
-    parts = prefix[:, :FIRST], prefix[:, FIRST:]
-    parts = lax.optimization_barrier(parts)
+        outs = [total.astype(BF16) for total in totals]
+        outs[1], order = lax.optimization_barrier((outs[1], core))
+        received = [swapped(out, "tm", 1 << b) for out in outs]
+        if filler is not None:
+            out = filler(order)
+            received[0], out = lax.optimization_barrier((received[0], out))
+            if left == 0:
+                qfeat = out
+            else:
+                local.append(out)
+        for i, other in enumerate(received):
+            other = other.astype(F32)
+            prefixes[i] = prefixes[i] + mask * other
+            totals[i] = totals[i] + other
+    parts = [prefix.astype(BF16) for prefix in prefixes]
     others = [swapped(part, "space", 1) for part in parts]
     early = early_heads(core, parts[0], others[0], qfeat)
     others[1], early = lax.optimization_barrier((others[1], early))

time: 47.3 us -> 46.1 us (0.975)
  waiting for transfers between devices: 7.33 us -> 3.67 us
  starting transfers between devices: 8.57 us -> 10.9 us
    ppermute x7 -> x11, waiting for transfers between devices: 7.33 us -> 3.67 us  [swapped(): lax.ppermute(block, axis, [(i, i ^ bit) for i in range(lax.axis_size(axis...]
    ppermute x7 -> x11, starting transfers between devices: 8.57 us -> 10.9 us  [swapped(): lax.ppermute(block, axis, [(i, i ^ bit) for i in range(lax.axis_size(axis...]
  transfers between devices with their start and end apart: 7 -> 11, of which waited for: 5 -> 4; matrix products, arithmetic and copies ran while one was open for 0% -> 1% of each run, Pallas kernels for 17% -> 18%
where the time goes in v4:
time: 46.1 us; the launch traced here: 45.9 us
  Pallas kernels  30.7 us (67%)
  starting transfers between devices  10.9 us (24%)
  waiting for transfers between devices  3.67 us (8%)
    pallas_call x1, Pallas kernels, project(): pl.pallas_call(project_kernel, in_specs=[SMEM] + [HBM] * 4, out_specs=[VM...  19.3 us
    ppermute x11, starting transfers between devices, swapped(): lax.ppermute(block, axis, [(i, i ^ bit) for i in range(lax.axis_size(axis...  10.9 us
    pallas_call x2, Pallas kernels, local_rows(): pl.pallas_call(functools.partial(kernel, width=width), in_specs=[SMEM] +...  4.77 us
    ppermute x11, waiting for transfers between devices, swapped(): lax.ppermute(block, axis, [(i, i ^ bit) for i in range(lax.axis_size(axis...  3.67 us
    pallas_call x1, Pallas kernels, late_heads(): pl.pallas_call(late_kernel, in_specs=[SMEM] + [VMEM] * 9, out_specs=HBM,...  3.27 us
    pallas_call x1, Pallas kernels, phi_queries(): pl.pallas_call(phi_kernel, in_specs=[SMEM, VMEM], out_specs=VMEM, out_sha...  2.3 us
    pallas_call x1, Pallas kernels, early_heads(): pl.pallas_call(early_kernel, in_specs=[SMEM] + [VMEM] * 3, out_specs=VMEM...  1.05 us
  transfers between devices with their start and end apart: 11, of which 4 were waited for; matrix products, arithmetic and copies ran while one was open for 1% of the time, Pallas kernels for 18%

profile of v4, /device:TPU:0, one launch (start us, length us, event | category | flops | bytes accessed | tf_op | source)
XLA Modules:
  0.0 45.9 jit_solution(11297169579691839277)
XLA Ops:
  0.0 0.0 copy-start.1
  0.0 0.0 copy-start
  0.0 19.3 %project.1 = (bf16[1280,1120]{1,0:T(8,128)(2,1)S(1)}, f32[56,1120]{1,0:T(8,128)S(1)}, bf16[56,1120]{1,0:T(8,128)(2,1)S(1)}, bf16[80,1120]{1,0:T(8,128)(2,1)S(1)}, bf16[1280,1120]{1,0:T(8,128)(2,1)S(1)}) custom-call(s32[1]{0:T(128)} %bitcast.core_ref.order_ref, bf16[1280,2240]{1,0:T(8,128)(2,1)} %bitcast.4, bf16[2240,1120]{1,0:T(8,128)(2,1)} %wk_hbm.1, ...), custom_call_target="tpu_custom_call" | custom-call | flops 12845056000 | bytes 15769600 | tf_op jit(solution)/shard_map/project/pallas_call | solution.py:133
  19.4 0.5 %collective-permute-start = (bf16[56,512]{1,0:T(8,128)(2,1)S(1)}, bf16[56,512]{1,0:T(8,128)(2,1)S(1)}, u32[]{:S(2)}, u32[]{:S(2)}) collective-permute-start(bf16[56,512]{1,0:T(8,128)(2,1)S(1)} %slice.13), channel_id=1, source_target_pairs={{0,1},{1,0},{2,3},{3,2},{4,5},{5,4},{6,7},{7,6},{8,9},{9,8},{10,11... | collective-permute-start | bytes 172040 | tf_op jit(solution)/shard_map/ppermute | solution.py:402
  19.9 0.1 collective-permute-start.2
  20.0 0.4 collective-permute-start.5
  20.4 0.0 copy-done.1
  20.4 0.4 collective-permute-done
  20.8 2.9 %collective-permute-start.1 = (bf16[56,512]{1,0:T(8,128)(2,1)S(1)}, bf16[56,512]{1,0:T(8,128)(2,1)S(1)}, u32[]{:S(2)}, u32[]{:S(2)}) collective-permute-start(bf16[56,512]{1,0:T(8,128)(2,1)S(1)} %fusion.12), channel_id=1, source_target_pairs={{0,2},{2,0},{4,6},{6,4},{8,10},{10,8},{12,14},{14,12},{1,3},{3,1},... | collective-permute-start | bytes 172040 | tf_op jit(solution)/shard_map/ppermute | solution.py:402
  23.7 0.0 collective-permute-done.2
  23.8 0.2 collective-permute-start.4
  23.9 0.0 copy-done
  23.9 2.4 %middle_rows.1.mid_ref = f32[640,1120]{1,0:T(8,128)S(1)} custom-call(s32[1]{0:T(128)} %bitcast.core_ref.order_ref, bf16[1280,1120]{1,0:T(8,128)(2,1)S(1)} %get-tuple-element.33.v_ref, f32[9,1120]{1,0:T(8,128)S(1)} %copy-done), custom_call_target="tpu_custom_call" | custom-call | flops 14336000 | bytes 5734400 | tf_op jit(solution)/shard_map/middle_rows/pallas_call | solution.py:266
  26.3 0.0 collective-permute-done.1
  26.4 2.0 %collective-permute-start.3 = (bf16[56,512]{1,0:T(8,128)(2,1)S(1)}, bf16[56,512]{1,0:T(8,128)(2,1)S(1)}, u32[]{:S(2)}, u32[]{:S(2)}) collective-permute-start(bf16[56,512]{1,0:T(8,128)(2,1)S(1)} %fusion.11), channel_id=1, source_target_pairs={{0,4},{2,6},{4,0},{6,2},{8,12},{10,14},{12,8},{14,10},{1,5},{3,7},... | collective-permute-start | bytes 172040 | tf_op jit(solution)/shard_map/ppermute | solution.py:402
  28.4 0.0 collective-permute-done.4
  28.4 1.4 %collective-permute-start.7 = (bf16[56,608]{1,0:T(8,128)(2,1)S(1)}, bf16[56,608]{1,0:T(8,128)(2,1)S(1)}, u32[]{:S(2)}, u32[]{:S(2)}) collective-permute-start(bf16[56,608]{1,0:T(8,128)(2,1)S(1)} %fusion.10), channel_id=1, source_target_pairs={{0,4},{2,6},{4,0},{6,2},{8,12},{10,14},{12,8},{14,10},{1,5},{3,7},... | collective-permute-start | bytes 204296 | tf_op jit(solution)/shard_map/ppermute | solution.py:402
  29.8 0.0 collective-permute-done.5.halo_ref
  29.8 2.4 %border_rows.1.edge_ref = f32[640,1120]{1,0:T(8,128)S(1)} custom-call(s32[1]{0:T(128)} %bitcast.core_ref.order_ref, bf16[1280,1120]{1,0:T(8,128)(2,1)S(1)} %get-tuple-element.33.v_ref, bf16[80,1120]{1,0:T(8,128)(2,1)S(1)} %collective-permute-done.5.halo_ref, f32[9,1120]{1,0:T(8,128)S(1)} %copy-done), custom_call_target="tpu_custom_call" | custom-call | flops 14336000 | bytes 5734400 | tf_op jit(solution)/shard_map/border_rows/pallas_call | solution.py:266
  32.2 0.0 collective-permute-done.3
  32.3 2.7 %collective-permute-start.6 = (bf16[56,512]{1,0:T(8,128)(2,1)S(1)}, bf16[56,512]{1,0:T(8,128)(2,1)S(1)}, u32[]{:S(2)}, u32[]{:S(2)}) collective-permute-start(bf16[56,512]{1,0:T(8,128)(2,1)S(1)} %fusion.9), channel_id=1, source_target_pairs={{0,8},{2,10},{4,12},{6,14},{8,0},{10,2},{12,4},{14,6},{1,9},{3,11}... | collective-permute-start | bytes 172040 | tf_op jit(solution)/shard_map/ppermute | solution.py:402
  34.9 0.0 collective-permute-done.7
  35.0 0.6 %collective-permute-start.9 = (bf16[56,608]{1,0:T(8,128)(2,1)S(1)}, bf16[56,608]{1,0:T(8,128)(2,1)S(1)}, u32[]{:S(2)}, u32[]{:S(2)}) collective-permute-start(bf16[56,608]{1,0:T(8,128)(2,1)S(1)} %fusion.4), channel_id=1, source_target_pairs={{0,8},{2,10},{4,12},{6,14},{8,0},{10,2},{12,4},{14,6},{1,9},{3,11}... | collective-permute-start | bytes 204296 | tf_op jit(solution)/shard_map/ppermute | solution.py:402
  35.5 2.3 %phi_queries.1.qf_ref = bf16[1280,1280]{1,0:T(8,128)(2,1)S(1)} custom-call(s32[1]{0:T(128)} %bitcast.core_ref.order_ref, bf16[1280,1120]{1,0:T(8,128)(2,1)S(1)} %get-tuple-element.43.q_ref), custom_call_target="tpu_custom_call" | custom-call | flops 11468800 | bytes 5734400 | tf_op jit(solution)/shard_map/phi_queries/pallas_call | solution.py:196
  37.9 1.6 %collective-permute-done.6 = bf16[56,512]{1,0:T(8,128)(2,1)S(1)} collective-permute-done((bf16[56,512]{1,0:T(8,128)(2,1)S(1)}, bf16[56,512]{1,0:T(8,128)(2,1)S(1)}, u32[]{:S(2)}, u32[]{:S(2)}) %collective-permute-start.6) | collective-permute-done | bytes 57376 | tf_op jit(solution)/shard_map/ppermute | solution.py:402
  39.4 0.1 fusion.8.own_ref.owna_ref
  39.5 0.1 collective-permute-start.8
  39.5 1.6 %collective-permute-done.9 = bf16[56,608]{1,0:T(8,128)(2,1)S(1)} collective-permute-done((bf16[56,608]{1,0:T(8,128)(2,1)S(1)}, bf16[56,608]{1,0:T(8,128)(2,1)S(1)}, u32[]{:S(2)}, u32[]{:S(2)}) %collective-permute-start.9) | collective-permute-done | bytes 68128 | tf_op jit(solution)/shard_map/ppermute | solution.py:402
  41.1 0.1 fusion.3.ownb_ref
  41.2 0.1 collective-permute-start.10
  41.2 0.0 collective-permute-done.8.other_ref.othera_ref
  41.3 1.0 %early_heads.1.early_ref = f32[1280,512]{1,0:T(8,128)S(1)} custom-call(s32[1]{0:T(128)} %bitcast.core_ref.order_ref, bf16[56,512]{1,0:T(8,128)(2,1)S(1)} %fusion.8.own_ref.owna_ref, bf16[56,512]{1,0:T(8,128)(2,1)S(1)} %collective-permute-done.8.other_ref.othera_ref, bf16[1280,1280]{1,0:T(8,128)(2,1)S(1)} %phi_queries.1.qf_ref), custom_call_target="tpu_custom_call" | custom-call | flops 1342177280 | bytes 2621440 | tf_op jit(solution)/shard_map/early_heads/pallas_call | solution.py:338
  42.3 0.2 collective-permute-done.10.otherb_ref
  42.5 3.3 %late_heads.1 = bf16[1280,1120]{1,0:T(8,128)(2,1)} custom-call(s32[1]{0:T(128)} %bitcast.core_ref.order_ref, bf16[56,512]{1,0:T(8,128)(2,1)S(1)} %fusion.8.own_ref.owna_ref, bf16[56,512]{1,0:T(8,128)(2,1)S(1)} %collective-permute-done.8.other_ref.othera_ref, bf16[56,608]{1,0:T(8,128)(2,1)S(1)} %fusion.3.ownb_ref, ...), custom_call_target="tpu_custom_call" | custom-call | flops 2936012800 | bytes 11468800 | tf_op jit(solution)/shard_map/late_heads/pallas_call | solution.py:389
  (9 shorter events, 0.2 us)
Async XLA Ops:
  0.0 20.4 %copy-start.1 = (f32[1120]{0:T(1024)S(1)}, f32[1120]{0:T(1024)}, u32[]{:S(2)}) copy-start(f32[1120]{0:T(1024)} %param.11) | copy-start | bytes 13444
  0.0 23.9 %copy-start = (f32[9,1120]{1,0:T(8,128)S(1)}, f32[9,1120]{1,0:T(8,128)}, u32[]{:S(2)}) copy-start(f32[9,1120]{1,0:T(8,128)} %w_ref.3) | copy-start | bytes 120964
  19.4 1.4 %collective-permute-start = (bf16[56,512]{1,0:T(8,128)(2,1)S(1)}, bf16[56,512]{1,0:T(8,128)(2,1)S(1)}, u32[]{:S(2)}, u32[]{:S(2)}) collective-permute-start(bf16[56,512]{1,0:T(8,128)(2,1)S(1)} %slice.13), channel_id=1, source_target_pairs={{0,1},{1,0},{2,3},{3,2},{4,5},{5,4},{6,7},{7,6},{8,9},{9,8},{10,11... | collective-permute-start | bytes 172040 | tf_op jit(solution)/shard_map/ppermute | solution.py:402
  19.9 3.8 %collective-permute-start.2 = (bf16[56,608]{1,0:T(8,128)(2,1)S(1)}, bf16[56,608]{1,0:T(8,128)(2,1)S(1)}, u32[]{:S(2)}, u32[]{:S(2)}) collective-permute-start(bf16[56,608]{1,0:T(8,128)(2,1)S(1)} %slice.15), channel_id=1, source_target_pairs={{0,1},{1,0},{2,3},{3,2},{4,5},{5,4},{6,7},{7,6},{8,9},{9,8},{10,11... | collective-permute-start | bytes 204296 | tf_op jit(solution)/shard_map/ppermute | solution.py:402
  20.0 9.8 %collective-permute-start.5 = (bf16[80,1120]{1,0:T(8,128)(2,1)S(1)}, bf16[80,1120]{1,0:T(8,128)(2,1)S(1)}, u32[]{:S(2)}, u32[]{:S(2)}) collective-permute-start(bf16[80,1120]{1,0:T(8,128)(2,1)S(1)} %get-tuple-element.38), channel_id=1, source_target_pairs={{0,1},{1,0},{2,3},{3,2},{4,5},{5,4},{6,7},{7,6},{8,9},{9,8},{10,11... | collective-permute-start | bytes 537608 | tf_op jit(solution)/shard_map/ppermute | solution.py:402
  20.8 5.5 %collective-permute-start.1 = (bf16[56,512]{1,0:T(8,128)(2,1)S(1)}, bf16[56,512]{1,0:T(8,128)(2,1)S(1)}, u32[]{:S(2)}, u32[]{:S(2)}) collective-permute-start(bf16[56,512]{1,0:T(8,128)(2,1)S(1)} %fusion.12), channel_id=1, source_target_pairs={{0,2},{2,0},{4,6},{6,4},{8,10},{10,8},{12,14},{14,12},{1,3},{3,1},... | collective-permute-start | bytes 172040 | tf_op jit(solution)/shard_map/ppermute | solution.py:402
  23.8 4.7 %collective-permute-start.4 = (bf16[56,608]{1,0:T(8,128)(2,1)S(1)}, bf16[56,608]{1,0:T(8,128)(2,1)S(1)}, u32[]{:S(2)}, u32[]{:S(2)}) collective-permute-start(bf16[56,608]{1,0:T(8,128)(2,1)S(1)} %fusion.13), channel_id=1, source_target_pairs={{0,2},{2,0},{4,6},{6,4},{8,10},{10,8},{12,14},{14,12},{1,3},{3,1},... | collective-permute-start | bytes 204296 | tf_op jit(solution)/shard_map/ppermute | solution.py:402
  26.4 5.9 %collective-permute-start.3 = (bf16[56,512]{1,0:T(8,128)(2,1)S(1)}, bf16[56,512]{1,0:T(8,128)(2,1)S(1)}, u32[]{:S(2)}, u32[]{:S(2)}) collective-permute-start(bf16[56,512]{1,0:T(8,128)(2,1)S(1)} %fusion.11), channel_id=1, source_target_pairs={{0,4},{2,6},{4,0},{6,2},{8,12},{10,14},{12,8},{14,10},{1,5},{3,7},... | collective-permute-start | bytes 172040 | tf_op jit(solution)/shard_map/ppermute | solution.py:402
  28.4 6.5 %collective-permute-start.7 = (bf16[56,608]{1,0:T(8,128)(2,1)S(1)}, bf16[56,608]{1,0:T(8,128)(2,1)S(1)}, u32[]{:S(2)}, u32[]{:S(2)}) collective-permute-start(bf16[56,608]{1,0:T(8,128)(2,1)S(1)} %fusion.10), channel_id=1, source_target_pairs={{0,4},{2,6},{4,0},{6,2},{8,12},{10,14},{12,8},{14,10},{1,5},{3,7},... | collective-permute-start | bytes 204296 | tf_op jit(solution)/shard_map/ppermute | solution.py:402
  32.3 7.1 %collective-permute-start.6 = (bf16[56,512]{1,0:T(8,128)(2,1)S(1)}, bf16[56,512]{1,0:T(8,128)(2,1)S(1)}, u32[]{:S(2)}, u32[]{:S(2)}) collective-permute-start(bf16[56,512]{1,0:T(8,128)(2,1)S(1)} %fusion.9), channel_id=1, source_target_pairs={{0,8},{2,10},{4,12},{6,14},{8,0},{10,2},{12,4},{14,6},{1,9},{3,11}... | collective-permute-start | bytes 172040 | tf_op jit(solution)/shard_map/ppermute | solution.py:402
  35.0 6.1 %collective-permute-start.9 = (bf16[56,608]{1,0:T(8,128)(2,1)S(1)}, bf16[56,608]{1,0:T(8,128)(2,1)S(1)}, u32[]{:S(2)}, u32[]{:S(2)}) collective-permute-start(bf16[56,608]{1,0:T(8,128)(2,1)S(1)} %fusion.4), channel_id=1, source_target_pairs={{0,8},{2,10},{4,12},{6,14},{8,0},{10,2},{12,4},{14,6},{1,9},{3,11}... | collective-permute-start | bytes 204296 | tf_op jit(solution)/shard_map/ppermute | solution.py:402
  39.5 1.8 %collective-permute-start.8 = (bf16[56,512]{1,0:T(8,128)(2,1)S(1)}, bf16[56,512]{1,0:T(8,128)(2,1)S(1)}, u32[]{:S(2)}, u32[]{:S(2)}) collective-permute-start(bf16[56,512]{1,0:T(8,128)(2,1)S(1)} %fusion.8.own_ref.owna_ref), channel_id=1, source_target_pairs={{0,1},{1,0},{2,3},{3,2},{4,5},{5,4},{6,7},{7,6},{8,9},{9,8},{10,11... | collective-permute-start | bytes 172040 | tf_op jit(solution)/shard_map/ppermute | solution.py:402
  41.2 1.3 %collective-permute-start.10 = (bf16[56,608]{1,0:T(8,128)(2,1)S(1)}, bf16[56,608]{1,0:T(8,128)(2,1)S(1)}, u32[]{:S(2)}, u32[]{:S(2)}) collective-permute-start(bf16[56,608]{1,0:T(8,128)(2,1)S(1)} %fusion.3.ownb_ref), channel_id=1, source_target_pairs={{0,1},{1,0},{2,3},{3,2},{4,5},{5,4},{6,7},{7,6},{8,9},{9,8},{10,11... | collective-permute-start | bytes 204296 | tf_op jit(solution)/shard_map/ppermute | solution.py:402

commit v5 on v4

--- a/solution.py
+++ b/solution.py
@@ -236,42 +236,44 @@
     lax.fori_loop(0, number, row, 0)
 
 
-def middle_kernel(order_ref, v_ref, w_ref, out_ref, *, width):
+def middle_kernel(order_ref, v_ref, w_ref, out_ref, *, width, first):
+    inner_rows(v_ref, w_ref, out_ref, width, first, out_ref.shape[0] // width, 0)
+
+
+def border_kernel(core_ref, v_ref, halo_ref, w_ref, out_ref, *, width, top, bottom):
     rows = v_ref.shape[0] // width
-    inner_rows(v_ref, w_ref, out_ref, width, rows // 4, rows // 2, 0)
-
-
-def border_kernel(core_ref, v_ref, halo_ref, w_ref, out_ref, *, width):
-    rows = v_ref.shape[0] // width
-    quarter = rows // 4
-    inner_rows(v_ref, w_ref, out_ref, width, 1, quarter - 1, 1)
-    inner_rows(v_ref, w_ref, out_ref, width, rows - quarter, quarter - 1, quarter)
+    inner_rows(v_ref, w_ref, out_ref, width, 1, top - 1, 1)
+    inner_rows(v_ref, w_ref, out_ref, width, rows - bottom, bottom - 1, top)
     core = core_ref[0]
-    top = (core == 1).astype(F32)
-    bottom = (core == 0).astype(F32)
+    above = (core == 1).astype(F32)
+    below = (core == 0).astype(F32)
     last = (rows - 1) * width
     for low, high in lane_tiles(out_ref.shape[1]):
         halo = halo_ref[:, low:high].astype(F32)
-        taps = [halo * top] + [v_ref[d * width : (d + 1) * width, low:high].astype(F32) for d in range(2)]
+        taps = [halo * above] + [v_ref[d * width : (d + 1) * width, low:high].astype(F32) for d in range(2)]
         out_ref[:width, low:high] = row_branch(taps, w_ref, low, high)
-        taps = [v_ref[last + d * width : last + (d + 1) * width, low:high].astype(F32) for d in (-1, 0)] + [halo * bottom]
-        end = (2 * quarter - 1) * width
-        out_ref[end : end + width, low:high] = row_branch(taps, w_ref, low, high)
-
-
-def local_rows(order, values, halo, conv_weight, width):
-    count, inner = values.shape
-    kernel = middle_kernel if halo is None else border_kernel
-    operands = [values] + ([] if halo is None else [halo]) + [conv_weight]
+        taps = [v_ref[last + d * width : last + (d + 1) * width, low:high].astype(F32) for d in (-1, 0)]
+        end = (top + bottom - 1) * width
+        out_ref[end : end + width, low:high] = row_branch(taps + [halo * below], w_ref, low, high)
+
+
+def local_rows(kernel, number, name, order, *operands):
+    width, inner = kernel.keywords["width"], operands[0].shape[1]
     return pl.pallas_call(
-        functools.partial(kernel, width=width),
+        kernel,
         in_specs=[SMEM] + [VMEM] * len(operands),
         out_specs=VMEM,
-        out_shape=shape((count // 2, inner), F32),
+        out_shape=shape((number * width, inner), F32),
         compiler_params=params(4),
-        cost_estimate=cost(10 * count * inner, 4 * count * inner),
-        name="middle_rows" if halo is None else "border_rows",
+        cost_estimate=cost(20 * number * width * inner, 8 * number * width * inner),
+        name=name,
     )(order, *operands)
+
+
+def row_pieces(rows):
+    top, bottom = rows // 4, 2
+    upper = (rows - top - bottom) // 2
+    return top, bottom, upper, rows - top - bottom - upper
 
 
 def halves(core, own, other):
@@ -347,12 +349,11 @@
 
 
 def late_kernel(
-    core_ref, owna_ref, othera_ref, ownb_ref, otherb_ref, qf_ref, mid_ref, edge_ref, early_ref, gain_ref, out_hbm,
-    out, sems
+    core_ref, owna_ref, othera_ref, ownb_ref, otherb_ref, qf_ref, upper_ref, lower_ref, edge_ref, early_ref,
+    gain_ref, out_hbm, out, sems, *, width
 ):
     core = core_ref[0]
     count, inner = out_hbm.shape
-    quarter = count // 4
     first = FIRST // (2 * HEAD)
     low = 2 * HEAD * first // 128 * 128
     state = jnp.concatenate(
@@ -361,7 +362,13 @@
     sums = head_sums()
     pairs = range(first, inner // (2 * HEAD))
     matrices = [pair_matrix(state, low, pair, inner) for pair in pairs]
-    local = [edge_ref.at[:quarter], mid_ref.at[:quarter], mid_ref.at[quarter:], edge_ref.at[quarter:]]
+    top, bottom, upper, lower = (n * width for n in row_pieces(count // width))
+    pieces = [
+        (0, top, edge_ref, 0),
+        (top, upper, upper_ref, 0),
+        (top + upper, lower, lower_ref, 0),
+        (count - bottom, bottom, edge_ref, top),
+    ]
     copies = []
     for at in range(0, count, CHUNK):
         rows = slice(at, at + CHUNK)
@@ -369,33 +376,37 @@
             normed_pair(qf_ref[rows, pair * 256 : (pair + 1) * 256], matrices[pair - first], sums) for pair in pairs
         ]
         later = {a: (b, tile) for a, b, tile in placed(normed, pairs, low, inner)}
-        for part in range(at // quarter, (at + CHUNK) // quarter):
-            here = slice(part * quarter, (part + 1) * quarter)
-            inside = slice(part * quarter - at, (part + 1) * quarter - at)
+        for start, number, ref, base in pieces:
+            lo, hi = max(start, at), min(start + number, at + CHUNK)
+            if lo >= hi:
+                continue
+            here = slice(lo, hi)
+            inside = slice(lo - at, hi - at)
+            there = slice(lo - start + base, hi - start + base)
             for a in range(0, inner, 128):
                 b, tile = later.get(a, (a + 128, None))
                 value = 0.0 if tile is None else tile[inside]
                 if a < FIRST:
                     value = value + early_ref[here, a:b]
-                out[here, a:b] = (value * gain_ref[:, a:b] + local[part][:, a:b]).astype(BF16)
-            copies.append(pltpu.make_async_copy(out.at[here], out_hbm.at[here], sems.at[part]))
+                out[here, a:b] = (value * gain_ref[:, a:b] + ref[there, a:b]).astype(BF16)
+            copies.append(pltpu.make_async_copy(out.at[here], out_hbm.at[here], sems.at[len(copies)]))
             copies[-1].start()
     for copy in copies:
         copy.wait()
 
 
-def late_heads(core, first, second, qfeat, mid, edge, early, gain):
+def late_heads(core, first, second, qfeat, local, early, gain, width):
     count, inner = qfeat.shape[0], gain.shape[1]
     return pl.pallas_call(
-        late_kernel,
-        in_specs=[SMEM] + [VMEM] * 9,
+        functools.partial(late_kernel, width=width),
+        in_specs=[SMEM] + [VMEM] * 10,
         out_specs=HBM,
-        scratch_shapes=[pltpu.VMEM((count, inner), BF16), pltpu.SemaphoreType.DMA((4,))],
+        scratch_shapes=[pltpu.VMEM((count, inner), BF16), pltpu.SemaphoreType.DMA((8,))],
         out_shape=shape((count, inner)),
         compiler_params=params(14),
         cost_estimate=cost(4 * count * inner * 512, 8 * count * inner),
         name="late_heads",
-    )(core, *first, *second, qfeat, mid, edge, early, gain)
+    )(core, *first, *second, qfeat, *local, early, gain)
 
 
 def swapped(block, axis, bit):
@@ -422,16 +433,21 @@
     halo = swapped(edge, "space", 1)
     totals = [mine[:, cut] + other.astype(F32) for cut, other in zip(cuts, received)]
     prefixes = list(totals)
+    top, bottom, upper, lower = row_pieces(rows)
+    middle = lambda first: functools.partial(middle_kernel, width=width, first=first)
+    border = functools.partial(border_kernel, width=width, top=top, bottom=bottom)
+    kernels = {
+        2: lambda order: local_rows(middle(top), upper, "upper_rows", order, values, conv_weight),
+        1: lambda order: local_rows(middle(top + upper), lower, "lower_rows", order, values, conv_weight),
+        0: lambda order: (
+            phi_queries(order, q),
+            local_rows(border, top + bottom, "border_rows", order, values, halo, conv_weight),
+        ),
+    }
     local, qfeat = [], None
     for b, mask in enumerate(masks):
         left = len(masks) - 1 - b
-        filler = None
-        if left == 0:
-            filler = lambda order: phi_queries(order, q)
-        elif left == 1:
-            filler = lambda order: local_rows(order, values, halo, conv_weight, width)
-        elif left == 2:
-            filler = lambda order: local_rows(order, values, None, conv_weight, width)
+        filler = kernels.get(left)
         outs = [total.astype(BF16) for total in totals]
         outs[1], order = lax.optimization_barrier((outs[1], core))
         received = [swapped(out, "tm", 1 << b) for out in outs]
@@ -439,9 +455,8 @@
             out = filler(order)
             received[0], out = lax.optimization_barrier((received[0], out))
             if left == 0:
-                qfeat = out
-            else:
-                local.append(out)
+                qfeat, out = out
+            local.append(out)
         for i, other in enumerate(received):
             other = other.astype(F32)
             prefixes[i] = prefixes[i] + mask * other
@@ -450,7 +465,7 @@
     others = [swapped(part, "space", 1) for part in parts]
     early = early_heads(core, parts[0], others[0], qfeat)
     others[1], early = lax.optimization_barrier((others[1], early))
-    mixed = late_heads(core, (parts[0], others[0]), (parts[1], others[1]), qfeat, *local, early, gain)
+    mixed = late_heads(core, (parts[0], others[0]), (parts[1], others[1]), qfeat, local, early, gain, width)
     return mixed.reshape(1, rows, width, inner)
 
 

time: 46.1 us -> 45.6 us (0.989)
  waiting for transfers between devices: 3.67 us -> 1.57 us
  starting transfers between devices: 10.9 us -> 12.5 us
    ppermute x11, waiting for transfers between devices: 3.67 us -> 1.57 us  [swapped(): lax.ppermute(block, axis, [(i, i ^ bit) for i in range(lax.axis_size(axis...]
    ppermute x11, starting transfers between devices: 10.9 us -> 12.5 us  [swapped(): lax.ppermute(block, axis, [(i, i ^ bit) for i in range(lax.axis_size(axis...]
    pallas_call x3 -> x4, Pallas kernels: 8.04 us -> 8.15 us  [the longest x3 4.76 us: local_rows(): pl.pallas_call(kernel, in_specs=[SMEM] + [VMEM] * len(operands), out_spec...]
  transfers between devices with their start and end apart: 11 -> 11, of which waited for: 4 -> 3; matrix products, arithmetic and copies ran while one was open for 1% -> 1% of each run, Pallas kernels for 18% -> 18%
where the time goes in v5:
time: 45.6 us; the launch traced here: 45.5 us
  Pallas kernels  30.8 us (68%)
  starting transfers between devices  12.5 us (27%)
  waiting for transfers between devices  1.57 us (3%)
    pallas_call x1, Pallas kernels, project(): pl.pallas_call(project_kernel, in_specs=[SMEM] + [HBM] * 4, out_specs=[VM...  19.3 us
    ppermute x11, starting transfers between devices, swapped(): lax.ppermute(block, axis, [(i, i ^ bit) for i in range(lax.axis_size(axis...  12.5 us
    pallas_call x3, Pallas kernels, local_rows(): pl.pallas_call(kernel, in_specs=[SMEM] + [VMEM] * len(operands), out_spec...  4.76 us
    pallas_call x1, Pallas kernels, late_heads(): pl.pallas_call(functools.partial(late_kernel, width=width), in_specs=[SME...  3.39 us
    pallas_call x1, Pallas kernels, phi_queries(): pl.pallas_call(phi_kernel, in_specs=[SMEM, VMEM], out_specs=VMEM, out_sha...  2.31 us
    ppermute x11, waiting for transfers between devices, swapped(): lax.ppermute(block, axis, [(i, i ^ bit) for i in range(lax.axis_size(axis...  1.57 us
    pallas_call x1, Pallas kernels, early_heads(): pl.pallas_call(early_kernel, in_specs=[SMEM] + [VMEM] * 3, out_specs=VMEM...  1.04 us
  transfers between devices with their start and end apart: 11, of which 3 were waited for; matrix products, arithmetic and copies ran while one was open for 1% of the time, Pallas kernels for 18%

profile of v5, /device:TPU:0, one launch (start us, length us, event | category | flops | bytes accessed | tf_op | source)
XLA Modules:
  0.0 45.5 jit_solution(5142153802587996105)
XLA Ops:
  0.0 0.0 copy-start.1
  0.0 0.0 copy-start
  0.0 19.3 %project.1 = (bf16[1280,1120]{1,0:T(8,128)(2,1)S(1)}, f32[56,1120]{1,0:T(8,128)S(1)}, bf16[56,1120]{1,0:T(8,128)(2,1)S(1)}, bf16[80,1120]{1,0:T(8,128)(2,1)S(1)}, bf16[1280,1120]{1,0:T(8,128)(2,1)S(1)}) custom-call(s32[1]{0:T(128)} %bitcast.core_ref.order_ref, bf16[1280,2240]{1,0:T(8,128)(2,1)} %bitcast.4, bf16[2240,1120]{1,0:T(8,128)(2,1)} %wk_hbm.1, ...), custom_call_target="tpu_custom_call" | custom-call | flops 12845056000 | bytes 15769600 | tf_op jit(solution)/shard_map/project/pallas_call | solution.py:133
  19.4 0.5 %collective-permute-start = (bf16[56,512]{1,0:T(8,128)(2,1)S(1)}, bf16[56,512]{1,0:T(8,128)(2,1)S(1)}, u32[]{:S(2)}, u32[]{:S(2)}) collective-permute-start(bf16[56,512]{1,0:T(8,128)(2,1)S(1)} %slice.13), channel_id=1, source_target_pairs={{0,1},{1,0},{2,3},{3,2},{4,5},{5,4},{6,7},{7,6},{8,9},{9,8},{10,11... | collective-permute-start | bytes 172040 | tf_op jit(solution)/shard_map/ppermute | solution.py:413
  19.9 0.1 collective-permute-start.2
  20.0 0.4 collective-permute-start.7
  20.4 0.0 copy-done.1
  20.4 0.4 collective-permute-done
  20.8 2.9 %collective-permute-start.1 = (bf16[56,512]{1,0:T(8,128)(2,1)S(1)}, bf16[56,512]{1,0:T(8,128)(2,1)S(1)}, u32[]{:S(2)}, u32[]{:S(2)}) collective-permute-start(bf16[56,512]{1,0:T(8,128)(2,1)S(1)} %fusion.12), channel_id=1, source_target_pairs={{0,2},{2,0},{4,6},{6,4},{8,10},{10,8},{12,14},{14,12},{1,3},{3,1},... | collective-permute-start | bytes 172040 | tf_op jit(solution)/shard_map/ppermute | solution.py:413
  23.7 0.0 collective-permute-done.2
  23.8 0.2 collective-permute-start.4
  23.9 0.0 copy-done
  23.9 1.5 %upper_rows.1.upper_ref = f32[400,1120]{1,0:T(8,128)S(1)} custom-call(s32[1]{0:T(128)} %bitcast.core_ref.order_ref, bf16[1280,1120]{1,0:T(8,128)(2,1)S(1)} %get-tuple-element.34.v_ref, f32[9,1120]{1,0:T(8,128)S(1)} %copy-done), custom_call_target="tpu_custom_call" | custom-call | flops 8960000 | bytes 3584000 | tf_op jit(solution)/shard_map/upper_rows/pallas_call | solution.py:262
  25.4 0.6 %collective-permute-done.1 = bf16[56,512]{1,0:T(8,128)(2,1)S(1)} collective-permute-done((bf16[56,512]{1,0:T(8,128)(2,1)S(1)}, bf16[56,512]{1,0:T(8,128)(2,1)S(1)}, u32[]{:S(2)}, u32[]{:S(2)}) %collective-permute-start.1) | collective-permute-done | bytes 57376 | tf_op jit(solution)/shard_map/ppermute | solution.py:413
  26.0 2.2 %collective-permute-start.3 = (bf16[56,512]{1,0:T(8,128)(2,1)S(1)}, bf16[56,512]{1,0:T(8,128)(2,1)S(1)}, u32[]{:S(2)}, u32[]{:S(2)}) collective-permute-start(bf16[56,512]{1,0:T(8,128)(2,1)S(1)} %fusion.11), channel_id=1, source_target_pairs={{0,4},{2,6},{4,0},{6,2},{8,12},{10,14},{12,8},{14,10},{1,5},{3,7},... | collective-permute-start | bytes 172040 | tf_op jit(solution)/shard_map/ppermute | solution.py:413
  28.2 0.0 collective-permute-done.4
  28.3 1.6 %collective-permute-start.6 = (bf16[56,608]{1,0:T(8,128)(2,1)S(1)}, bf16[56,608]{1,0:T(8,128)(2,1)S(1)}, u32[]{:S(2)}, u32[]{:S(2)}) collective-permute-start(bf16[56,608]{1,0:T(8,128)(2,1)S(1)} %fusion.10), channel_id=1, source_target_pairs={{0,4},{2,6},{4,0},{6,2},{8,12},{10,14},{12,8},{14,10},{1,5},{3,7},... | collective-permute-start | bytes 204296 | tf_op jit(solution)/shard_map/ppermute | solution.py:413
  29.8 1.5 %lower_rows.1.lower_ref = f32[400,1120]{1,0:T(8,128)S(1)} custom-call(s32[1]{0:T(128)} %bitcast.core_ref.order_ref, bf16[1280,1120]{1,0:T(8,128)(2,1)S(1)} %get-tuple-element.34.v_ref, f32[9,1120]{1,0:T(8,128)S(1)} %copy-done), custom_call_target="tpu_custom_call" | custom-call | flops 8960000 | bytes 3584000 | tf_op jit(solution)/shard_map/lower_rows/pallas_call | solution.py:262
  31.3 0.0 collective-permute-done.3
  31.4 2.7 %collective-permute-start.5 = (bf16[56,512]{1,0:T(8,128)(2,1)S(1)}, bf16[56,512]{1,0:T(8,128)(2,1)S(1)}, u32[]{:S(2)}, u32[]{:S(2)}) collective-permute-start(bf16[56,512]{1,0:T(8,128)(2,1)S(1)} %fusion.9), channel_id=1, source_target_pairs={{0,8},{2,10},{4,12},{6,14},{8,0},{10,2},{12,4},{14,6},{1,9},{3,11}... | collective-permute-start | bytes 172040 | tf_op jit(solution)/shard_map/ppermute | solution.py:413
  34.0 0.0 collective-permute-done.6
  34.1 1.3 %collective-permute-start.9 = (bf16[56,608]{1,0:T(8,128)(2,1)S(1)}, bf16[56,608]{1,0:T(8,128)(2,1)S(1)}, u32[]{:S(2)}, u32[]{:S(2)}) collective-permute-start(bf16[56,608]{1,0:T(8,128)(2,1)S(1)} %fusion.4), channel_id=1, source_target_pairs={{0,8},{2,10},{4,12},{6,14},{8,0},{10,2},{12,4},{14,6},{1,9},{3,11}... | collective-permute-start | bytes 204296 | tf_op jit(solution)/shard_map/ppermute | solution.py:413
  35.4 0.0 collective-permute-done.7.halo_ref
  35.4 1.8 %border_rows.1.edge_ref = f32[480,1120]{1,0:T(8,128)S(1)} custom-call(s32[1]{0:T(128)} %bitcast.core_ref.order_ref, bf16[1280,1120]{1,0:T(8,128)(2,1)S(1)} %get-tuple-element.34.v_ref, bf16[80,1120]{1,0:T(8,128)(2,1)S(1)} %collective-permute-done.7.halo_ref, f32[9,1120]{1,0:T(8,128)S(1)} %copy-done), custom_call_target="tpu_custom_call" | custom-call | flops 10752000 | bytes 4300800 | tf_op jit(solution)/shard_map/border_rows/pallas_call | solution.py:262
  37.2 2.3 %phi_queries.1.qf_ref = bf16[1280,1280]{1,0:T(8,128)(2,1)S(1)} custom-call(s32[1]{0:T(128)} %bitcast.core_ref.order_ref, bf16[1280,1120]{1,0:T(8,128)(2,1)S(1)} %get-tuple-element.43.q_ref), custom_call_target="tpu_custom_call" | custom-call | flops 11468800 | bytes 5734400 | tf_op jit(solution)/shard_map/phi_queries/pallas_call | solution.py:196
  39.5 0.0 collective-permute-done.5
  39.5 0.1 fusion.8.own_ref.owna_ref
  39.6 0.1 collective-permute-start.8
  39.6 0.0 collective-permute-done.9
  39.6 0.1 fusion.3.ownb_ref
  39.7 0.5 %collective-permute-start.10 = (bf16[56,608]{1,0:T(8,128)(2,1)S(1)}, bf16[56,608]{1,0:T(8,128)(2,1)S(1)}, u32[]{:S(2)}, u32[]{:S(2)}) collective-permute-start(bf16[56,608]{1,0:T(8,128)(2,1)S(1)} %fusion.3.ownb_ref), channel_id=1, source_target_pairs={{0,1},{1,0},{2,3},{3,2},{4,5},{5,4},{6,7},{7,6},{8,9},{9,8},{10,11... | collective-permute-start | bytes 204296 | tf_op jit(solution)/shard_map/ppermute | solution.py:413
  40.3 0.6 %collective-permute-done.8.other_ref.othera_ref = bf16[56,512]{1,0:T(8,128)(2,1)S(1)} collective-permute-done((bf16[56,512]{1,0:T(8,128)(2,1)S(1)}, bf16[56,512]{1,0:T(8,128)(2,1)S(1)}, u32[]{:S(2)}, u32[]{:S(2)}) %collective-permute-start.8) | collective-permute-done | bytes 57376 | tf_op jit(solution)/shard_map/ppermute | solution.py:413
  40.9 1.0 %early_heads.1.early_ref = f32[1280,512]{1,0:T(8,128)S(1)} custom-call(s32[1]{0:T(128)} %bitcast.core_ref.order_ref, bf16[56,512]{1,0:T(8,128)(2,1)S(1)} %fusion.8.own_ref.owna_ref, bf16[56,512]{1,0:T(8,128)(2,1)S(1)} %collective-permute-done.8.other_ref.othera_ref, bf16[1280,1280]{1,0:T(8,128)(2,1)S(1)} %phi_queries.1.qf_ref), custom_call_target="tpu_custom_call" | custom-call | flops 1342177280 | bytes 2621440 | tf_op jit(solution)/shard_map/early_heads/pallas_call | solution.py:340
  41.9 0.0 collective-permute-done.10.otherb_ref
  41.9 3.4 %late_heads.1 = bf16[1280,1120]{1,0:T(8,128)(2,1)} custom-call(s32[1]{0:T(128)} %bitcast.core_ref.order_ref, bf16[56,512]{1,0:T(8,128)(2,1)S(1)} %fusion.8.own_ref.owna_ref, bf16[56,512]{1,0:T(8,128)(2,1)S(1)} %collective-permute-done.8.other_ref.othera_ref, bf16[56,608]{1,0:T(8,128)(2,1)S(1)} %fusion.3.ownb_ref, ...), custom_call_target="tpu_custom_call" | custom-call | flops 2936012800 | bytes 11468800 | tf_op jit(solution)/shard_map/late_heads/pallas_call | solution.py:400
  (9 shorter events, 0.2 us)
Async XLA Ops:
  0.0 20.4 %copy-start.1 = (f32[1120]{0:T(1024)S(1)}, f32[1120]{0:T(1024)}, u32[]{:S(2)}) copy-start(f32[1120]{0:T(1024)} %param.11) | copy-start | bytes 13444
  0.0 23.9 %copy-start = (f32[9,1120]{1,0:T(8,128)S(1)}, f32[9,1120]{1,0:T(8,128)}, u32[]{:S(2)}) copy-start(f32[9,1120]{1,0:T(8,128)} %w_ref.5) | copy-start | bytes 120964
  19.4 1.4 %collective-permute-start = (bf16[56,512]{1,0:T(8,128)(2,1)S(1)}, bf16[56,512]{1,0:T(8,128)(2,1)S(1)}, u32[]{:S(2)}, u32[]{:S(2)}) collective-permute-start(bf16[56,512]{1,0:T(8,128)(2,1)S(1)} %slice.13), channel_id=1, source_target_pairs={{0,1},{1,0},{2,3},{3,2},{4,5},{5,4},{6,7},{7,6},{8,9},{9,8},{10,11... | collective-permute-start | bytes 172040 | tf_op jit(solution)/shard_map/ppermute | solution.py:413
  19.9 3.8 %collective-permute-start.2 = (bf16[56,608]{1,0:T(8,128)(2,1)S(1)}, bf16[56,608]{1,0:T(8,128)(2,1)S(1)}, u32[]{:S(2)}, u32[]{:S(2)}) collective-permute-start(bf16[56,608]{1,0:T(8,128)(2,1)S(1)} %slice.15), channel_id=1, source_target_pairs={{0,1},{1,0},{2,3},{3,2},{4,5},{5,4},{6,7},{7,6},{8,9},{9,8},{10,11... | collective-permute-start | bytes 204296 | tf_op jit(solution)/shard_map/ppermute | solution.py:413
  20.0 15.4 %collective-permute-start.7 = (bf16[80,1120]{1,0:T(8,128)(2,1)S(1)}, bf16[80,1120]{1,0:T(8,128)(2,1)S(1)}, u32[]{:S(2)}, u32[]{:S(2)}) collective-permute-start(bf16[80,1120]{1,0:T(8,128)(2,1)S(1)} %get-tuple-element.44), channel_id=1, source_target_pairs={{0,1},{1,0},{2,3},{3,2},{4,5},{5,4},{6,7},{7,6},{8,9},{9,8},{10,11... | collective-permute-start | bytes 537608 | tf_op jit(solution)/shard_map/ppermute | solution.py:413
  20.8 5.2 %collective-permute-start.1 = (bf16[56,512]{1,0:T(8,128)(2,1)S(1)}, bf16[56,512]{1,0:T(8,128)(2,1)S(1)}, u32[]{:S(2)}, u32[]{:S(2)}) collective-permute-start(bf16[56,512]{1,0:T(8,128)(2,1)S(1)} %fusion.12), channel_id=1, source_target_pairs={{0,2},{2,0},{4,6},{6,4},{8,10},{10,8},{12,14},{14,12},{1,3},{3,1},... | collective-permute-start | bytes 172040 | tf_op jit(solution)/shard_map/ppermute | solution.py:413
  23.8 4.5 %collective-permute-start.4 = (bf16[56,608]{1,0:T(8,128)(2,1)S(1)}, bf16[56,608]{1,0:T(8,128)(2,1)S(1)}, u32[]{:S(2)}, u32[]{:S(2)}) collective-permute-start(bf16[56,608]{1,0:T(8,128)(2,1)S(1)} %fusion.13), channel_id=1, source_target_pairs={{0,2},{2,0},{4,6},{6,4},{8,10},{10,8},{12,14},{14,12},{1,3},{3,1},... | collective-permute-start | bytes 204296 | tf_op jit(solution)/shard_map/ppermute | solution.py:413
  26.0 5.3 %collective-permute-start.3 = (bf16[56,512]{1,0:T(8,128)(2,1)S(1)}, bf16[56,512]{1,0:T(8,128)(2,1)S(1)}, u32[]{:S(2)}, u32[]{:S(2)}) collective-permute-start(bf16[56,512]{1,0:T(8,128)(2,1)S(1)} %fusion.11), channel_id=1, source_target_pairs={{0,4},{2,6},{4,0},{6,2},{8,12},{10,14},{12,8},{14,10},{1,5},{3,7},... | collective-permute-start | bytes 172040 | tf_op jit(solution)/shard_map/ppermute | solution.py:413
  28.3 5.8 %collective-permute-start.6 = (bf16[56,608]{1,0:T(8,128)(2,1)S(1)}, bf16[56,608]{1,0:T(8,128)(2,1)S(1)}, u32[]{:S(2)}, u32[]{:S(2)}) collective-permute-start(bf16[56,608]{1,0:T(8,128)(2,1)S(1)} %fusion.10), channel_id=1, source_target_pairs={{0,4},{2,6},{4,0},{6,2},{8,12},{10,14},{12,8},{14,10},{1,5},{3,7},... | collective-permute-start | bytes 204296 | tf_op jit(solution)/shard_map/ppermute | solution.py:413
  31.4 8.1 %collective-permute-start.5 = (bf16[56,512]{1,0:T(8,128)(2,1)S(1)}, bf16[56,512]{1,0:T(8,128)(2,1)S(1)}, u32[]{:S(2)}, u32[]{:S(2)}) collective-permute-start(bf16[56,512]{1,0:T(8,128)(2,1)S(1)} %fusion.9), channel_id=1, source_target_pairs={{0,8},{2,10},{4,12},{6,14},{8,0},{10,2},{12,4},{14,6},{1,9},{3,11}... | collective-permute-start | bytes 172040 | tf_op jit(solution)/shard_map/ppermute | solution.py:413
  34.1 5.6 %collective-permute-start.9 = (bf16[56,608]{1,0:T(8,128)(2,1)S(1)}, bf16[56,608]{1,0:T(8,128)(2,1)S(1)}, u32[]{:S(2)}, u32[]{:S(2)}) collective-permute-start(bf16[56,608]{1,0:T(8,128)(2,1)S(1)} %fusion.4), channel_id=1, source_target_pairs={{0,8},{2,10},{4,12},{6,14},{8,0},{10,2},{12,4},{14,6},{1,9},{3,11}... | collective-permute-start | bytes 204296 | tf_op jit(solution)/shard_map/ppermute | solution.py:413
  39.6 1.3 %collective-permute-start.8 = (bf16[56,512]{1,0:T(8,128)(2,1)S(1)}, bf16[56,512]{1,0:T(8,128)(2,1)S(1)}, u32[]{:S(2)}, u32[]{:S(2)}) collective-permute-start(bf16[56,512]{1,0:T(8,128)(2,1)S(1)} %fusion.8.own_ref.owna_ref), channel_id=1, source_target_pairs={{0,1},{1,0},{2,3},{3,2},{4,5},{5,4},{6,7},{7,6},{8,9},{9,8},{10,11... | collective-permute-start | bytes 172040 | tf_op jit(solution)/shard_map/ppermute | solution.py:413
  39.7 2.2 %collective-permute-start.10 = (bf16[56,608]{1,0:T(8,128)(2,1)S(1)}, bf16[56,608]{1,0:T(8,128)(2,1)S(1)}, u32[]{:S(2)}, u32[]{:S(2)}) collective-permute-start(bf16[56,608]{1,0:T(8,128)(2,1)S(1)} %fusion.3.ownb_ref), channel_id=1, source_target_pairs={{0,1},{1,0},{2,3},{3,2},{4,5},{5,4},{6,7},{7,6},{8,9},{9,8},{10,11... | collective-permute-start | bytes 204296 | tf_op jit(solution)/shard_map/ppermute | solution.py:413

commit v6 on v5

--- a/solution.py
+++ b/solution.py
@@ -182,9 +182,8 @@
         here = pl.ds(pl.multiple_of(i * step, 16), step)
         for pair in range(inner // (2 * HEAD)):
             low, _, wide = pair_span(pair)
-            q = q_ref[here, low : min(low + wide, inner)].astype(F32)
-            q = feature_map(paired(q, low, pair, inner))
-            qf_ref[here, pair * 256 : (pair + 1) * 256] = q.astype(BF16)
+            q = feature_map(q_ref[here, low : min(low + wide, inner)].astype(F32)).astype(BF16)
+            qf_ref[here, pair * 256 : (pair + 1) * 256] = paired(q, low, pair, inner)
         return carry
 
     lax.fori_loop(0, q_ref.shape[0] // step, rows, 0)
@@ -271,8 +270,8 @@
 
 
 def row_pieces(rows):
-    top, bottom = rows // 4, 2
-    upper = (rows - top - bottom) // 2
+    top, bottom = rows // 4 - 1, 2
+    upper = (rows - top - bottom + 1) // 2
     return top, bottom, upper, rows - top - bottom - upper
 
 
@@ -320,7 +319,7 @@
         yield at, min(at + 128, high), tiles[at][:, : min(128, high - at)]
 
 
-CHUNK = 640
+CHUNK = 320
 
 
 def early_kernel(core_ref, own_ref, other_ref, qf_ref, out_ref):

time: 45.6 us -> 44.9 us (0.985)
  Pallas kernels: 30.8 us -> 30.2 us
  transfers between devices with their start and end apart: 11 -> 11, of which waited for: 3 -> 4; matrix products, arithmetic and copies ran while one was open for 1% -> 1% of each run, Pallas kernels for 18% -> 17%
where the time goes in v6:
time: 44.9 us; the launch traced here: 44.8 us
  Pallas kernels  30.2 us (67%)
  starting transfers between devices  12.5 us (28%)
  waiting for transfers between devices  1.48 us (3%)
    pallas_call x1, Pallas kernels, project(): pl.pallas_call(project_kernel, in_specs=[SMEM] + [HBM] * 4, out_specs=[VM...  19.3 us
    ppermute x11, starting transfers between devices, swapped(): lax.ppermute(block, axis, [(i, i ^ bit) for i in range(lax.axis_size(axis...  12.5 us
    pallas_call x3, Pallas kernels, local_rows(): pl.pallas_call(kernel, in_specs=[SMEM] + [VMEM] * len(operands), out_spec...  4.76 us
    pallas_call x1, Pallas kernels, late_heads(): pl.pallas_call(functools.partial(late_kernel, width=width), in_specs=[SME...  3.1 us
    pallas_call x1, Pallas kernels, phi_queries(): pl.pallas_call(phi_kernel, in_specs=[SMEM, VMEM], out_specs=VMEM, out_sha...  1.96 us
    ppermute x11, waiting for transfers between devices, swapped(): lax.ppermute(block, axis, [(i, i ^ bit) for i in range(lax.axis_size(axis...  1.48 us
    pallas_call x1, Pallas kernels, early_heads(): pl.pallas_call(early_kernel, in_specs=[SMEM] + [VMEM] * 3, out_specs=VMEM...  1.05 us
  transfers between devices with their start and end apart: 11, of which 4 were waited for; matrix products, arithmetic and copies ran while one was open for 1% of the time, Pallas kernels for 17%

profile of v6, /device:TPU:0, one launch (start us, length us, event | category | flops | bytes accessed | tf_op | source)
XLA Modules:
  0.0 44.8 jit_solution(10536292561482727497)
XLA Ops:
  0.0 0.0 copy-start.1
  0.0 0.0 copy-start
  0.0 19.3 %project.1 = (bf16[1280,1120]{1,0:T(8,128)(2,1)S(1)}, f32[56,1120]{1,0:T(8,128)S(1)}, bf16[56,1120]{1,0:T(8,128)(2,1)S(1)}, bf16[80,1120]{1,0:T(8,128)(2,1)S(1)}, bf16[1280,1120]{1,0:T(8,128)(2,1)S(1)}) custom-call(s32[1]{0:T(128)} %bitcast.core_ref.order_ref, bf16[1280,2240]{1,0:T(8,128)(2,1)} %bitcast.4, bf16[2240,1120]{1,0:T(8,128)(2,1)} %wk_hbm.1, ...), custom_call_target="tpu_custom_call" | custom-call | flops 12845056000 | bytes 15769600 | tf_op jit(solution)/shard_map/project/pallas_call | solution.py:133
  19.4 0.5 %collective-permute-start = (bf16[56,512]{1,0:T(8,128)(2,1)S(1)}, bf16[56,512]{1,0:T(8,128)(2,1)S(1)}, u32[]{:S(2)}, u32[]{:S(2)}) collective-permute-start(bf16[56,512]{1,0:T(8,128)(2,1)S(1)} %slice.13), channel_id=1, source_target_pairs={{0,1},{1,0},{2,3},{3,2},{4,5},{5,4},{6,7},{7,6},{8,9},{9,8},{10,11... | collective-permute-start | bytes 172040 | tf_op jit(solution)/shard_map/ppermute | solution.py:412
  19.9 0.1 collective-permute-start.2
  20.0 0.4 collective-permute-start.7
  20.4 0.0 copy-done.1
  20.4 0.4 collective-permute-done
  20.8 2.9 %collective-permute-start.1 = (bf16[56,512]{1,0:T(8,128)(2,1)S(1)}, bf16[56,512]{1,0:T(8,128)(2,1)S(1)}, u32[]{:S(2)}, u32[]{:S(2)}) collective-permute-start(bf16[56,512]{1,0:T(8,128)(2,1)S(1)} %fusion.12), channel_id=1, source_target_pairs={{0,2},{2,0},{4,6},{6,4},{8,10},{10,8},{12,14},{14,12},{1,3},{3,1},... | collective-permute-start | bytes 172040 | tf_op jit(solution)/shard_map/ppermute | solution.py:412
  23.7 0.0 collective-permute-done.2
  23.8 0.2 collective-permute-start.4
  23.9 0.0 copy-done
  23.9 1.8 %upper_rows.1.upper_ref = f32[480,1120]{1,0:T(8,128)S(1)} custom-call(s32[1]{0:T(128)} %bitcast.core_ref.order_ref, bf16[1280,1120]{1,0:T(8,128)(2,1)S(1)} %get-tuple-element.34.v_ref, f32[9,1120]{1,0:T(8,128)S(1)} %copy-done), custom_call_target="tpu_custom_call" | custom-call | flops 10752000 | bytes 4300800 | tf_op jit(solution)/shard_map/upper_rows/pallas_call | solution.py:261
  25.7 0.3 collective-permute-done.1
  26.0 2.2 %collective-permute-start.3 = (bf16[56,512]{1,0:T(8,128)(2,1)S(1)}, bf16[56,512]{1,0:T(8,128)(2,1)S(1)}, u32[]{:S(2)}, u32[]{:S(2)}) collective-permute-start(bf16[56,512]{1,0:T(8,128)(2,1)S(1)} %fusion.11), channel_id=1, source_target_pairs={{0,4},{2,6},{4,0},{6,2},{8,12},{10,14},{12,8},{14,10},{1,5},{3,7},... | collective-permute-start | bytes 172040 | tf_op jit(solution)/shard_map/ppermute | solution.py:412
  28.2 0.0 collective-permute-done.4
  28.3 1.6 %collective-permute-start.6 = (bf16[56,608]{1,0:T(8,128)(2,1)S(1)}, bf16[56,608]{1,0:T(8,128)(2,1)S(1)}, u32[]{:S(2)}, u32[]{:S(2)}) collective-permute-start(bf16[56,608]{1,0:T(8,128)(2,1)S(1)} %fusion.10), channel_id=1, source_target_pairs={{0,4},{2,6},{4,0},{6,2},{8,12},{10,14},{12,8},{14,10},{1,5},{3,7},... | collective-permute-start | bytes 204296 | tf_op jit(solution)/shard_map/ppermute | solution.py:412
  29.8 1.5 %lower_rows.1.lower_ref = f32[400,1120]{1,0:T(8,128)S(1)} custom-call(s32[1]{0:T(128)} %bitcast.core_ref.order_ref, bf16[1280,1120]{1,0:T(8,128)(2,1)S(1)} %get-tuple-element.34.v_ref, f32[9,1120]{1,0:T(8,128)S(1)} %copy-done), custom_call_target="tpu_custom_call" | custom-call | flops 8960000 | bytes 3584000 | tf_op jit(solution)/shard_map/lower_rows/pallas_call | solution.py:261
  31.3 0.0 collective-permute-done.3
  31.4 2.7 %collective-permute-start.5 = (bf16[56,512]{1,0:T(8,128)(2,1)S(1)}, bf16[56,512]{1,0:T(8,128)(2,1)S(1)}, u32[]{:S(2)}, u32[]{:S(2)}) collective-permute-start(bf16[56,512]{1,0:T(8,128)(2,1)S(1)} %fusion.9), channel_id=1, source_target_pairs={{0,8},{2,10},{4,12},{6,14},{8,0},{10,2},{12,4},{14,6},{1,9},{3,11}... | collective-permute-start | bytes 172040 | tf_op jit(solution)/shard_map/ppermute | solution.py:412
  34.0 0.0 collective-permute-done.6
  34.1 1.6 %collective-permute-start.9 = (bf16[56,608]{1,0:T(8,128)(2,1)S(1)}, bf16[56,608]{1,0:T(8,128)(2,1)S(1)}, u32[]{:S(2)}, u32[]{:S(2)}) collective-permute-start(bf16[56,608]{1,0:T(8,128)(2,1)S(1)} %fusion.4), channel_id=1, source_target_pairs={{0,8},{2,10},{4,12},{6,14},{8,0},{10,2},{12,4},{14,6},{1,9},{3,11}... | collective-permute-start | bytes 204296 | tf_op jit(solution)/shard_map/ppermute | solution.py:412
  35.6 0.0 collective-permute-done.7.halo_ref
  35.6 1.5 %border_rows.1.edge_ref = f32[400,1120]{1,0:T(8,128)S(1)} custom-call(s32[1]{0:T(128)} %bitcast.core_ref.order_ref, bf16[1280,1120]{1,0:T(8,128)(2,1)S(1)} %get-tuple-element.34.v_ref, bf16[80,1120]{1,0:T(8,128)(2,1)S(1)} %collective-permute-done.7.halo_ref, f32[9,1120]{1,0:T(8,128)S(1)} %copy-done), custom_call_target="tpu_custom_call" | custom-call | flops 8960000 | bytes 3584000 | tf_op jit(solution)/shard_map/border_rows/pallas_call | solution.py:261
  37.1 2.0 %phi_queries.1.qf_ref = bf16[1280,1280]{1,0:T(8,128)(2,1)S(1)} custom-call(s32[1]{0:T(128)} %bitcast.core_ref.order_ref, bf16[1280,1120]{1,0:T(8,128)(2,1)S(1)} %get-tuple-element.43.q_ref), custom_call_target="tpu_custom_call" | custom-call | flops 11468800 | bytes 5734400 | tf_op jit(solution)/shard_map/phi_queries/pallas_call | solution.py:195
  39.1 0.0 collective-permute-done.5
  39.1 0.1 fusion.8.own_ref.owna_ref
  39.2 0.1 collective-permute-start.8
  39.2 0.2 collective-permute-done.9
  39.5 0.1 fusion.3.ownb_ref
  39.5 0.4 collective-permute-start.10
  39.9 0.6 %collective-permute-done.8.other_ref.othera_ref = bf16[56,512]{1,0:T(8,128)(2,1)S(1)} collective-permute-done((bf16[56,512]{1,0:T(8,128)(2,1)S(1)}, bf16[56,512]{1,0:T(8,128)(2,1)S(1)}, u32[]{:S(2)}, u32[]{:S(2)}) %collective-permute-start.8) | collective-permute-done | bytes 57376 | tf_op jit(solution)/shard_map/ppermute | solution.py:412
  40.5 1.0 %early_heads.1.early_ref = f32[1280,512]{1,0:T(8,128)S(1)} custom-call(s32[1]{0:T(128)} %bitcast.core_ref.order_ref, bf16[56,512]{1,0:T(8,128)(2,1)S(1)} %fusion.8.own_ref.owna_ref, bf16[56,512]{1,0:T(8,128)(2,1)S(1)} %collective-permute-done.8.other_ref.othera_ref, bf16[1280,1280]{1,0:T(8,128)(2,1)S(1)} %phi_queries.1.qf_ref), custom_call_target="tpu_custom_call" | custom-call | flops 1342177280 | bytes 2621440 | tf_op jit(solution)/shard_map/early_heads/pallas_call | solution.py:339
  41.5 0.0 collective-permute-done.10.otherb_ref
  41.5 3.1 %late_heads.1 = bf16[1280,1120]{1,0:T(8,128)(2,1)} custom-call(s32[1]{0:T(128)} %bitcast.core_ref.order_ref, bf16[56,512]{1,0:T(8,128)(2,1)S(1)} %fusion.8.own_ref.owna_ref, bf16[56,512]{1,0:T(8,128)(2,1)S(1)} %collective-permute-done.8.other_ref.othera_ref, bf16[56,608]{1,0:T(8,128)(2,1)S(1)} %fusion.3.ownb_ref, ...), custom_call_target="tpu_custom_call" | custom-call | flops 2936012800 | bytes 11468800 | tf_op jit(solution)/shard_map/late_heads/pallas_call | solution.py:399
  (9 shorter events, 0.2 us)
Async XLA Ops:
  0.0 20.4 %copy-start.1 = (f32[1120]{0:T(1024)S(1)}, f32[1120]{0:T(1024)}, u32[]{:S(2)}) copy-start(f32[1120]{0:T(1024)} %param.11) | copy-start | bytes 13444
  0.0 23.9 %copy-start = (f32[9,1120]{1,0:T(8,128)S(1)}, f32[9,1120]{1,0:T(8,128)}, u32[]{:S(2)}) copy-start(f32[9,1120]{1,0:T(8,128)} %w_ref.5) | copy-start | bytes 120964
  19.4 1.4 %collective-permute-start = (bf16[56,512]{1,0:T(8,128)(2,1)S(1)}, bf16[56,512]{1,0:T(8,128)(2,1)S(1)}, u32[]{:S(2)}, u32[]{:S(2)}) collective-permute-start(bf16[56,512]{1,0:T(8,128)(2,1)S(1)} %slice.13), channel_id=1, source_target_pairs={{0,1},{1,0},{2,3},{3,2},{4,5},{5,4},{6,7},{7,6},{8,9},{9,8},{10,11... | collective-permute-start | bytes 172040 | tf_op jit(solution)/shard_map/ppermute | solution.py:412
  19.9 3.8 %collective-permute-start.2 = (bf16[56,608]{1,0:T(8,128)(2,1)S(1)}, bf16[56,608]{1,0:T(8,128)(2,1)S(1)}, u32[]{:S(2)}, u32[]{:S(2)}) collective-permute-start(bf16[56,608]{1,0:T(8,128)(2,1)S(1)} %slice.15), channel_id=1, source_target_pairs={{0,1},{1,0},{2,3},{3,2},{4,5},{5,4},{6,7},{7,6},{8,9},{9,8},{10,11... | collective-permute-start | bytes 204296 | tf_op jit(solution)/shard_map/ppermute | solution.py:412
  20.0 15.6 %collective-permute-start.7 = (bf16[80,1120]{1,0:T(8,128)(2,1)S(1)}, bf16[80,1120]{1,0:T(8,128)(2,1)S(1)}, u32[]{:S(2)}, u32[]{:S(2)}) collective-permute-start(bf16[80,1120]{1,0:T(8,128)(2,1)S(1)} %get-tuple-element.44), channel_id=1, source_target_pairs={{0,1},{1,0},{2,3},{3,2},{4,5},{5,4},{6,7},{7,6},{8,9},{9,8},{10,11... | collective-permute-start | bytes 537608 | tf_op jit(solution)/shard_map/ppermute | solution.py:412
  20.8 5.2 %collective-permute-start.1 = (bf16[56,512]{1,0:T(8,128)(2,1)S(1)}, bf16[56,512]{1,0:T(8,128)(2,1)S(1)}, u32[]{:S(2)}, u32[]{:S(2)}) collective-permute-start(bf16[56,512]{1,0:T(8,128)(2,1)S(1)} %fusion.12), channel_id=1, source_target_pairs={{0,2},{2,0},{4,6},{6,4},{8,10},{10,8},{12,14},{14,12},{1,3},{3,1},... | collective-permute-start | bytes 172040 | tf_op jit(solution)/shard_map/ppermute | solution.py:412
  23.8 4.5 %collective-permute-start.4 = (bf16[56,608]{1,0:T(8,128)(2,1)S(1)}, bf16[56,608]{1,0:T(8,128)(2,1)S(1)}, u32[]{:S(2)}, u32[]{:S(2)}) collective-permute-start(bf16[56,608]{1,0:T(8,128)(2,1)S(1)} %fusion.13), channel_id=1, source_target_pairs={{0,2},{2,0},{4,6},{6,4},{8,10},{10,8},{12,14},{14,12},{1,3},{3,1},... | collective-permute-start | bytes 204296 | tf_op jit(solution)/shard_map/ppermute | solution.py:412
  26.0 5.3 %collective-permute-start.3 = (bf16[56,512]{1,0:T(8,128)(2,1)S(1)}, bf16[56,512]{1,0:T(8,128)(2,1)S(1)}, u32[]{:S(2)}, u32[]{:S(2)}) collective-permute-start(bf16[56,512]{1,0:T(8,128)(2,1)S(1)} %fusion.11), channel_id=1, source_target_pairs={{0,4},{2,6},{4,0},{6,2},{8,12},{10,14},{12,8},{14,10},{1,5},{3,7},... | collective-permute-start | bytes 172040 | tf_op jit(solution)/shard_map/ppermute | solution.py:412
  28.3 5.8 %collective-permute-start.6 = (bf16[56,608]{1,0:T(8,128)(2,1)S(1)}, bf16[56,608]{1,0:T(8,128)(2,1)S(1)}, u32[]{:S(2)}, u32[]{:S(2)}) collective-permute-start(bf16[56,608]{1,0:T(8,128)(2,1)S(1)} %fusion.10), channel_id=1, source_target_pairs={{0,4},{2,6},{4,0},{6,2},{8,12},{10,14},{12,8},{14,10},{1,5},{3,7},... | collective-permute-start | bytes 204296 | tf_op jit(solution)/shard_map/ppermute | solution.py:412
  31.4 7.7 %collective-permute-start.5 = (bf16[56,512]{1,0:T(8,128)(2,1)S(1)}, bf16[56,512]{1,0:T(8,128)(2,1)S(1)}, u32[]{:S(2)}, u32[]{:S(2)}) collective-permute-start(bf16[56,512]{1,0:T(8,128)(2,1)S(1)} %fusion.9), channel_id=1, source_target_pairs={{0,8},{2,10},{4,12},{6,14},{8,0},{10,2},{12,4},{14,6},{1,9},{3,11}... | collective-permute-start | bytes 172040 | tf_op jit(solution)/shard_map/ppermute | solution.py:412
  34.1 5.4 %collective-permute-start.9 = (bf16[56,608]{1,0:T(8,128)(2,1)S(1)}, bf16[56,608]{1,0:T(8,128)(2,1)S(1)}, u32[]{:S(2)}, u32[]{:S(2)}) collective-permute-start(bf16[56,608]{1,0:T(8,128)(2,1)S(1)} %fusion.4), channel_id=1, source_target_pairs={{0,8},{2,10},{4,12},{6,14},{8,0},{10,2},{12,4},{14,6},{1,9},{3,11}... | collective-permute-start | bytes 204296 | tf_op jit(solution)/shard_map/ppermute | solution.py:412
  39.2 1.3 %collective-permute-start.8 = (bf16[56,512]{1,0:T(8,128)(2,1)S(1)}, bf16[56,512]{1,0:T(8,128)(2,1)S(1)}, u32[]{:S(2)}, u32[]{:S(2)}) collective-permute-start(bf16[56,512]{1,0:T(8,128)(2,1)S(1)} %fusion.8.own_ref.owna_ref), channel_id=1, source_target_pairs={{0,1},{1,0},{2,3},{3,2},{4,5},{5,4},{6,7},{7,6},{8,9},{9,8},{10,11... | collective-permute-start | bytes 172040 | tf_op jit(solution)/shard_map/ppermute | solution.py:412
  39.5 2.0 %collective-permute-start.10 = (bf16[56,608]{1,0:T(8,128)(2,1)S(1)}, bf16[56,608]{1,0:T(8,128)(2,1)S(1)}, u32[]{:S(2)}, u32[]{:S(2)}) collective-permute-start(bf16[56,608]{1,0:T(8,128)(2,1)S(1)} %fusion.3.ownb_ref), channel_id=1, source_target_pairs={{0,1},{1,0},{2,3},{3,2},{4,5},{5,4},{6,7},{7,6},{8,9},{9,8},{10,11... | collective-permute-start | bytes 204296 | tf_op jit(solution)/shard_map/ppermute | solution.py:412

commit v7 on v6

--- a/solution.py
+++ b/solution.py
@@ -270,7 +270,7 @@
 
 
 def row_pieces(rows):
-    top, bottom = rows // 4 - 1, 2
+    top, bottom = rows // 8, 2
     upper = (rows - top - bottom + 1) // 2
     return top, bottom, upper, rows - top - bottom - upper
 

time: 44.9 us -> 45.3 us (level)
  waiting for transfers between devices: 1.48 us -> 2.12 us
    ppermute x11, waiting for transfers between devices: 1.48 us -> 2.12 us  [swapped(): lax.ppermute(block, axis, [(i, i ^ bit) for i in range(lax.axis_size(axis...]
where the time goes in v7:
time: 45.3 us; the launch traced here: 45.1 us
  Pallas kernels  30.2 us (67%)
  starting transfers between devices  12.2 us (27%)
  waiting for transfers between devices  2.12 us (5%)
    pallas_call x1, Pallas kernels, project(): pl.pallas_call(project_kernel, in_specs=[SMEM] + [HBM] * 4, out_specs=[VM...  19.3 us
    ppermute x11, starting transfers between devices, swapped(): lax.ppermute(block, axis, [(i, i ^ bit) for i in range(lax.axis_size(axis...  12.2 us
    pallas_call x3, Pallas kernels, local_rows(): pl.pallas_call(kernel, in_specs=[SMEM] + [VMEM] * len(operands), out_spec...  4.76 us
    pallas_call x1, Pallas kernels, late_heads(): pl.pallas_call(functools.partial(late_kernel, width=width), in_specs=[SME...  3.07 us
    ppermute x11, waiting for transfers between devices, swapped(): lax.ppermute(block, axis, [(i, i ^ bit) for i in range(lax.axis_size(axis...  2.12 us
    pallas_call x1, Pallas kernels, phi_queries(): pl.pallas_call(phi_kernel, in_specs=[SMEM, VMEM], out_specs=VMEM, out_sha...  1.96 us
    pallas_call x1, Pallas kernels, early_heads(): pl.pallas_call(early_kernel, in_specs=[SMEM] + [VMEM] * 3, out_specs=VMEM...  1.05 us
  transfers between devices with their start and end apart: 11, of which 4 were waited for; matrix products, arithmetic and copies ran while one was open for 1% of the time, Pallas kernels for 17%

profile of v7, /device:TPU:0, one launch (start us, length us, event | category | flops | bytes accessed | tf_op | source)
XLA Modules:
  0.0 45.1 jit_solution(18445382392708136890)
XLA Ops:
  0.0 0.0 copy-start.1
  0.0 0.0 copy-start
  0.0 19.3 %project.1 = (bf16[1280,1120]{1,0:T(8,128)(2,1)S(1)}, f32[56,1120]{1,0:T(8,128)S(1)}, bf16[56,1120]{1,0:T(8,128)(2,1)S(1)}, bf16[80,1120]{1,0:T(8,128)(2,1)S(1)}, bf16[1280,1120]{1,0:T(8,128)(2,1)S(1)}) custom-call(s32[1]{0:T(128)} %bitcast.core_ref.order_ref, bf16[1280,2240]{1,0:T(8,128)(2,1)} %bitcast.4, bf16[2240,1120]{1,0:T(8,128)(2,1)} %wk_hbm.1, ...), custom_call_target="tpu_custom_call" | custom-call | flops 12845056000 | bytes 15769600 | tf_op jit(solution)/shard_map/project/pallas_call | solution.py:133
  19.4 0.5 %collective-permute-start = (bf16[56,512]{1,0:T(8,128)(2,1)S(1)}, bf16[56,512]{1,0:T(8,128)(2,1)S(1)}, u32[]{:S(2)}, u32[]{:S(2)}) collective-permute-start(bf16[56,512]{1,0:T(8,128)(2,1)S(1)} %slice.13), channel_id=1, source_target_pairs={{0,1},{1,0},{2,3},{3,2},{4,5},{5,4},{6,7},{7,6},{8,9},{9,8},{10,11... | collective-permute-start | bytes 172040 | tf_op jit(solution)/shard_map/ppermute | solution.py:412
  19.9 0.1 collective-permute-start.2
  20.0 0.4 collective-permute-start.7
  20.4 0.0 copy-done.1
  20.4 0.4 collective-permute-done
  20.8 2.9 %collective-permute-start.1 = (bf16[56,512]{1,0:T(8,128)(2,1)S(1)}, bf16[56,512]{1,0:T(8,128)(2,1)S(1)}, u32[]{:S(2)}, u32[]{:S(2)}) collective-permute-start(bf16[56,512]{1,0:T(8,128)(2,1)S(1)} %fusion.12), channel_id=1, source_target_pairs={{0,2},{2,0},{4,6},{6,4},{8,10},{10,8},{12,14},{14,12},{1,3},{3,1},... | collective-permute-start | bytes 172040 | tf_op jit(solution)/shard_map/ppermute | solution.py:412
  23.7 0.0 collective-permute-done.2
  23.8 0.2 collective-permute-start.4
  23.9 0.0 copy-done
  23.9 1.8 %upper_rows.1.upper_ref = f32[480,1120]{1,0:T(8,128)S(1)} custom-call(s32[1]{0:T(128)} %bitcast.core_ref.order_ref, bf16[1280,1120]{1,0:T(8,128)(2,1)S(1)} %get-tuple-element.34.v_ref, f32[9,1120]{1,0:T(8,128)S(1)} %copy-done), custom_call_target="tpu_custom_call" | custom-call | flops 10752000 | bytes 4300800 | tf_op jit(solution)/shard_map/upper_rows/pallas_call | solution.py:261
  25.7 0.3 collective-permute-done.1
  26.0 2.2 %collective-permute-start.3 = (bf16[56,512]{1,0:T(8,128)(2,1)S(1)}, bf16[56,512]{1,0:T(8,128)(2,1)S(1)}, u32[]{:S(2)}, u32[]{:S(2)}) collective-permute-start(bf16[56,512]{1,0:T(8,128)(2,1)S(1)} %fusion.11), channel_id=1, source_target_pairs={{0,4},{2,6},{4,0},{6,2},{8,12},{10,14},{12,8},{14,10},{1,5},{3,7},... | collective-permute-start | bytes 172040 | tf_op jit(solution)/shard_map/ppermute | solution.py:412
  28.2 0.0 collective-permute-done.4
  28.3 1.6 %collective-permute-start.6 = (bf16[56,608]{1,0:T(8,128)(2,1)S(1)}, bf16[56,608]{1,0:T(8,128)(2,1)S(1)}, u32[]{:S(2)}, u32[]{:S(2)}) collective-permute-start(bf16[56,608]{1,0:T(8,128)(2,1)S(1)} %fusion.10), channel_id=1, source_target_pairs={{0,4},{2,6},{4,0},{6,2},{8,12},{10,14},{12,8},{14,10},{1,5},{3,7},... | collective-permute-start | bytes 204296 | tf_op jit(solution)/shard_map/ppermute | solution.py:412
  29.8 1.8 %lower_rows.1.lower_ref = f32[480,1120]{1,0:T(8,128)S(1)} custom-call(s32[1]{0:T(128)} %bitcast.core_ref.order_ref, bf16[1280,1120]{1,0:T(8,128)(2,1)S(1)} %get-tuple-element.34.v_ref, f32[9,1120]{1,0:T(8,128)S(1)} %copy-done), custom_call_target="tpu_custom_call" | custom-call | flops 10752000 | bytes 4300800 | tf_op jit(solution)/shard_map/lower_rows/pallas_call | solution.py:261
  31.6 0.0 collective-permute-done.3
  31.7 2.7 %collective-permute-start.5 = (bf16[56,512]{1,0:T(8,128)(2,1)S(1)}, bf16[56,512]{1,0:T(8,128)(2,1)S(1)}, u32[]{:S(2)}, u32[]{:S(2)}) collective-permute-start(bf16[56,512]{1,0:T(8,128)(2,1)S(1)} %fusion.9), channel_id=1, source_target_pairs={{0,8},{2,10},{4,12},{6,14},{8,0},{10,2},{12,4},{14,6},{1,9},{3,11}... | collective-permute-start | bytes 172040 | tf_op jit(solution)/shard_map/ppermute | solution.py:412
  34.3 0.0 collective-permute-done.6
  34.4 1.6 %collective-permute-start.9 = (bf16[56,608]{1,0:T(8,128)(2,1)S(1)}, bf16[56,608]{1,0:T(8,128)(2,1)S(1)}, u32[]{:S(2)}, u32[]{:S(2)}) collective-permute-start(bf16[56,608]{1,0:T(8,128)(2,1)S(1)} %fusion.4), channel_id=1, source_target_pairs={{0,8},{2,10},{4,12},{6,14},{8,0},{10,2},{12,4},{14,6},{1,9},{3,11}... | collective-permute-start | bytes 204296 | tf_op jit(solution)/shard_map/ppermute | solution.py:412
  35.9 0.0 collective-permute-done.7.halo_ref
  36.0 1.2 %border_rows.1.edge_ref = f32[320,1120]{1,0:T(8,128)S(1)} custom-call(s32[1]{0:T(128)} %bitcast.core_ref.order_ref, bf16[1280,1120]{1,0:T(8,128)(2,1)S(1)} %get-tuple-element.34.v_ref, bf16[80,1120]{1,0:T(8,128)(2,1)S(1)} %collective-permute-done.7.halo_ref, f32[9,1120]{1,0:T(8,128)S(1)} %copy-done), custom_call_target="tpu_custom_call" | custom-call | flops 7168000 | bytes 2867200 | tf_op jit(solution)/shard_map/border_rows/pallas_call | solution.py:261
  37.1 2.0 %phi_queries.1.qf_ref = bf16[1280,1280]{1,0:T(8,128)(2,1)S(1)} custom-call(s32[1]{0:T(128)} %bitcast.core_ref.order_ref, bf16[1280,1120]{1,0:T(8,128)(2,1)S(1)} %get-tuple-element.43.q_ref), custom_call_target="tpu_custom_call" | custom-call | flops 11468800 | bytes 5734400 | tf_op jit(solution)/shard_map/phi_queries/pallas_call | solution.py:195
  39.1 0.0 collective-permute-done.5
  39.1 0.1 fusion.8.own_ref.owna_ref
  39.2 0.1 collective-permute-start.8
  39.2 1.3 %collective-permute-done.9 = bf16[56,608]{1,0:T(8,128)(2,1)S(1)} collective-permute-done((bf16[56,608]{1,0:T(8,128)(2,1)S(1)}, bf16[56,608]{1,0:T(8,128)(2,1)S(1)}, u32[]{:S(2)}, u32[]{:S(2)}) %collective-permute-start.9) | collective-permute-done | bytes 68128 | tf_op jit(solution)/shard_map/ppermute | solution.py:412
  40.5 0.1 fusion.3.ownb_ref
  40.6 0.1 collective-permute-start.10
  40.7 0.0 collective-permute-done.8.other_ref.othera_ref
  40.7 1.1 %early_heads.1.early_ref = f32[1280,512]{1,0:T(8,128)S(1)} custom-call(s32[1]{0:T(128)} %bitcast.core_ref.order_ref, bf16[56,512]{1,0:T(8,128)(2,1)S(1)} %fusion.8.own_ref.owna_ref, bf16[56,512]{1,0:T(8,128)(2,1)S(1)} %collective-permute-done.8.other_ref.othera_ref, bf16[1280,1280]{1,0:T(8,128)(2,1)S(1)} %phi_queries.1.qf_ref), custom_call_target="tpu_custom_call" | custom-call | flops 1342177280 | bytes 2621440 | tf_op jit(solution)/shard_map/early_heads/pallas_call | solution.py:339
  41.7 0.2 collective-permute-done.10.otherb_ref
  41.9 3.1 %late_heads.1 = bf16[1280,1120]{1,0:T(8,128)(2,1)} custom-call(s32[1]{0:T(128)} %bitcast.core_ref.order_ref, bf16[56,512]{1,0:T(8,128)(2,1)S(1)} %fusion.8.own_ref.owna_ref, bf16[56,512]{1,0:T(8,128)(2,1)S(1)} %collective-permute-done.8.other_ref.othera_ref, bf16[56,608]{1,0:T(8,128)(2,1)S(1)} %fusion.3.ownb_ref, ...), custom_call_target="tpu_custom_call" | custom-call | flops 2936012800 | bytes 11468800 | tf_op jit(solution)/shard_map/late_heads/pallas_call | solution.py:399
  (9 shorter events, 0.2 us)
Async XLA Ops:
  0.0 20.4 %copy-start.1 = (f32[1120]{0:T(1024)S(1)}, f32[1120]{0:T(1024)}, u32[]{:S(2)}) copy-start(f32[1120]{0:T(1024)} %param.11) | copy-start | bytes 13444
  0.0 23.9 %copy-start = (f32[9,1120]{1,0:T(8,128)S(1)}, f32[9,1120]{1,0:T(8,128)}, u32[]{:S(2)}) copy-start(f32[9,1120]{1,0:T(8,128)} %w_ref.5) | copy-start | bytes 120964
  19.4 1.4 %collective-permute-start = (bf16[56,512]{1,0:T(8,128)(2,1)S(1)}, bf16[56,512]{1,0:T(8,128)(2,1)S(1)}, u32[]{:S(2)}, u32[]{:S(2)}) collective-permute-start(bf16[56,512]{1,0:T(8,128)(2,1)S(1)} %slice.13), channel_id=1, source_target_pairs={{0,1},{1,0},{2,3},{3,2},{4,5},{5,4},{6,7},{7,6},{8,9},{9,8},{10,11... | collective-permute-start | bytes 172040 | tf_op jit(solution)/shard_map/ppermute | solution.py:412
  19.9 3.8 %collective-permute-start.2 = (bf16[56,608]{1,0:T(8,128)(2,1)S(1)}, bf16[56,608]{1,0:T(8,128)(2,1)S(1)}, u32[]{:S(2)}, u32[]{:S(2)}) collective-permute-start(bf16[56,608]{1,0:T(8,128)(2,1)S(1)} %slice.15), channel_id=1, source_target_pairs={{0,1},{1,0},{2,3},{3,2},{4,5},{5,4},{6,7},{7,6},{8,9},{9,8},{10,11... | collective-permute-start | bytes 204296 | tf_op jit(solution)/shard_map/ppermute | solution.py:412
  20.0 15.9 %collective-permute-start.7 = (bf16[80,1120]{1,0:T(8,128)(2,1)S(1)}, bf16[80,1120]{1,0:T(8,128)(2,1)S(1)}, u32[]{:S(2)}, u32[]{:S(2)}) collective-permute-start(bf16[80,1120]{1,0:T(8,128)(2,1)S(1)} %get-tuple-element.44), channel_id=1, source_target_pairs={{0,1},{1,0},{2,3},{3,2},{4,5},{5,4},{6,7},{7,6},{8,9},{9,8},{10,11... | collective-permute-start | bytes 537608 | tf_op jit(solution)/shard_map/ppermute | solution.py:412
  20.8 5.2 %collective-permute-start.1 = (bf16[56,512]{1,0:T(8,128)(2,1)S(1)}, bf16[56,512]{1,0:T(8,128)(2,1)S(1)}, u32[]{:S(2)}, u32[]{:S(2)}) collective-permute-start(bf16[56,512]{1,0:T(8,128)(2,1)S(1)} %fusion.12), channel_id=1, source_target_pairs={{0,2},{2,0},{4,6},{6,4},{8,10},{10,8},{12,14},{14,12},{1,3},{3,1},... | collective-permute-start | bytes 172040 | tf_op jit(solution)/shard_map/ppermute | solution.py:412
  23.8 4.5 %collective-permute-start.4 = (bf16[56,608]{1,0:T(8,128)(2,1)S(1)}, bf16[56,608]{1,0:T(8,128)(2,1)S(1)}, u32[]{:S(2)}, u32[]{:S(2)}) collective-permute-start(bf16[56,608]{1,0:T(8,128)(2,1)S(1)} %fusion.13), channel_id=1, source_target_pairs={{0,2},{2,0},{4,6},{6,4},{8,10},{10,8},{12,14},{14,12},{1,3},{3,1},... | collective-permute-start | bytes 204296 | tf_op jit(solution)/shard_map/ppermute | solution.py:412
  26.0 5.6 %collective-permute-start.3 = (bf16[56,512]{1,0:T(8,128)(2,1)S(1)}, bf16[56,512]{1,0:T(8,128)(2,1)S(1)}, u32[]{:S(2)}, u32[]{:S(2)}) collective-permute-start(bf16[56,512]{1,0:T(8,128)(2,1)S(1)} %fusion.11), channel_id=1, source_target_pairs={{0,4},{2,6},{4,0},{6,2},{8,12},{10,14},{12,8},{14,10},{1,5},{3,7},... | collective-permute-start | bytes 172040 | tf_op jit(solution)/shard_map/ppermute | solution.py:412
  28.3 6.1 %collective-permute-start.6 = (bf16[56,608]{1,0:T(8,128)(2,1)S(1)}, bf16[56,608]{1,0:T(8,128)(2,1)S(1)}, u32[]{:S(2)}, u32[]{:S(2)}) collective-permute-start(bf16[56,608]{1,0:T(8,128)(2,1)S(1)} %fusion.10), channel_id=1, source_target_pairs={{0,4},{2,6},{4,0},{6,2},{8,12},{10,14},{12,8},{14,10},{1,5},{3,7},... | collective-permute-start | bytes 204296 | tf_op jit(solution)/shard_map/ppermute | solution.py:412
  31.7 7.4 %collective-permute-start.5 = (bf16[56,512]{1,0:T(8,128)(2,1)S(1)}, bf16[56,512]{1,0:T(8,128)(2,1)S(1)}, u32[]{:S(2)}, u32[]{:S(2)}) collective-permute-start(bf16[56,512]{1,0:T(8,128)(2,1)S(1)} %fusion.9), channel_id=1, source_target_pairs={{0,8},{2,10},{4,12},{6,14},{8,0},{10,2},{12,4},{14,6},{1,9},{3,11}... | collective-permute-start | bytes 172040 | tf_op jit(solution)/shard_map/ppermute | solution.py:412
  34.4 6.1 %collective-permute-start.9 = (bf16[56,608]{1,0:T(8,128)(2,1)S(1)}, bf16[56,608]{1,0:T(8,128)(2,1)S(1)}, u32[]{:S(2)}, u32[]{:S(2)}) collective-permute-start(bf16[56,608]{1,0:T(8,128)(2,1)S(1)} %fusion.4), channel_id=1, source_target_pairs={{0,8},{2,10},{4,12},{6,14},{8,0},{10,2},{12,4},{14,6},{1,9},{3,11}... | collective-permute-start | bytes 204296 | tf_op jit(solution)/shard_map/ppermute | solution.py:412
  39.2 1.5 %collective-permute-start.8 = (bf16[56,512]{1,0:T(8,128)(2,1)S(1)}, bf16[56,512]{1,0:T(8,128)(2,1)S(1)}, u32[]{:S(2)}, u32[]{:S(2)}) collective-permute-start(bf16[56,512]{1,0:T(8,128)(2,1)S(1)} %fusion.8.own_ref.owna_ref), channel_id=1, source_target_pairs={{0,1},{1,0},{2,3},{3,2},{4,5},{5,4},{6,7},{7,6},{8,9},{9,8},{10,11... | collective-permute-start | bytes 172040 | tf_op jit(solution)/shard_map/ppermute | solution.py:412
  40.6 1.3 %collective-permute-start.10 = (bf16[56,608]{1,0:T(8,128)(2,1)S(1)}, bf16[56,608]{1,0:T(8,128)(2,1)S(1)}, u32[]{:S(2)}, u32[]{:S(2)}) collective-permute-start(bf16[56,608]{1,0:T(8,128)(2,1)S(1)} %fusion.3.ownb_ref), channel_id=1, source_target_pairs={{0,1},{1,0},{2,3},{3,2},{4,5},{5,4},{6,7},{7,6},{8,9},{9,8},{10,11... | collective-permute-start | bytes 204296 | tf_op jit(solution)/shard_map/ppermute | solution.py:412
